TPU v7x, 128 devices: a whole 4x4x4 slice. The times are simulated.
128 devices in a mesh: dp: 16 (over z, x_lo, core), ctx: 8 (over x_hi, y).
Axes of the slice: x: 4 (x_hi: 2, x_lo: 2; x = x_hi * 2 + x_lo), y: 4, z: 4, core: 2. Of those that a mesh axis runs over, the one named last changes fastest.
Arguments:
- hidden: bfloat16 [16, 1024, 4096], P('dp', 'ctx'), may hold values from -6 to 6
- queries: bfloat16 [16, 1024, 4096], P('dp', 'ctx'), may hold values from -6 to 6
- keys: bfloat16 [16, 1024, 256], P('dp', 'ctx'), may hold values from -6 to 6
- values: bfloat16 [16, 1024, 256], P('dp', 'ctx'), may hold values from -24 to 24
- out_weight: bfloat16 [4096, 4096], P(None, 'ctx'), may hold values from -0.09375 to 0.09375
- norm_gain: float32 [4096], replicated, may hold values from 0.1 to 1.9
- routes: int32 [16, 1024, 8], P('dp', 'ctx'), may hold values from 0 to 127, all different within a row; in each aligned block of 128 rows (0 to 127, 128 to 255, ..., all dimensions but the last counted through in order) at most 9 rows name the same one
- slot_scores: float32 [16, 1024, 8], P('dp', 'ctx'), may hold values from 0.1 to 1
- gate_weight: bfloat16 [128, 4096, 768], P(('dp', 'ctx')), may hold values from -0.09375 to 0.09375
- up_weight: bfloat16 [128, 4096, 768], P(('dp', 'ctx')), may hold values from -0.09375 to 0.09375
- down_weight: bfloat16 [128, 768, 4096], P(('dp', 'ctx')), may hold values from -0.21875 to 0.21875
Outputs:
- output: bfloat16 [16, 1024, 4096], P('dp', 'ctx')
Inputs may be any that keep to these rules, and one draw needn't show every extreme that they name: In each aligned block of 128 tokens (the tokens of one device, sequences in order) no expert is named by more than 9 of the block's routes, a bound that some block reaches.
All inputs are finite; a program needn't handle non-finite values.
Results may differ from a plain program's by a relative error of at most 0.0065.
Values may be sent and summed in bfloat16 or wider, within the bound.
No kernel may reach another device: no remote copies, remote signals or barrier semaphores. Data moves between devices by JAX's collectives and lax.ppermute only.
A program may use at most 192 MiB of HBM per device.

v0:
```python
import jax
import jax.numpy as jnp
from jax import lax
from jax.sharding import PartitionSpec as P

HQ = 32
KVH = 2
DH = 128
TOP = 8


def expert_ffn(slots_in, w_gate, w_up, w_down):
    flat_rows = slots_in.reshape(-1, slots_in.shape[-1])
    gated = jnp.dot(flat_rows, w_gate, preferred_element_type=jnp.float32)
    lifted = jnp.dot(flat_rows, w_up, preferred_element_type=jnp.float32)
    activated = (jax.nn.silu(gated) * lifted).astype(jnp.bfloat16)
    result = jnp.dot(activated, w_down, preferred_element_type=jnp.float32).astype(jnp.bfloat16)
    return result.reshape(slots_in.shape)


def local(
    hidden,
    queries,
    keys,
    values,
    out_weight,
    norm_gain,
    routes,
    slot_scores,
    gate_weight,
    up_weight,
    down_weight,
):
    tok_count = hidden.shape[1]
    model_width = hidden.shape[2]
    group_size = HQ // KVH
    score_scale = DH ** (-0.5)
    ctx_index = lax.axis_index("ctx")
    query_rows = queries[0].reshape(tok_count, KVH, group_size, DH)
    query_pos = ctx_index * tok_count + jnp.arange(tok_count, dtype=jnp.int32)
    key_piece = lax.all_gather(keys, "ctx", axis=1, tiled=True)
    value_piece = lax.all_gather(values, "ctx", axis=1, tiled=True)
    key_count = key_piece.shape[1]
    key_rows = key_piece[0].reshape(key_count, KVH, DH)
    value_rows = value_piece[0].reshape(key_count, KVH, DH)
    key_pos = jnp.arange(key_count, dtype=jnp.int32)
    running_max = jnp.full((KVH, group_size, tok_count), -1e30, jnp.float32)
    scores = (
        jnp.einsum("qkgd,jkd->kgqj", query_rows, key_rows, preferred_element_type=jnp.float32)
        * score_scale
    )
    causal = key_pos[None, :] <= query_pos[:, None]
    scores = jnp.where(causal, scores, -1e30)
    new_max = jnp.maximum(running_max, jnp.max(scores, axis=-1))
    weights = jnp.where(causal, jnp.exp(scores - new_max[..., None]), 0.0)
    running_sum = jnp.sum(weights, axis=-1)
    numerator = jnp.einsum(
        "kgqj,jkd->kgqd",
        weights.astype(jnp.bfloat16),
        value_rows,
        preferred_element_type=jnp.float32,
    )
    running_max, running_sum, numerator = (new_max, running_sum, numerator)
    attended = numerator / running_sum[..., None]
    attended = (
        jnp.transpose(attended, (2, 0, 1, 3)).reshape(tok_count, HQ * DH).astype(jnp.bfloat16)
    )
    columns = jnp.dot(
        lax.all_gather(attended, "ctx", axis=0, tiled=True),
        out_weight,
        preferred_element_type=jnp.float32,
    ).astype(jnp.bfloat16)
    projected = lax.all_to_all(columns, "ctx", split_axis=0, concat_axis=1, tiled=True)
    residual = hidden[0].astype(jnp.float32) + projected.astype(jnp.float32)
    normed = (
        residual
        * lax.rsqrt(jnp.mean(residual * residual, axis=1, keepdims=True) + 1e-06)
        * norm_gain
    ).astype(jnp.bfloat16)
    score_rows = slot_scores[0]
    slot_gates = score_rows / jnp.sum(score_rows, axis=1, keepdims=True)
    expert_total = lax.axis_size(("dp", "ctx"))
    capacity = max(2, tok_count * TOP * 9 // (8 * expert_total))
    expert_ids = routes[0].reshape(tok_count * TOP)
    one_hot = (expert_ids[:, None] == jnp.arange(expert_total, dtype=jnp.int32)[None, :]).astype(
        jnp.int32
    )
    earlier = jnp.sum((jnp.cumsum(one_hot, axis=0) - one_hot) * one_hot, axis=1)
    slot_index = expert_ids * capacity + earlier
    token_of = jnp.arange(tok_count * TOP, dtype=jnp.int32) // TOP
    outgoing = (
        jnp.zeros((expert_total * capacity, model_width), jnp.bfloat16)
        .at[slot_index]
        .set(normed[token_of])
    )
    outgoing = outgoing.reshape(expert_total, capacity, model_width)
    served = expert_ffn(
        lax.all_to_all(outgoing, ("dp", "ctx"), split_axis=0, concat_axis=0, tiled=True),
        gate_weight[0],
        up_weight[0],
        down_weight[0],
    )
    returned = lax.all_to_all(served, ("dp", "ctx"), split_axis=0, concat_axis=0, tiled=True)
    returned = returned.reshape(expert_total * capacity, model_width)
    picked = returned[slot_index].reshape(tok_count, TOP, model_width)
    mixture = jnp.sum(slot_gates[:, :, None] * picked.astype(jnp.float32), axis=1)
    return (residual + mixture).astype(jnp.bfloat16)[None]


def solution(mesh):
    return jax.shard_map(
        local,
        mesh=mesh,
        in_specs=(
            P("dp", "ctx", None),
            P("dp", "ctx", None),
            P("dp", "ctx", None),
            P("dp", "ctx", None),
            P(None, "ctx"),
            P(),
            P("dp", "ctx", None),
            P("dp", "ctx", None),
            P(("dp", "ctx"), None, None),
            P(("dp", "ctx"), None, None),
            P(("dp", "ctx"), None, None),
        ),
        out_specs=P("dp", "ctx", None),
        check_vma=False,
    )
```

profile of v0, /device:TPU:91, one launch (start us, length us, event | category | flops | bytes accessed | tf_op | source)
XLA Modules:
  0.0 829.0 jit_solution(7543872358024971029)
XLA Ops:
  6.5 29.6 %all_gather.10 = bf16[1,1024,256]{2,1,0:T(8,128)(2,1)S(1)} all-gather(bf16[1,128,256]{2,1,0:T(8,128)(2,1)} %param.14), channel_id=1, replica_groups=mesh['dp'=16,'ctx'=8] {'ctx'}, dimensions={1}, use_global_device_ids=true | all-gather | bytes 589824 | tf_op jit(solution)/shard_map/all_gather | solution.py:42
  37.5 25.4 %all_gather.9 = bf16[1,1024,256]{1,2,0:T(8,128)(2,1)S(1)} all-gather(bf16[1,128,256]{1,2,0:T(8,128)(2,1)S(1)} %copy.18), channel_id=1, replica_groups=mesh['dp'=16,'ctx'=8] {'ctx'}, dimensions={1}, use_global_device_ids=true | all-gather | bytes 589824 | tf_op jit(solution)/shard_map/all_gather | solution.py:41
  67.3 4.1 fusion.2
  71.4 5.1 fusion.23
  77.4 118.9 %all-gather.2.cloned.1.call-done = bf16[1024,4096]{0,1:T(8,128)(2,1)} async-done(((bf16[128,4096]{0,1:T(8,128)(2,1)}), bf16[1024,4096]{0,1:T(8,128)(2,1)}) %all-gather.2.cloned.1.call-update) | async-done | bytes 8388624 | tf_op jit(solution)/shard_map/all_gather | solution.py:69
  196.4 10.1 %convolution_convert_fusion.1 = bf16[1024,512]{1,0:T(8,128)(2,1)} fusion(bf16[1024,4096]{0,1:T(8,128)(2,1)} %all-gather.2.cloned.1.call-done, bf16[4096,512]{1,0:T(8,128)(2,1)} %param.15), kind=kOutput, calls=%fused_computation.33 | convolution fusion | flops 4295491584 | bytes 13631488 | tf_op jit(solution)/shard_map/dot_general | solution.py:68
  206.4 6.2 all-to-all-start
  213.2 12.8 %all-to-all-done = bf16[8,128,512]{2,1,0:T(8,128)(2,1)S(1)} async-done(((bf16[8,128,512]{2,1,0:T(8,128)(2,1)}), bf16[8,128,512]{2,1,0:T(8,128)(2,1)S(1)}, u32[]{:S(2)}, u32[]{:S(2)}) %all-to-all-start) | async-done | bytes 1048608 | tf_op jit(solution)/shard_map/all_to_all | solution.py:73
  228.7 7.7 gather_fusion
  236.5 18.4 %scatter_custom_fusion = bf16[1152,4096]{1,0:T(8,128)(2,1)} fusion(s32[1024]{0:T(1024)S(1)} %bitcast.96, bf16[1024,4096]{1,0:T(8,128)(2,1)} %gather_fusion, bf16[]{:T(256)} %constant.43.clone.1), kind=kCustom, calls=%fused_computation.18 | custom fusion | bytes 9437696 | tf_op jit(solution)/shard_map/scatter | solution.py:94
  254.9 15.1 %reshape.163 = bf16[128,9,4096]{2,1,0:T(8,128)(2,1)} reshape(bf16[1152,4096]{1,0:T(8,128)(2,1)} %scatter_custom_fusion) | data formatting | bytes 18874368 | tf_op jit(solution)/shard_map/reshape | solution.py:96
  270.0 197.8 %all_to_all.23 = bf16[128,9,4096]{2,1,0:T(8,128)(2,1)} all-to-all(bf16[128,9,4096]{2,1,0:T(8,128)(2,1)} %reshape.163), channel_id=1, replica_groups=mesh['dp'=16,'ctx'=8] {'dp','ctx'}, dimensions={0} | all-to-all | bytes 18874368 | tf_op jit(solution)/shard_map/all_to_all | solution.py:98
  467.7 15.8 %reshape.164 = bf16[1152,4096]{1,0:T(8,128)(2,1)} reshape(bf16[128,9,4096]{2,1,0:T(8,128)(2,1)} %all_to_all.23) | data formatting | bytes 18874368 | tf_op jit(solution)/shard_map/reshape | solution.py:13
  483.6 12.0 %fusion.10 = f32[1152,768]{1,0:T(8,128)S(1)} fusion(bf16[1152,4096]{1,0:T(8,128)(2,1)} %reshape.164, bf16[1,4096,768]{2,1,0:T(8,128)(2,1)} %param.19), kind=kOutput, calls=%fused_computation.16 | convolution fusion | flops 7247757312 | bytes 19267584 | tf_op jit(solution)/shard_map/dot_general | solution.py:14
  495.6 10.3 %fusion.17 = bf16[1152,768]{1,0:T(8,128)(2,1)S(1)} fusion(bf16[1152,4096]{1,0:T(8,128)(2,1)S(1)} %copy-done, bf16[1,4096,768]{2,1,0:T(8,128)(2,1)} %param.20, f32[1152,768]{1,0:T(8,128)S(1)} %fusion.10), kind=kOutput, calls=%fused_computation.21 | convolution fusion | flops 7253065728 | bytes 21037056 | tf_op jit(solution)/shard_map/dot_general | solution.py:15
  505.9 9.6 %convolution_convert_fusion = bf16[1152,4096]{1,0:T(8,128)(2,1)} fusion(bf16[1152,768]{1,0:T(8,128)(2,1)S(1)} %fusion.17, bf16[1,768,4096]{2,1,0:T(8,128)(2,1)S(1)} %bitcast.101), kind=kOutput, calls=%fused_computation.7 | convolution fusion | flops 7252475904 | bytes 17498112 | tf_op jit(solution)/shard_map/dot_general | solution.py:17
  515.5 15.1 %reshape.165 = bf16[128,9,4096]{2,1,0:T(8,128)(2,1)} reshape(bf16[1152,4096]{1,0:T(8,128)(2,1)} %convolution_convert_fusion) | data formatting | bytes 18874368 | tf_op jit(solution)/shard_map/reshape | solution.py:18
  530.6 9.5 %all-to-all-start.2 = ((bf16[128,9,4096]{2,1,0:T(8,128)(2,1)}), bf16[128,9,4096]{2,1,0:T(8,128)(2,1)}, u32[]{:S(2)}, u32[]{:S(2)}) async-start(bf16[128,9,4096]{2,1,0:T(8,128)(2,1)} %reshape.165), calls=%async_computation.2 | async-start | bytes 33554432 | tf_op jit(solution)/shard_map/all_to_all | solution.py:103
  540.3 4.2 copy.23
  547.2 222.0 %all-to-all-done.2 = bf16[128,9,4096]{2,1,0:T(8,128)(2,1)} async-done(((bf16[128,9,4096]{2,1,0:T(8,128)(2,1)}), bf16[128,9,4096]{2,1,0:T(8,128)(2,1)}, u32[]{:S(2)}, u32[]{:S(2)}) %all-to-all-start.2) | async-done | bytes 9437216 | tf_op jit(solution)/shard_map/all_to_all | solution.py:103
  769.3 15.8 %reshape.166 = bf16[1152,4096]{1,0:T(8,128)(2,1)} reshape(bf16[128,9,4096]{2,1,0:T(8,128)(2,1)} %all-to-all-done.2) | data formatting | bytes 18874368 | tf_op jit(solution)/shard_map/reshape | solution.py:104
  785.1 20.0 %gather_fusion.1 = bf16[1024,4096]{1,0:T(8,128)(2,1)} fusion(bf16[1152,4096]{1,0:T(8,128)(2,1)} %reshape.166, s32[1024]{0:T(1024)S(1)} %broadcast_clamp_fusion), kind=kCustom, calls=%fused_computation.1 | custom fusion | bytes 16781312 | tf_op jit(solution)/shard_map/gather | solution.py:105
  805.0 13.2 %fusion = f32[128,4096]{1,0:T(8,128)} fusion(bf16[1024,4096]{1,0:T(8,128)(2,1)} %gather_fusion.1, f32[128,8]{1,0:T(8,128)S(1)} %copy.24), kind=kLoop, calls=%fused_computation.4 | loop fusion | flops 12058624 | bytes 10489856 | tf_op jit(solution)/shard_map/reduce_sum | solution.py:106
  818.2 3.5 fusion.21
  (51 shorter events, 12.5 us)
Async XLA Ops:
  6.5 189.8 %all-gather.2.cloned.1.call-start = ((), (), s32[]{:S(2)}) async-start(), calls=%async_computation.3 | async-start | bytes 9437184 | tf_op jit(solution)/shard_map/all_gather | solution.py:69
  71.4 5.2 copy-start.3
  206.4 21.5 %copy-start.1 = (bf16[1,128,4096]{2,1,0:T(8,128)(2,1)S(1)}, bf16[1,128,4096]{2,1,0:T(8,128)(2,1)}, u32[]{:S(2)}) copy-start(bf16[1,128,4096]{2,1,0:T(8,128)(2,1)} %param.11) | copy-start | bytes 3145732
  206.4 21.9 %copy-start.2 = (f32[4096]{0:T(1024)S(1)}, f32[4096]{0:T(1024)}, u32[]{:S(2)}) copy-start(f32[4096]{0:T(1024)} %param.16) | copy-start | bytes 49156
  206.4 19.6 %all-to-all-start = ((bf16[8,128,512]{2,1,0:T(8,128)(2,1)}), bf16[8,128,512]{2,1,0:T(8,128)(2,1)S(1)}, u32[]{:S(2)}, u32[]{:S(2)}) async-start(bf16[8,128,512]{2,1,0:T(8,128)(2,1)} %bitcast.93), calls=%async_computation | async-start | bytes 2097152 | tf_op jit(solution)/shard_map/all_to_all | solution.py:73
  483.6 12.0 %copy-start = (bf16[1152,4096]{1,0:T(8,128)(2,1)S(1)}, bf16[1152,4096]{1,0:T(8,128)(2,1)}, u32[]{:S(2)}) copy-start(bf16[1152,4096]{1,0:T(8,128)(2,1)} %reshape.164) | copy-start | bytes 28311556
  483.6 22.3 %slice-start = ((s8[6291456]{0:T(1024)(128)(4,1)}), s8[4194304]{0:T(1024)(128)(4,1)S(1)}, s32[]{:S(2)}) async-start(s8[6291456]{0:T(1024)(128)(4,1)} %bitcast.100), calls=%async_computation.4 | async-start | bytes 8388608
  495.6 10.3 %slice-start.1 = ((s8[6291456]{0:T(1024)(128)(4,1)}), s8[2097152]{0:T(1024)(128)(4,1)S(1)}, s32[]{:S(2)}) async-start(s8[6291456]{0:T(1024)(128)(4,1)} %bitcast.100), calls=%async_computation.5 | async-start | bytes 4194304
  530.6 9.6 %copy-start.4 = (f32[1,128,8]{1,2,0:T(8,128)S(1)}, f32[1,128,8]{1,2,0:T(8,128)}, u32[]{:S(2)}) copy-start(f32[1,128,8]{1,2,0:T(8,128)} %param.18) | copy-start | bytes 12292
  530.6 238.7 %all-to-all-start.2 = ((bf16[128,9,4096]{2,1,0:T(8,128)(2,1)}), bf16[128,9,4096]{2,1,0:T(8,128)(2,1)}, u32[]{:S(2)}, u32[]{:S(2)}) async-start(bf16[128,9,4096]{2,1,0:T(8,128)(2,1)} %reshape.165), calls=%async_computation.2 | async-start | bytes 33554432 | tf_op jit(solution)/shard_map/all_to_all | solution.py:103
Sparse Core Ops, SparseCore 0:
  76.7 119.6 all-gather.1
where the time goes:
time: 839 us; the launch traced here: 829 us
  waiting for transfers between devices  354 us (42%)
  blocking collectives  253 us (30%)
  local copies, waits for them, and re-layouts  119 us (14%)
  matrix products  49.9 us (6%)
  other arithmetic  24.1 us (3%)
  starting transfers between devices  15.8 us (2%)
  between operations  14.1 us (2%)
    all_to_all x1, waiting for transfers between devices, local(): lax.all_to_all(served, ('dp', 'ctx'), split_axis=0, concat_axis=0, tiled=...  222 us
    all_to_all x1, blocking collectives, local(): lax.all_to_all(outgoing, ('dp', 'ctx'), split_axis=0, concat_axis=0, tile...  198 us
    all_gather x1, waiting for transfers between devices, local(): lax.all_gather(attended, 'ctx', axis=0, tiled=True)  119 us
    all_gather x1, blocking collectives, local(): value_piece = lax.all_gather(values, 'ctx', axis=1, tiled=True)  29.6 us
    all_gather x1, blocking collectives, local(): key_piece = lax.all_gather(keys, 'ctx', axis=1, tiled=True)  25.4 us
    gather x1, local copies, waits for them, and re-layouts, local(): picked = returned[slot_index].reshape(tok_count, TOP, model_width)  20 us
    scatter x1, local copies, waits for them, and re-layouts, local(): outgoing = jnp.zeros((expert_total * capacity, model_width), jnp.bfloat16...  18.4 us
  transfers between devices with their start and end apart: 3, of which 3 were waited for; matrix products, arithmetic and copies ran while one was open for 1% of the time, Pallas kernels for 0%

commit v1 on v0

v1 whole, which is shorter than its diff:
```python
import jax
import jax.numpy as jnp
from jax import lax
from jax.sharding import Mesh, PartitionSpec as P

HQ = 32
KVH = 2
DH = 128
TOP = 8
EXPERTS = 128
FULL = 8
CHUNKS = 2

DP = ("z", "xl", "core")
CTX = ("xh", "y")
ALL = DP + CTX
BF = jnp.bfloat16
F32 = jnp.float32


def exchange(blocks, axes):
    return lax.all_to_all(blocks, axes, split_axis=0, concat_axis=0, tiled=True)


def neighbour_pairs():
    pairs = []
    for z in range(4):
        for xl in range(2):
            for core in range(2):
                for xh in range(2):
                    for y in range(4):
                        src = (((z * 2 + xl) * 2 + core) * 2 + xh) * 4 + y
                        dst = (((z * 2 + 1 - xl) * 2 + core) * 2 + 1 - xh) * 4 + y
                        pairs.append((src, dst))
    return pairs


def shift(block, step):
    return lax.ppermute(block, "y", [(i, (i + step) % 4) for i in range(4)])


def partner_weight(out_weight):
    core = lax.axis_index("core")
    half = out_weight.shape[0] // 2
    mine = lax.dynamic_slice_in_dim(out_weight, core * half, half, axis=0)
    fetched = lax.ppermute(mine, ALL, neighbour_pairs())
    other = lax.ppermute(fetched, "core", [(0, 1), (1, 0)])
    first = jnp.where(core == 0, fetched, other)
    second = jnp.where(core == 0, other, fetched)
    return jnp.concatenate([first, second], axis=0)


def attention(queries, keys, values):
    tok_count = queries.shape[0]
    group_size = HQ // KVH
    ctx_index = lax.axis_index(CTX)
    query_rows = queries.reshape(tok_count, KVH, group_size, DH)
    query_pos = ctx_index * tok_count + jnp.arange(tok_count, dtype=jnp.int32)
    pair = jnp.concatenate([keys, values], axis=1)
    width = keys.shape[1]
    gathered = exchange(jnp.broadcast_to(pair[None], (8,) + pair.shape), CTX)
    gathered = gathered.reshape(8 * tok_count, 2 * width)
    key_count = gathered.shape[0]
    key_rows = gathered[:, :width].reshape(key_count, KVH, DH)
    value_rows = gathered[:, width:].reshape(key_count, KVH, DH)
    key_pos = jnp.arange(key_count, dtype=jnp.int32)
    scores = (
        jnp.einsum("qkgd,jkd->kgqj", query_rows, key_rows, preferred_element_type=F32)
        * DH ** (-0.5)
    )
    causal = key_pos[None, :] <= query_pos[:, None]
    scores = jnp.where(causal, scores, -1e30)
    row_max = jnp.max(scores, axis=-1, keepdims=True)
    weights = jnp.where(causal, jnp.exp(scores - row_max), 0.0)
    total = jnp.sum(weights, axis=-1)
    numerator = jnp.einsum(
        "kgqj,jkd->kgqd", weights.astype(BF), value_rows, preferred_element_type=F32
    )
    attended = numerator / total[..., None]
    return jnp.transpose(attended, (2, 0, 1, 3)).reshape(tok_count, HQ * DH).astype(BF)


def project(attended, out_weight):
    partner = partner_weight(out_weight)
    width = attended.shape[1]

    def columns(rows):
        own = jnp.dot(rows, out_weight, preferred_element_type=F32).astype(BF)
        pair = jnp.dot(rows, partner, preferred_element_type=F32).astype(BF)
        return jnp.concatenate([own, pair], axis=1)

    below = shift(attended, 1)
    above = shift(attended, -1)
    far_left = shift(below[:, : width // 2], 1)
    far_right = shift(above[:, width // 2 :], -1)
    here = columns(attended)
    from_above = shift(columns(below), -1)
    from_below = shift(columns(above), 1)
    from_far = shift(columns(jnp.concatenate([far_left, far_right], axis=1)), 2)
    tok = attended.shape[0]
    y = lax.axis_index("y")
    xh = lax.axis_index("xh")
    ring = jnp.stack([here, from_above * 1, from_far, from_below])
    own_first = ring.reshape(4, tok, 2, 512).transpose(2, 0, 1, 3)
    turned = lax.dynamic_slice_in_dim(
        jnp.concatenate([own_first, own_first], axis=1), (4 - y) % 4, 4, axis=1
    )
    turned = jnp.where(xh == 0, turned, turned[::-1])
    return turned.reshape(8, tok, 512).transpose(1, 0, 2).reshape(tok, width)


def slots_of(routes, slot_gates):
    tok = routes.shape[0]
    named = routes[:, :, None] == jnp.arange(EXPERTS, dtype=jnp.int32)[None, None, :]
    hit = jnp.any(named, axis=1)
    gate = jnp.sum(jnp.where(named, slot_gates[:, :, None], 0.0), axis=1)
    before = jnp.arange(tok)[None, :] < jnp.arange(tok)[:, None]
    rank = jnp.dot(before.astype(BF), hit.astype(BF), preferred_element_type=F32)
    return hit, jnp.where(hit, rank, -1.0), gate


def local(
    hidden,
    queries,
    keys,
    values,
    out_weight,
    norm_gain,
    routes,
    slot_scores,
    gate_weight,
    up_weight,
    down_weight,
):
    tok, width = hidden.shape[1:]
    attended = attention(queries[0], keys[0], values[0])

    score_rows = slot_scores[0]
    slot_gates = score_rows / jnp.sum(score_rows, axis=1, keepdims=True)
    hit, rank, gate = slots_of(routes[0], slot_gates)
    places = jnp.arange(FULL, dtype=F32)
    pick = (rank.T[:, None, :] == places[None, :, None]).astype(BF).reshape(EXPERTS * FULL, tok)
    pick_last = (rank.T == float(FULL)).astype(BF)
    weigh = jnp.where(rank[:, :, None] == places, gate[:, :, None], 0.0).reshape(tok, EXPERTS * FULL)
    weigh_last = jnp.where(rank == float(FULL), gate, 0.0)
    weigh = jnp.concatenate([weigh, weigh_last], axis=1)
    high = weigh.astype(BF)
    low = (weigh - high.astype(F32)).astype(BF)
    split = jnp.concatenate([high, low], axis=0)

    projected = project(attended, out_weight)
    residual = hidden[0].astype(F32) + projected.astype(F32)
    normed = (
        residual
        * lax.rsqrt(jnp.mean(residual * residual, axis=1, keepdims=True) + 1e-06)
        * norm_gain
    ).astype(BF)

    step = width // CHUNKS
    w_gate, w_up, w_down = gate_weight[0], up_weight[0], down_weight[0]
    last = jnp.dot(pick_last, normed, preferred_element_type=F32).astype(BF)
    last = exchange(last.reshape(EXPERTS, 8, width // 8), ALL).reshape(EXPERTS, width)
    gated = lifted = 0.0
    for c in range(CHUNKS):
        cols = slice(c * step, (c + 1) * step)
        sent = jnp.dot(pick, normed[:, cols], preferred_element_type=F32).astype(BF)
        got = exchange(sent.reshape(EXPERTS, FULL, step), ALL).reshape(EXPERTS * FULL, step)
        got = jnp.concatenate([got, last[:, cols]], axis=0)
        gated = gated + jnp.dot(got, w_gate[cols], preferred_element_type=F32)
        lifted = lifted + jnp.dot(got, w_up[cols], preferred_element_type=F32)
    activated = (jax.nn.silu(gated) * lifted).astype(BF)

    rows = EXPERTS * FULL
    back_last = jnp.dot(activated[rows:], w_down, preferred_element_type=F32).astype(BF)
    back_last = exchange(back_last.reshape(EXPERTS, 8, width // 8), ALL).reshape(EXPERTS, width)
    outs = []
    for c in range(CHUNKS):
        cols = slice(c * step, (c + 1) * step)
        served = jnp.dot(activated[:rows], w_down[:, cols], preferred_element_type=F32).astype(BF)
        back = exchange(served.reshape(EXPERTS, FULL, step), ALL).reshape(rows, step)
        back = jnp.concatenate([back, back_last[:, cols]], axis=0)
        sums = jnp.dot(split, back, preferred_element_type=F32)
        outs.append((residual[:, cols] + (sums[:tok] + sums[tok:])).astype(BF))
    return jnp.concatenate(outs, axis=1)[None]


def solution(mesh):
    fine = Mesh(mesh.devices.reshape(4, 2, 2, 2, 4), ALL)
    return jax.shard_map(
        local,
        mesh=fine,
        in_specs=(
            P(DP, CTX, None),
            P(DP, CTX, None),
            P(DP, CTX, None),
            P(DP, CTX, None),
            P(None, CTX),
            P(),
            P(DP, CTX, None),
            P(DP, CTX, None),
            P(ALL, None, None),
            P(ALL, None, None),
            P(ALL, None, None),
        ),
        out_specs=P(DP, CTX, None),
        check_vma=False,
    )
```

time: 839 us -> 431 us (0.51)
  the two profiles are of different devices: /device:TPU:91 before, /device:TPU:0 now
where the time goes in v1:
time: 431 us; the launch traced here: 423 us
  waiting for transfers between devices  250 us (58%)
  matrix products  89.2 us (21%)
  starting transfers between devices  61.2 us (14%)
  local copies, waits for them, and re-layouts  14.7 us (3%)
  other arithmetic  7.39 us (2%)
    all_to_all x7, waiting for transfers between devices, exchange(): return lax.all_to_all(blocks, axes, split_axis=0, concat_axis=0, tiled=True)  207 us
    all_to_all x7, starting transfers between devices, exchange(): return lax.all_to_all(blocks, axes, split_axis=0, concat_axis=0, tiled=True)  45.5 us
    ppermute x1, waiting for transfers between devices, partner_weight(): fetched = lax.ppermute(mine, ALL, neighbour_pairs())  25.4 us
    ppermute x7, waiting for transfers between devices, shift(): return lax.ppermute(block, 'y', [(i, (i + step) % 4) for i in range(4)])  17.7 us
    dot_general x2, matrix products, local(): lifted = lifted + jnp.dot(got, w_up[cols], preferred_element_type=F32)  17.1 us
    dot_general x2, matrix products, local(): gated = gated + jnp.dot(got, w_gate[cols], preferred_element_type=F32)  16.1 us
    dot_general x2, matrix products, local(): jnp.dot(activated[:rows], w_down[:, cols], preferred_element_type=F32)  15.6 us
    ppermute x7, starting transfers between devices, shift(): return lax.ppermute(block, 'y', [(i, (i + step) % 4) for i in range(4)])  12.4 us
  transfers between devices with their start and end apart: 16, of which 12 were waited for; matrix products, arithmetic and copies ran while one was open for 18% of the time, Pallas kernels for 0%

profile of v1, /device:TPU:0, one launch (start us, length us, event | category | flops | bytes accessed | tf_op | source)
XLA Modules:
  0.0 422.9 jit_solution(681387273167046604)
XLA Ops:
  2.2 7.0 %all-to-all-start = ((bf16[8,128,512]{1,2,0:T(8,128)(2,1)}), bf16[8,128,512]{1,2,0:T(8,128)(2,1)S(1)}, u32[]{:S(2)}, u32[]{:S(2)}) async-start(bf16[8,128,512]{1,2,0:T(8,128)(2,1)} %broadcast_in_dim.71), calls=%async_computation | async-start | bytes 2097152 | tf_op jit(solution)/shard_map/all_to_all | solution.py:22
  16.0 9.2 %all-to-all-done = bf16[8,128,512]{1,2,0:T(8,128)(2,1)S(1)} async-done(((bf16[8,128,512]{1,2,0:T(8,128)(2,1)}), bf16[8,128,512]{1,2,0:T(8,128)(2,1)S(1)}, u32[]{:S(2)}, u32[]{:S(2)}) %all-to-all-start) | async-done | bytes 1048608 | tf_op jit(solution)/shard_map/all_to_all | solution.py:22
  25.4 10.0 %fusion.73 = (f32[2,16,128]{2,1,0:T(8,128)S(1)}, bf16[2,16,128,1024]{2,3,1,0:T(8,128)(2,1)}) fusion(pred[128,1024]{0,1:T(8,128)(4,1)S(1)} %iota_compare_fusion.1, bf16[1024,2,128,1]{0,2,3,1:T(8,128)(2,1)S(1)} %bitcast.145, bf16[128,2,16,128]{3,2,1,0:T(8,128)(2,1)S(1)} %bitcast.139), kind=kOutput, calls=%fused_computation.125 | convolution fusion | flops 1098908672 | bytes 10108928 | tf_op jit(solution)/shard_map/sub | solution.py:74
  44.0 25.4 %collective-permute-done = bf16[2048,512]{1,0:T(8,128)(2,1)} collective-permute-done((bf16[2048,512]{1,0:T(8,128)(2,1)}, bf16[2048,512]{1,0:T(8,128)(2,1)}, u32[]{:S(2)}, u32[]{:S(2)}) %collective-permute-start) | collective-permute-done | bytes 2097184 | tf_op jit(solution)/shard_map/ppermute | solution.py:46
  77.8 10.4 %collective-permute-done.4 = bf16[128,2048]{0,1:T(8,128)(2,1)S(1)} collective-permute-done((bf16[128,2048]{0,1:T(8,128)(2,1)S(1)}, bf16[128,2048]{0,1:T(8,128)(2,1)S(1)}, u32[]{:S(2)}, u32[]{:S(2)}) %collective-permute-start.4) | collective-permute-done | bytes 524320 | tf_op jit(solution)/shard_map/ppermute | solution.py:39
  114.5 8.3 %all-to-all-start.2 = ((bf16[128,8,512]{2,1,0:T(8,128)(2,1)}), bf16[128,8,512]{2,1,0:T(8,128)(2,1)}, u32[]{:S(2)}, u32[]{:S(2)}) async-start(bf16[128,8,512]{2,1,0:T(8,128)(2,1)} %bitcast.131), calls=%async_computation.2 | async-start | bytes 2097152 | tf_op jit(solution)/shard_map/all_to_all | solution.py:22
  126.1 15.0 %all-to-all-done.2 = bf16[128,8,512]{2,1,0:T(8,128)(2,1)} async-done(((bf16[128,8,512]{2,1,0:T(8,128)(2,1)}), bf16[128,8,512]{2,1,0:T(8,128)(2,1)}, u32[]{:S(2)}, u32[]{:S(2)}) %all-to-all-start.2) | async-done | bytes 1048608 | tf_op jit(solution)/shard_map/all_to_all | solution.py:22
  141.2 5.8 %all-to-all-start.1 = ((bf16[128,8,2048]{2,1,0:T(8,128)(2,1)}), bf16[128,8,2048]{2,1,0:T(8,128)(2,1)}, u32[]{:S(2)}, u32[]{:S(2)}) async-start(bf16[128,8,2048]{2,1,0:T(8,128)(2,1)} %convert_bitcast_fusion.3), calls=%async_computation.1 | async-start | bytes 8388608 | tf_op jit(solution)/shard_map/all_to_all | solution.py:22
  150.3 48.7 %all-to-all-done.1 = bf16[128,8,2048]{2,1,0:T(8,128)(2,1)} async-done(((bf16[128,8,2048]{2,1,0:T(8,128)(2,1)}), bf16[128,8,2048]{2,1,0:T(8,128)(2,1)}, u32[]{:S(2)}, u32[]{:S(2)}) %all-to-all-start.1) | async-done | bytes 4194336 | tf_op jit(solution)/shard_map/all_to_all | solution.py:22
  199.0 6.4 %all-to-all-start.3 = ((bf16[128,8,2048]{2,1,0:T(8,128)(2,1)}), bf16[128,8,2048]{2,1,0:T(8,128)(2,1)}, u32[]{:S(2)}, u32[]{:S(2)}) async-start(bf16[128,8,2048]{2,1,0:T(8,128)(2,1)} %convert_bitcast_fusion.2), calls=%async_computation.3 | async-start | bytes 8388608 | tf_op jit(solution)/shard_map/all_to_all | solution.py:22
  207.4 8.9 %fusion.20 = f32[1152,768]{1,0:T(8,128)} fusion(bf16[1,4096,768]{2,1,0:T(8,128)(2,1)} %param.20, bf16[128,2048]{1,0:T(8,128)(2,1)S(1)} %get-tuple-element.14, bf16[1024,2048]{1,0:T(8,128)(2,1)} %bitcast.22), kind=kOutput, calls=%fused_computation.33 | convolution fusion | flops 3633315840 | bytes 11403264 | tf_op jit(solution)/shard_map/dot_general | solution.py:170
  216.3 7.8 %fusion.23 = f32[1152,768]{1,0:T(8,128)} fusion(bf16[1,4096,768]{2,1,0:T(8,128)(2,1)S(1)} %bitcast.150, bf16[128,2048]{1,0:T(8,128)(2,1)S(1)} %get-tuple-element.14, bf16[1024,2048]{1,0:T(8,128)(2,1)} %bitcast.22), kind=kOutput, calls=%fused_computation.36 | convolution fusion | flops 3633315840 | bytes 11403264 | tf_op jit(solution)/shard_map/dot_general | solution.py:169
  224.1 33.2 %all-to-all-done.3 = bf16[128,8,2048]{2,1,0:T(8,128)(2,1)} async-done(((bf16[128,8,2048]{2,1,0:T(8,128)(2,1)}), bf16[128,8,2048]{2,1,0:T(8,128)(2,1)}, u32[]{:S(2)}, u32[]{:S(2)}) %all-to-all-start.3) | async-done | bytes 4194336 | tf_op jit(solution)/shard_map/all_to_all | solution.py:22
  257.3 8.3 %convolution_add_fusion.1 = f32[1152,768]{1,0:T(8,128)S(1)} fusion(f32[1152,768]{1,0:T(8,128)} %fusion.23, bf16[1,4096,768]{2,1,0:T(8,128)(2,1)} %param.19, bf16[128,2048]{1,0:T(8,128)(2,1)S(1)} %get-tuple-element.13, bf16[1024,2048]{1,0:T(8,128)(2,1)} %bitcast.25), kind=kOutput, calls=%fused_computation.28 | convolution fusion | flops 3634200576 | bytes 14942208 | tf_op jit(solution)/shard_map/dot_general | solution.py:169
  265.6 8.2 %fusion.16 = bf16[1152,768]{1,0:T(8,128)(2,1)S(1)} fusion(f32[1152,768]{1,0:T(8,128)S(1)} %copy-done.12, f32[1152,768]{1,0:T(8,128)S(1)} %convolution_add_fusion.1, bf16[1,4096,768]{2,1,0:T(8,128)(2,1)} %param.20, bf16[128,2048]{1,0:T(8,128)(2,1)S(1)} %get-tuple-element.13, bf16[1024,2048]{1,0:T(8,128)(2,1)} %bitcast.25), kind=kOutput, calls=%fused_computation.29 | convolution fusion | flops 3639508992 | bytes 16711680 | tf_op jit(solution)/shard_map/dot_general | solution.py:170
  276.2 5.7 %all-to-all-start.5 = ((bf16[128,8,512]{2,1,0:T(8,128)(2,1)}), bf16[128,8,512]{2,1,0:T(8,128)(2,1)S(1)}, u32[]{:S(2)}, u32[]{:S(2)}) async-start(bf16[128,8,512]{2,1,0:T(8,128)(2,1)} %bitcast.132), calls=%async_computation.5 | async-start | bytes 2097152 | tf_op jit(solution)/shard_map/all_to_all | solution.py:22
  281.9 7.8 %convert_bitcast_fusion.1 = bf16[128,8,2048]{2,1,0:T(8,128)(2,1)} fusion(bf16[768,4096]{1,0:T(8,128)(2,1)} %bitcast.125, bf16[1152,768]{1,0:T(8,128)(2,1)} %copy-done.8), kind=kOutput, calls=%fused_computation.23 | convolution fusion | flops 3223322624 | bytes 8912896 | tf_op jit(solution)/shard_map/dot_general | solution.py:179
  289.6 11.0 %all-to-all-done.5 = bf16[128,8,512]{2,1,0:T(8,128)(2,1)S(1)} async-done(((bf16[128,8,512]{2,1,0:T(8,128)(2,1)}), bf16[128,8,512]{2,1,0:T(8,128)(2,1)S(1)}, u32[]{:S(2)}, u32[]{:S(2)}) %all-to-all-start.5) | async-done | bytes 1048608 | tf_op jit(solution)/shard_map/all_to_all | solution.py:22
  300.7 5.8 %all-to-all-start.4 = ((bf16[128,8,2048]{2,1,0:T(8,128)(2,1)}), bf16[128,8,2048]{2,1,0:T(8,128)(2,1)}, u32[]{:S(2)}, u32[]{:S(2)}) async-start(bf16[128,8,2048]{2,1,0:T(8,128)(2,1)} %convert_bitcast_fusion.1), calls=%async_computation.4 | async-start | bytes 8388608 | tf_op jit(solution)/shard_map/all_to_all | solution.py:22
  306.5 7.8 %convert_bitcast_fusion = bf16[128,8,2048]{2,1,0:T(8,128)(2,1)} fusion(bf16[768,4096]{1,0:T(8,128)(2,1)} %bitcast.126, bf16[1152,768]{1,0:T(8,128)(2,1)} %copy-done.8), kind=kOutput, calls=%fused_computation.22 | convolution fusion | flops 3223322624 | bytes 8912896 | tf_op jit(solution)/shard_map/dot_general | solution.py:179
  314.4 44.2 %all-to-all-done.4 = bf16[128,8,2048]{2,1,0:T(8,128)(2,1)} async-done(((bf16[128,8,2048]{2,1,0:T(8,128)(2,1)}), bf16[128,8,2048]{2,1,0:T(8,128)(2,1)}, u32[]{:S(2)}, u32[]{:S(2)}) %all-to-all-start.4) | async-done | bytes 4194336 | tf_op jit(solution)/shard_map/all_to_all | solution.py:22
  358.6 6.4 %all-to-all-start.6 = ((bf16[128,8,2048]{2,1,0:T(8,128)(2,1)}), bf16[128,8,2048]{2,1,0:T(8,128)(2,1)}, u32[]{:S(2)}, u32[]{:S(2)}) async-start(bf16[128,8,2048]{2,1,0:T(8,128)(2,1)} %convert_bitcast_fusion), calls=%async_computation.6 | async-start | bytes 8388608 | tf_op jit(solution)/shard_map/all_to_all | solution.py:22
  366.8 5.0 %fusion.7 = f32[256,2048]{1,0:T(8,128)} fusion(bf16[128,2048]{1,0:T(8,128)(2,1)S(1)} %get-tuple-element.11, bf16[1024,2048]{1,0:T(8,128)(2,1)} %bitcast.31, bf16[128,1152]{0,1:T(8,128)(2,1)S(1)} %subtract_convert_fusion, bf16[128,1152]{0,1:T(8,128)(2,1)S(1)} %fusion.51), kind=kOutput, calls=%fused_computation.13 | convolution fusion | flops 1218576384 | bytes 7405568 | tf_op jit(solution)/shard_map/dot_general | solution.py:182
  371.9 45.1 %all-to-all-done.6 = bf16[128,8,2048]{2,1,0:T(8,128)(2,1)} async-done(((bf16[128,8,2048]{2,1,0:T(8,128)(2,1)}), bf16[128,8,2048]{2,1,0:T(8,128)(2,1)}, u32[]{:S(2)}, u32[]{:S(2)}) %all-to-all-start.6) | async-done | bytes 4194336 | tf_op jit(solution)/shard_map/all_to_all | solution.py:22
  (125 shorter events, 70.4 us)
Async XLA Ops:
  0.0 15.6 %copy-start.2 = (bf16[1,128,4096]{2,1,0:T(8,128)(2,1)S(1)}, bf16[1,128,4096]{2,1,0:T(8,128)(2,1)}, u32[]{:S(2)}) copy-start(bf16[1,128,4096]{2,1,0:T(8,128)(2,1)} %param.12) | copy-start | bytes 3145732
  2.2 23.0 %all-to-all-start = ((bf16[8,128,512]{1,2,0:T(8,128)(2,1)}), bf16[8,128,512]{1,2,0:T(8,128)(2,1)S(1)}, u32[]{:S(2)}, u32[]{:S(2)}) async-start(bf16[8,128,512]{1,2,0:T(8,128)(2,1)} %broadcast_in_dim.71), calls=%async_computation | async-start | bytes 2097152 | tf_op jit(solution)/shard_map/all_to_all | solution.py:22
  12.3 57.1 %collective-permute-start = (bf16[2048,512]{1,0:T(8,128)(2,1)}, bf16[2048,512]{1,0:T(8,128)(2,1)}, u32[]{:S(2)}, u32[]{:S(2)}) collective-permute-start(bf16[2048,512]{1,0:T(8,128)(2,1)} %constant_dynamic-slice_fusion), channel_id=1, source_target_pairs={{0,20},{1,21},{2,22},{3,23},{4,16},{5,17},{6,18},{7,19},{8,28},{9,... | collective-permute-start | bytes 6291464 | tf_op jit(solution)/shard_map/ppermute | solution.py:46
  40.2 36.9 %copy-start.4 = (bf16[128,2,16,128]{0,3,2,1:T(8,128)(2,1)}, bf16[128,2,16,128]{0,3,2,1:T(8,128)(2,1)S(1)}, u32[]{:S(2)}) copy-start(bf16[128,2,16,128]{0,3,2,1:T(8,128)(2,1)S(1)} %fusion.29) | copy-start | bytes 3145732
  40.2 32.4 %collective-permute-start.2 = (bf16[128,4096]{0,1:T(8,128)(2,1)S(1)}, bf16[128,4096]{0,1:T(8,128)(2,1)S(1)}, u32[]{:S(2)}, u32[]{:S(2)}) collective-permute-start(bf16[128,4096]{0,1:T(8,128)(2,1)S(1)} %bitcast.140), channel_id=1, source_target_pairs={{0,1},{1,2},{2,3},{3,0},{4,5},{5,6},{6,7},{7,4},{8,9},{9,10},{10,1... | collective-permute-start | bytes 3145736 | tf_op jit(solution)/shard_map/ppermute | solution.py:39
  41.0 33.2 %collective-permute-start.5 = (bf16[128,4096]{0,1:T(8,128)(2,1)S(1)}, bf16[128,4096]{0,1:T(8,128)(2,1)S(1)}, u32[]{:S(2)}, u32[]{:S(2)}) collective-permute-start(bf16[128,4096]{0,1:T(8,128)(2,1)S(1)} %bitcast.141), channel_id=1, source_target_pairs={{0,3},{1,0},{2,1},{3,2},{4,7},{5,4},{6,5},{7,6},{8,11},{9,8},{10,9... | collective-permute-start | bytes 3145736 | tf_op jit(solution)/shard_map/ppermute | solution.py:39
  44.0 32.3 %copy-start = (bf16[4096,512]{1,0:T(8,128)(2,1)S(1)}, bf16[4096,512]{1,0:T(8,128)(2,1)}, u32[]{:S(2)}) copy-start(bf16[4096,512]{1,0:T(8,128)(2,1)} %param.15) | copy-start | bytes 12582916
  69.4 20.0 %collective-permute-start.1 = (bf16[2048,512]{1,0:T(8,128)(2,1)}, bf16[2048,512]{1,0:T(8,128)(2,1)S(1)}, u32[]{:S(2)}, u32[]{:S(2)}) collective-permute-start(bf16[2048,512]{1,0:T(8,128)(2,1)} %collective-permute-done), channel_id=1, source_target_pairs={{0,8},{8,0},{1,9},{9,1},{2,10},{10,2},{3,11},{11,3},{4,12},{12,4},... | collective-permute-start | bytes 6291464 | tf_op jit(solution)/shard_map/ppermute | solution.py:47
  72.6 15.6 %collective-permute-start.4 = (bf16[128,2048]{0,1:T(8,128)(2,1)S(1)}, bf16[128,2048]{0,1:T(8,128)(2,1)S(1)}, u32[]{:S(2)}, u32[]{:S(2)}) collective-permute-start(bf16[128,2048]{0,1:T(8,128)(2,1)S(1)} %slice.115), channel_id=1, source_target_pairs={{0,1},{1,2},{2,3},{3,0},{4,5},{5,6},{6,7},{7,4},{8,9},{9,10},{10,1... | collective-permute-start | bytes 1572872 | tf_op jit(solution)/shard_map/ppermute | solution.py:39
  74.2 14.3 %collective-permute-start.6 = (bf16[128,2048]{0,1:T(8,128)(2,1)S(1)}, bf16[128,2048]{0,1:T(8,128)(2,1)S(1)}, u32[]{:S(2)}, u32[]{:S(2)}) collective-permute-start(bf16[128,2048]{0,1:T(8,128)(2,1)S(1)} %slice.116), channel_id=1, source_target_pairs={{0,3},{1,0},{2,1},{3,2},{4,7},{5,4},{6,5},{7,6},{8,11},{9,8},{10,9... | collective-permute-start | bytes 1572872 | tf_op jit(solution)/shard_map/ppermute | solution.py:39
  92.9 9.5 %collective-permute-start.8 = (bf16[128,1024]{1,0:T(8,128)(2,1)S(1)}, bf16[128,1024]{1,0:T(8,128)(2,1)}, u32[]{:S(2)}, u32[]{:S(2)}) collective-permute-start(bf16[128,1024]{1,0:T(8,128)(2,1)S(1)} %pad_maximum_fusion.14), channel_id=1, source_target_pairs={{0,1},{1,2},{2,3},{3,0},{4,5},{5,6},{6,7},{7,4},{8,9},{9,10},{10,1... | collective-permute-start | bytes 786440 | tf_op jit(solution)/shard_map/ppermute | solution.py:39
  94.4 14.1 %collective-permute-start.7 = (bf16[128,1024]{1,0:T(8,128)(2,1)S(1)}, bf16[128,1024]{1,0:T(8,128)(2,1)S(1)}, u32[]{:S(2)}, u32[]{:S(2)}) collective-permute-start(bf16[128,1024]{1,0:T(8,128)(2,1)S(1)} %pad_maximum_fusion.13), channel_id=1, source_target_pairs={{0,2},{1,3},{2,0},{3,1},{4,6},{5,7},{6,4},{7,5},{8,10},{9,11},{10,... | collective-permute-start | bytes 786440 | tf_op jit(solution)/shard_map/ppermute | solution.py:39
  98.3 10.4 %collective-permute-start.3 = (bf16[128,1024]{1,0:T(8,128)(2,1)S(1)}, bf16[128,1024]{1,0:T(8,128)(2,1)}, u32[]{:S(2)}, u32[]{:S(2)}) collective-permute-start(bf16[128,1024]{1,0:T(8,128)(2,1)S(1)} %pad_maximum_fusion.12), channel_id=1, source_target_pairs={{0,3},{1,0},{2,1},{3,2},{4,7},{5,4},{6,5},{7,6},{8,11},{9,8},{10,9... | collective-permute-start | bytes 786440 | tf_op jit(solution)/shard_map/ppermute | solution.py:39
  114.5 26.7 %all-to-all-start.2 = ((bf16[128,8,512]{2,1,0:T(8,128)(2,1)}), bf16[128,8,512]{2,1,0:T(8,128)(2,1)}, u32[]{:S(2)}, u32[]{:S(2)}) async-start(bf16[128,8,512]{2,1,0:T(8,128)(2,1)} %bitcast.131), calls=%async_computation.2 | async-start | bytes 2097152 | tf_op jit(solution)/shard_map/all_to_all | solution.py:22
  141.2 57.9 %all-to-all-start.1 = ((bf16[128,8,2048]{2,1,0:T(8,128)(2,1)}), bf16[128,8,2048]{2,1,0:T(8,128)(2,1)}, u32[]{:S(2)}, u32[]{:S(2)}) async-start(bf16[128,8,2048]{2,1,0:T(8,128)(2,1)} %convert_bitcast_fusion.3), calls=%async_computation.1 | async-start | bytes 8388608 | tf_op jit(solution)/shard_map/all_to_all | solution.py:22
  199.0 58.3 %all-to-all-start.3 = ((bf16[128,8,2048]{2,1,0:T(8,128)(2,1)}), bf16[128,8,2048]{2,1,0:T(8,128)(2,1)}, u32[]{:S(2)}, u32[]{:S(2)}) async-start(bf16[128,8,2048]{2,1,0:T(8,128)(2,1)} %convert_bitcast_fusion.2), calls=%async_computation.3 | async-start | bytes 8388608 | tf_op jit(solution)/shard_map/all_to_all | solution.py:22
  205.5 10.8 %slice-start.2 = ((s8[6291456]{0:T(1024)(128)(4,1)}), s8[4194304]{0:T(1024)(128)(4,1)S(1)}, s32[]{:S(2)}) async-start(s8[6291456]{0:T(1024)(128)(4,1)} %bitcast.149), calls=%async_computation.9 | async-start | bytes 8388608
  207.4 8.9 %slice-start.3 = ((s8[6291456]{0:T(1024)(128)(4,1)}), s8[2097152]{0:T(1024)(128)(4,1)S(1)}, s32[]{:S(2)}) async-start(s8[6291456]{0:T(1024)(128)(4,1)} %bitcast.149), calls=%async_computation.10 | async-start | bytes 4194304
  257.3 8.3 %copy-start.12 = (f32[1152,768]{1,0:T(8,128)S(1)}, f32[1152,768]{1,0:T(8,128)}, u32[]{:S(2)}) copy-start(f32[1152,768]{1,0:T(8,128)} %fusion.20) | copy-start | bytes 10616836
  257.3 16.5 %slice-start = ((s8[6291456]{0:T(1024)(128)(4,1)}), s8[4194304]{0:T(1024)(128)(4,1)S(1)}, s32[]{:S(2)}) async-start(s8[6291456]{0:T(1024)(128)(4,1)} %bitcast.127), calls=%async_computation.7 | async-start | bytes 8388608
  276.2 24.5 %all-to-all-start.5 = ((bf16[128,8,512]{2,1,0:T(8,128)(2,1)}), bf16[128,8,512]{2,1,0:T(8,128)(2,1)S(1)}, u32[]{:S(2)}, u32[]{:S(2)}) async-start(bf16[128,8,512]{2,1,0:T(8,128)(2,1)} %bitcast.132), calls=%async_computation.5 | async-start | bytes 2097152 | tf_op jit(solution)/shard_map/all_to_all | solution.py:22
  300.7 57.9 %all-to-all-start.4 = ((bf16[128,8,2048]{2,1,0:T(8,128)(2,1)}), bf16[128,8,2048]{2,1,0:T(8,128)(2,1)}, u32[]{:S(2)}, u32[]{:S(2)}) async-start(bf16[128,8,2048]{2,1,0:T(8,128)(2,1)} %convert_bitcast_fusion.1), calls=%async_computation.4 | async-start | bytes 8388608 | tf_op jit(solution)/shard_map/all_to_all | solution.py:22
  314.4 50.7 %copy-start.10 = (f32[1,128,8]{1,2,0:T(8,128)S(1)}, f32[1,128,8]{1,2,0:T(8,128)}, u32[]{:S(2)}) copy-start(f32[1,128,8]{1,2,0:T(8,128)} %param.18) | copy-start | bytes 12292
  358.6 58.4 %all-to-all-start.6 = ((bf16[128,8,2048]{2,1,0:T(8,128)(2,1)}), bf16[128,8,2048]{2,1,0:T(8,128)(2,1)}, u32[]{:S(2)}, u32[]{:S(2)}) async-start(bf16[128,8,2048]{2,1,0:T(8,128)(2,1)} %convert_bitcast_fusion), calls=%async_computation.6 | async-start | bytes 8388608 | tf_op jit(solution)/shard_map/all_to_all | solution.py:22
  (9 other events, 31.6 us)

commit v2 on v1

v2 whole, which is shorter than its diff:
```python
import jax
import jax.numpy as jnp
from jax import lax
from jax.experimental import pallas as pl
from jax.experimental.pallas import tpu as pltpu
from jax.sharding import Mesh, PartitionSpec as P


HQ = 32
KVH = 2
DH = 128
EXPERTS = 128
FULL = 8
SLOTS = EXPERTS * FULL
WIDTH = 4096
PACK = WIDTH // 8
OUT_FIRST = 3072
BACK_FIRST = 1024
TILE = 256

DP = ("z", "xl", "core")
CTX = ("xh", "y")
ALL = DP + CTX
BF = jnp.bfloat16
F32 = jnp.float32


def exchange(blocks, axes):
    return lax.all_to_all(blocks, axes, split_axis=0, concat_axis=0, tiled=True)


def neighbour_pairs():
    pairs = []
    for z in range(4):
        for xl in range(2):
            for core in range(2):
                for xh in range(2):
                    for y in range(4):
                        src = (((z * 2 + xl) * 2 + core) * 2 + xh) * 4 + y
                        dst = (((z * 2 + 1 - xl) * 2 + core) * 2 + 1 - xh) * 4 + y
                        pairs.append((src, dst))
    return pairs


def shift(block, step):
    return lax.ppermute(block, "y", [(i, (i + step) % 4) for i in range(4)])


def attention(queries, keys, values):
    tok_count = queries.shape[0]
    group_size = HQ // KVH
    ctx_index = lax.axis_index(CTX)
    query_rows = queries.reshape(tok_count, KVH, group_size, DH)
    query_pos = ctx_index * tok_count + jnp.arange(tok_count, dtype=jnp.int32)
    pair = jnp.concatenate([keys, values], axis=1)
    width = keys.shape[1]
    gathered = exchange(jnp.broadcast_to(pair[None], (8,) + pair.shape), CTX)
    gathered = gathered.reshape(8 * tok_count, 2 * width)
    key_count = gathered.shape[0]
    key_pos = jnp.arange(key_count, dtype=jnp.int32)
    causal = key_pos[None, :] <= query_pos[:, None]
    outs = []
    for head in range(KVH):
        key_rows = gathered[:, head * DH : (head + 1) * DH]
        value_rows = gathered[:, width + head * DH : width + (head + 1) * DH]
        scores = (
            jnp.einsum("qgd,jd->gqj", query_rows[:, head], key_rows, preferred_element_type=F32)
            * DH ** (-0.5)
        )
        scores = jnp.where(causal, scores, -1e30)
        row_max = jnp.max(scores, axis=-1, keepdims=True)
        weights = jnp.where(causal, jnp.exp(scores - row_max), 0.0)
        total = jnp.sum(weights, axis=-1)
        numerator = jnp.einsum(
            "gqj,jd->gqd", weights.astype(BF), value_rows, preferred_element_type=F32
        )
        attended = numerator / total[..., None]
        outs.append(jnp.transpose(attended, (1, 0, 2)).reshape(tok_count, group_size * DH).astype(BF))
    return outs


def project(attended, out_weight):
    first, second = attended
    tok, half = first.shape
    core = lax.axis_index("core")
    mine = lax.dynamic_slice_in_dim(out_weight, core * half, half, axis=0)
    fetched = lax.ppermute(mine, ALL, neighbour_pairs())
    below_a, above_a = shift(first, 1), shift(first, -1)
    below_b, above_b = shift(second, 1), shift(second, -1)
    far_a = shift(below_a, 1)
    far_b = shift(above_b, -1)
    other = lax.ppermute(fetched, "core", [(0, 1), (1, 0)])
    partner_a = jnp.where(core == 0, fetched, other)
    partner_b = jnp.where(core == 0, other, fetched)

    def columns(rows_a, rows_b):
        def product(top, bottom):
            return (
                jnp.dot(rows_a, top, preferred_element_type=F32)
                + jnp.dot(rows_b, bottom, preferred_element_type=F32)
            ).astype(BF)

        own = product(out_weight[:half], out_weight[half:])
        return jnp.concatenate([own, product(partner_a, partner_b)], axis=1)

    here = columns(first, second)
    from_above = shift(columns(below_a, below_b), -1)
    from_below = shift(columns(above_a, above_b), 1)
    from_far = shift(columns(far_a, far_b), 2)
    y = lax.axis_index("y")
    xh = lax.axis_index("xh")
    ring = jnp.stack([here, from_above, from_far, from_below])
    own_first = ring.reshape(4, tok, 2, 512).transpose(2, 0, 1, 3)
    turned = lax.dynamic_slice_in_dim(
        jnp.concatenate([own_first, own_first], axis=1), (4 - y) % 4, 4, axis=1
    )
    turned = jnp.where(xh == 0, turned, turned[::-1])
    return turned.reshape(8, tok, 512).transpose(1, 0, 2).reshape(tok, 2 * half)


def product(left, right):
    return jnp.dot(left, right, preferred_element_type=F32)


def shuffle(packing):
    by_row = lax.broadcasted_iota(jnp.int32, (128, 128), 0 if packing else 1)
    by_piece = lax.broadcasted_iota(jnp.int32, (128, 128), 1 if packing else 0)
    return (lax.rem(by_row, 8) * 16 + lax.div(by_row, 8) == by_piece).astype(F32).astype(BF)


def pack(rows, out_ref, start):
    order = shuffle(True)
    for i in range(EXPERTS // 16):
        pieces = [rows[16 * i : 16 * i + 16, PACK * s : PACK * (s + 1)] for s in range(8)]
        packed = product(order, jnp.concatenate(pieces, axis=0))
        out_ref[128 * i : 128 * (i + 1), start : start + PACK] = packed.astype(BF)


def unpack(in_ref, start, rows):
    order = shuffle(False)
    for i in range(EXPERTS // 16):
        packed = in_ref[128 * i : 128 * (i + 1), start : start + PACK]
        pieces = product(order, packed).astype(BF)
        for s in range(8):
            rows[16 * i : 16 * i + 16, PACK * s : PACK * (s + 1)] = pieces[16 * s : 16 * s + 16]


def tiles(count, body):
    def step(i, carry):
        body(pl.ds(pl.multiple_of(i * TILE, TILE), TILE))
        return carry

    lax.fori_loop(0, count // TILE, step, 0)


def make_kernel(normed_ref, pick_ref, last_ref, out_ref, rows):
    rows[...] = product(last_ref[...], normed_ref[...]).astype(BF)
    pack(rows, out_ref, OUT_FIRST)

    def body(at):
        out_ref[at, :OUT_FIRST] = product(pick_ref[at], normed_ref[:, :OUT_FIRST]).astype(BF)

    tiles(SLOTS, body)


def silu_product(gated, lifted):
    return (gated / (1.0 + jnp.exp(-gated)) * lifted).astype(BF)


def first_kernel(got_ref, gate_ref, up_ref, down_ref, gated_ref, lifted_ref, last_ref, rows):
    def body(at):
        x = got_ref[at, :OUT_FIRST]
        gated_ref[at] = product(x, gate_ref[:OUT_FIRST])
        lifted_ref[at] = product(x, up_ref[:OUT_FIRST])

    tiles(SLOTS, body)
    unpack(got_ref, OUT_FIRST, rows)
    x = rows[...]
    activated = silu_product(product(x, gate_ref[...]), product(x, up_ref[...]))
    rows[...] = product(activated, down_ref[...]).astype(BF)
    pack(rows, last_ref, 0)


def second_kernel(got_ref, gate_ref, up_ref, down_ref, gated_ref, lifted_ref, last_ref, act_ref, out_ref):
    def body(at):
        x = got_ref[at]
        gated = gated_ref[at] + product(x, gate_ref[...])
        lifted = lifted_ref[at] + product(x, up_ref[...])
        activated = silu_product(gated, lifted)
        act_ref[at] = activated
        out_ref[at, :BACK_FIRST] = product(activated, down_ref[...]).astype(BF)
        out_ref[at, BACK_FIRST:] = last_ref[at]

    tiles(SLOTS, body)


def finish_kernel(base_ref, split_ref, back_ref, out_ref):
    fixed = BACK_FIRST // PACK

    @pl.when(pl.program_id(0) < fixed)
    def _():
        out_ref[...] = base_ref[...].astype(BF)

    @pl.when(pl.program_id(0) >= fixed)
    def _():
        sums = product(split_ref[...], back_ref[...])
        tok = base_ref.shape[0]
        out_ref[...] = (base_ref[...] + (sums[:tok] + sums[tok:])).astype(BF)


def whole(shape, index=(0, 0)):
    return pl.BlockSpec(shape, lambda i: index)


def call(body, grid, in_specs, out_specs, out_shape, scratch=(), flops=0, moved=0):
    return pl.pallas_call(
        body,
        grid=grid,
        in_specs=in_specs,
        out_specs=out_specs,
        out_shape=out_shape,
        scratch_shapes=scratch,
        compiler_params=pltpu.CompilerParams(vmem_limit_bytes=56 * 1024 * 1024),
        cost_estimate=pl.CostEstimate(flops=flops, bytes_accessed=moved, transcendentals=0),
    )


def two_terms(weigh):
    high = weigh.astype(BF)
    low = (weigh - high.astype(F32)).astype(BF)
    return jnp.concatenate([high, low], axis=0)


def slots_of(routes, slot_gates):
    tok = routes.shape[0]
    named = routes[:, :, None] == jnp.arange(EXPERTS, dtype=jnp.int32)[None, None, :]
    hit = jnp.any(named, axis=1)
    gate = jnp.sum(jnp.where(named, slot_gates[:, :, None], 0.0), axis=1)
    before = jnp.arange(tok)[None, :] < jnp.arange(tok)[:, None]
    rank = jnp.dot(before.astype(BF), hit.astype(BF), preferred_element_type=F32)
    return hit, jnp.where(hit, rank, -1.0), gate


def layer(
    hidden,
    queries,
    keys,
    values,
    out_weight,
    norm_gain,
    routes,
    slot_scores,
    gate_weight,
    up_weight,
    down_weight,
):
    tok, _ = hidden.shape[1:]
    attended = attention(queries[0], keys[0], values[0])

    score_rows = slot_scores[0]
    slot_gates = score_rows / jnp.sum(score_rows, axis=1, keepdims=True)
    _, rank, gate = slots_of(routes[0], slot_gates)
    places = jnp.arange(FULL, dtype=F32)
    pick = (rank.T[:, None, :] == places[None, :, None]).astype(BF).reshape(EXPERTS * FULL, tok)
    pick_last = (rank.T == float(FULL)).astype(BF)
    weigh = jnp.where(rank[:, :, None] == places, gate[:, :, None], 0.0).reshape(tok, EXPERTS * FULL)
    weigh_last = jnp.where(rank == float(FULL), gate, 0.0)
    split, split_last = two_terms(weigh), two_terms(weigh_last)

    projected = project(attended, out_weight)
    residual = hidden[0].astype(F32) + projected.astype(F32)
    normed = (
        residual
        * lax.rsqrt(jnp.mean(residual * residual, axis=1, keepdims=True) + 1e-06)
        * norm_gain
    ).astype(BF)

    hid = gate_weight.shape[2]
    w_gate, w_up, w_down = gate_weight[0], up_weight[0], down_weight[0]
    shape = jax.ShapeDtypeStruct
    rest = WIDTH - OUT_FIRST
    send_first = OUT_FIRST + PACK
    back_first = BACK_FIRST + PACK
    nine = pltpu.VMEM((EXPERTS, WIDTH), BF)

    sent = call(
        make_kernel, (1,),
        [whole((tok, WIDTH)), whole((SLOTS, tok)), whole((EXPERTS, tok))],
        whole((SLOTS, send_first)), shape((SLOTS, send_first), BF), [nine],
        flops=2 * SLOTS * tok * send_first, moved=SLOTS * send_first * 2,
    )(normed, pick, pick_last)
    got = exchange(sent.reshape(EXPERTS, FULL, send_first), ALL).reshape(SLOTS, send_first)
    sent_rest = product(pick, normed[:, OUT_FIRST:]).astype(BF)
    got_rest = exchange(sent_rest.reshape(EXPERTS, FULL, rest), ALL).reshape(SLOTS, rest)
    gated, lifted, last = call(
        first_kernel, (1,),
        [whole((SLOTS, send_first)), whole((WIDTH, hid)), whole((WIDTH, hid)), whole((hid, WIDTH))],
        [whole((SLOTS, hid)), whole((SLOTS, hid)), whole((SLOTS, PACK))],
        [shape((SLOTS, hid), F32), shape((SLOTS, hid), F32), shape((SLOTS, PACK), BF)], [nine],
        flops=4 * SLOTS * OUT_FIRST * hid, moved=SLOTS * (send_first + 4 * hid) * 2 + WIDTH * hid * 6,
    )(got, w_gate, w_up, w_down)
    activated, served = call(
        second_kernel, (1,),
        [
            whole((SLOTS, rest)), whole((rest, hid), (OUT_FIRST // rest, 0)),
            whole((rest, hid), (OUT_FIRST // rest, 0)), whole((hid, BACK_FIRST)),
            whole((SLOTS, hid)), whole((SLOTS, hid)), whole((SLOTS, PACK)),
        ],
        [whole((SLOTS, hid)), whole((SLOTS, back_first))],
        [shape((SLOTS, hid), BF), shape((SLOTS, back_first), BF)],
        flops=6 * SLOTS * rest * hid, moved=SLOTS * (rest + back_first + 4 * hid) * 2 + rest * hid * 6,
    )(got_rest, w_gate, w_up, w_down, gated, lifted, last)
    back = exchange(served.reshape(EXPERTS, FULL, back_first), ALL).reshape(SLOTS, back_first)
    served_rest = product(activated, w_down[:, BACK_FIRST:]).astype(BF)
    back_rest = exchange(
        served_rest.reshape(EXPERTS, FULL, WIDTH - BACK_FIRST), ALL
    ).reshape(SLOTS, WIDTH - BACK_FIRST)

    sums = product(split, back[:, :BACK_FIRST])
    nines = product(split_last, back[:, BACK_FIRST:].reshape(EXPERTS, WIDTH))
    base = residual + (nines[:tok] + nines[tok:])
    base = jnp.concatenate(
        [base[:, :BACK_FIRST] + (sums[:tok] + sums[tok:]), base[:, BACK_FIRST:]], axis=1
    )
    fixed = BACK_FIRST // PACK
    out = call(
        finish_kernel, (WIDTH // PACK,),
        [
            pl.BlockSpec((tok, PACK), lambda i: (0, i)),
            whole((2 * tok, SLOTS)),
            pl.BlockSpec((SLOTS, PACK), lambda i: (0, jnp.maximum(i - fixed, 0))),
        ],
        pl.BlockSpec((tok, PACK), lambda i: (0, i)), shape((tok, WIDTH), BF),
        flops=4 * tok * SLOTS * WIDTH, moved=SLOTS * WIDTH * 2,
    )(base, split, back_rest)
    return out[None]


def solution(mesh):
    fine = Mesh(mesh.devices.reshape(4, 2, 2, 2, 4), ALL)
    return jax.shard_map(
        layer,
        mesh=fine,
        in_specs=(
            P(DP, CTX, None),
            P(DP, CTX, None),
            P(DP, CTX, None),
            P(DP, CTX, None),
            P(None, CTX),
            P(),
            P(DP, CTX, None),
            P(DP, CTX, None),
            P(ALL, None, None),
            P(ALL, None, None),
            P(ALL, None, None),
        ),
        out_specs=P(DP, CTX, None),
        check_vma=False,
    )
```

time: 431 us -> 406 us (0.942)
  Pallas kernels: 0 us -> 51.4 us
  matrix products: 89.2 us -> 47.5 us
  waiting for transfers between devices: 250 us -> 220 us
  starting transfers between devices: 61.2 us -> 46.7 us
  other arithmetic: 7.39 us -> 13 us
  local copies, waits for them, and re-layouts: 14.7 us -> 19.3 us
    pallas_call x0 -> x4, Pallas kernels: none -> 51.4 us  [the longest x1 23.2 us: layer(): call(first_kernel, (1,), [whole((SLOTS, send_first)), whole((WIDTH, hid))...]
    dot_general x21 -> x22, matrix products: 79 us -> 33 us  [the longest x4 16.4 us: product(): return jnp.dot(left, right, preferred_element_type=F32)]
    all_to_all x7 -> x5, waiting for transfers between devices: 207 us -> 190 us  [exchange(): return lax.all_to_all(blocks, axes, split_axis=0, concat_axis=0, tiled=True)]
    ppermute x2, waiting for transfers between devices: 25.4 us -> 9.22 us  [the longest x1 9.22 us: project(): fetched = lax.ppermute(mine, ALL, neighbour_pairs())]
    all_to_all x7 -> x5, starting transfers between devices: 45.5 us -> 32.1 us  [exchange(): return lax.all_to_all(blocks, axes, split_axis=0, concat_axis=0, tiled=True)]
    convert_element_type x4 -> x7, other arithmetic: 0.98 us -> 6.34 us  [the longest x2 1.87 us: two_terms(): high = weigh.astype(BF)]
    ppermute x7 -> x9, waiting for transfers between devices: 17.7 us -> 21.3 us  [shift(): return lax.ppermute(block, 'y', [(i, (i + step) % 4) for i in range(4)])]
    sub x1 -> x2, matrix products: 10 us -> 13.7 us  [attention(): weights = jnp.where(causal, jnp.exp(scores - row_max), 0.0)]
  transfers between devices with their start and end apart: 16 -> 16, of which waited for: 12 -> 11; matrix products, arithmetic and copies ran while one was open for 18% -> 17% of each run, Pallas kernels for 0% -> 6%
where the time goes in v2:
time: 406 us; the launch traced here: 399 us
  waiting for transfers between devices  220 us (54%)
  Pallas kernels  51.4 us (13%)
  matrix products  47.5 us (12%)
  starting transfers between devices  46.7 us (12%)
  local copies, waits for them, and re-layouts  19.3 us (5%)
  other arithmetic  13 us (3%)
    all_to_all x5, waiting for transfers between devices, exchange(): return lax.all_to_all(blocks, axes, split_axis=0, concat_axis=0, tiled=True)  190 us
    all_to_all x5, starting transfers between devices, exchange(): return lax.all_to_all(blocks, axes, split_axis=0, concat_axis=0, tiled=True)  32.1 us
    pallas_call x1, Pallas kernels, layer(): call(first_kernel, (1,), [whole((SLOTS, send_first)), whole((WIDTH, hid))...  23.2 us
    ppermute x9, waiting for transfers between devices, shift(): return lax.ppermute(block, 'y', [(i, (i + step) % 4) for i in range(4)])  21.3 us
    dot_general x4, matrix products, product(): return jnp.dot(left, right, preferred_element_type=F32)  16.4 us
    sub x2, matrix products, attention(): weights = jnp.where(causal, jnp.exp(scores - row_max), 0.0)  13.7 us
    pallas_call x1, Pallas kernels, layer(): call(second_kernel, (1,), [whole((SLOTS, rest)), whole((rest, hid), (OUT_...  12.4 us
    ppermute x9, starting transfers between devices, shift(): return lax.ppermute(block, 'y', [(i, (i + step) % 4) for i in range(4)])  11.7 us
  transfers between devices with their start and end apart: 16, of which 11 were waited for; matrix products, arithmetic and copies ran while one was open for 17% of the time, Pallas kernels for 6%

profile of v2, /device:TPU:0, one launch (start us, length us, event | category | flops | bytes accessed | tf_op | source)
XLA Modules:
  0.0 398.9 jit_solution(3464661034603098869)
XLA Ops:
  5.8 4.7 %all-to-all-start = ((bf16[8,128,512]{2,1,0:T(8,128)(2,1)}), bf16[8,128,512]{2,1,0:T(8,128)(2,1)}, u32[]{:S(2)}, u32[]{:S(2)}) async-start(bf16[8,128,512]{2,1,0:T(8,128)(2,1)} %broadcast_in_dim.77), calls=%async_computation | async-start | bytes 2097152 | tf_op jit(solution)/shard_map/all_to_all | solution.py:29
  15.3 11.0 %all-to-all-done = bf16[8,128,512]{2,1,0:T(8,128)(2,1)} async-done(((bf16[8,128,512]{2,1,0:T(8,128)(2,1)}), bf16[8,128,512]{2,1,0:T(8,128)(2,1)}, u32[]{:S(2)}, u32[]{:S(2)}) %all-to-all-start) | async-done | bytes 1048608 | tf_op jit(solution)/shard_map/all_to_all | solution.py:29
  26.3 6.8 %fusion.104 = (f32[16,128]{1,0:T(8,128)S(1)}, bf16[16,128,1024]{1,2,0:T(8,128)(2,1)}) fusion(pred[128,1024]{0,1:T(8,128)(4,1)S(1)} %iota_compare_fusion.1, bf16[128,2,16,128]{0,3,2,1:T(8,128)(2,1)} %bitcast.189, bf16[1024,512]{1,0:T(8,128)(2,1)} %bitcast.3), kind=kOutput, calls=%fused_computation.126 | convolution fusion | flops 549454848 | bytes 5251072 | tf_op jit(solution)/shard_map/sub | solution.py:72
  33.1 3.8 fusion.46
  39.2 6.8 %fusion.105 = (f32[16,128]{1,0:T(8,128)S(1)}, bf16[16,128,1024]{1,2,0:T(8,128)(2,1)}) fusion(pred[128,1024]{0,1:T(8,128)(4,1)S(1)} %iota_compare_fusion.1, bf16[128,2,16,128]{0,3,2,1:T(8,128)(2,1)} %bitcast.190, bf16[1024,512]{1,0:T(8,128)(2,1)} %bitcast.3), kind=kOutput, calls=%fused_computation.127 | convolution fusion | flops 549454848 | bytes 5251072 | tf_op jit(solution)/shard_map/sub | solution.py:72
  46.0 3.1 fusion.49
  52.5 9.2 %collective-permute-done = bf16[2048,512]{1,0:T(8,128)(2,1)} collective-permute-done((bf16[2048,512]{1,0:T(8,128)(2,1)S(1)}, bf16[2048,512]{1,0:T(8,128)(2,1)}, u32[]{:S(2)}, u32[]{:S(2)}) %collective-permute-start) | collective-permute-done | bytes 2097184 | tf_op jit(solution)/shard_map/ppermute | solution.py:87
  63.7 3.3 collective-permute-start.7
  69.0 9.9 %collective-permute-done.7 = bf16[128,2048]{0,1:T(8,128)(2,1)S(1)} collective-permute-done((bf16[128,2048]{0,1:T(8,128)(2,1)S(1)}, bf16[128,2048]{0,1:T(8,128)(2,1)S(1)}, u32[]{:S(2)}, u32[]{:S(2)}) %collective-permute-start.7) | collective-permute-done | bytes 524320 | tf_op jit(solution)/shard_map/ppermute | solution.py:46
  92.8 5.0 %collective-permute-done.8 = bf16[128,1024]{1,0:T(8,128)(2,1)S(1)} collective-permute-done((bf16[128,1024]{1,0:T(8,128)(2,1)S(1)}, bf16[128,1024]{1,0:T(8,128)(2,1)S(1)}, u32[]{:S(2)}, u32[]{:S(2)}) %collective-permute-start.8) | collective-permute-done | bytes 262176 | tf_op jit(solution)/shard_map/ppermute | solution.py:46
  106.3 7.3 %shard_map.109 = bf16[1024,3584]{1,0:T(8,128)(2,1)} custom-call(bf16[128,4096]{1,0:T(8,128)(2,1)} %multiply_convert_fusion.normed_ref, bf16[1024,128]{1,0:T(8,128)(2,1)} %fusion.86.pick_ref, bf16[128,128]{1,0:T(8,128)(2,1)} %compare_convert_fusion.last_ref), custom_call_target="tpu_custom_call" | custom-call | flops 939524096 | bytes 7340032 | tf_op jit(solution)/shard_map/pallas_call | solution.py:286
  113.7 9.4 %all-to-all-start.2 = ((bf16[128,8,3584]{2,1,0:T(8,128)(2,1)}), bf16[128,8,3584]{2,1,0:T(8,128)(2,1)}, u32[]{:S(2)}, u32[]{:S(2)}) async-start(bf16[128,8,3584]{2,1,0:T(8,128)(2,1)} %bitcast.175), calls=%async_computation.2 | async-start | bytes 14680064 | tf_op jit(solution)/shard_map/all_to_all | solution.py:29
  123.1 3.0 convert_bitcast_fusion.1
  126.1 86.5 %all-to-all-done.2 = bf16[128,8,3584]{2,1,0:T(8,128)(2,1)} async-done(((bf16[128,8,3584]{2,1,0:T(8,128)(2,1)}), bf16[128,8,3584]{2,1,0:T(8,128)(2,1)}, u32[]{:S(2)}, u32[]{:S(2)}) %all-to-all-start.2) | async-done | bytes 7340064 | tf_op jit(solution)/shard_map/all_to_all | solution.py:29
  212.7 6.2 %all-to-all-start.1 = ((bf16[128,8,1024]{2,1,0:T(8,128)(2,1)}), bf16[128,8,1024]{2,1,0:T(8,128)(2,1)}, u32[]{:S(2)}, u32[]{:S(2)}) async-start(bf16[128,8,1024]{2,1,0:T(8,128)(2,1)} %convert_bitcast_fusion.1), calls=%async_computation.1 | async-start | bytes 4194304 | tf_op jit(solution)/shard_map/all_to_all | solution.py:29
  218.9 23.2 %shard_map.110 = (f32[1024,768]{1,0:T(8,128)}, f32[1024,768]{1,0:T(8,128)}, bf16[1024,512]{1,0:T(8,128)(2,1)}) custom-call(bf16[1024,3584]{1,0:T(8,128)(2,1)} %bitcast.36.got_ref, bf16[4096,768]{1,0:T(8,128)(2,1)} %bitcast.177, bf16[4096,768]{1,0:T(8,128)(2,1)} %bitcast.179, bf16[768,4096]{1,0:T(8,128)(2,1)} %bitcast.181), custom_call_target="tpu_custom_call" | custom-call | flops 9663676416 | bytes 32505856 | tf_op jit(solution)/shard_map/pallas_call | solution.py:295
  242.2 6.5 %all-to-all-done.1 = bf16[128,8,1024]{2,1,0:T(8,128)(2,1)} async-done(((bf16[128,8,1024]{2,1,0:T(8,128)(2,1)}), bf16[128,8,1024]{2,1,0:T(8,128)(2,1)}, u32[]{:S(2)}, u32[]{:S(2)}) %all-to-all-start.1) | async-done | bytes 2097184 | tf_op jit(solution)/shard_map/all_to_all | solution.py:29
  248.7 12.4 %shard_map.111 = (bf16[1024,768]{1,0:T(8,128)(2,1)}, bf16[1024,1536]{1,0:T(8,128)(2,1)}) custom-call(bf16[1024,1024]{1,0:T(8,128)(2,1)} %bitcast.31.got_ref, bf16[4096,768]{1,0:T(8,128)(2,1)} %bitcast.178, bf16[4096,768]{1,0:T(8,128)(2,1)} %bitcast.180, bf16[768,4096]{1,0:T(8,128)(2,1)} %bitcast.182, f32[1024,768]{1,0:T(8,128)} %get-tuple-element.10.gated_ref, ...), custom_call_target="tpu_custom_call" | custom-call | flops 4831838208 | bytes 16252928 | tf_op jit(solution)/shard_map/pallas_call | solution.py:302
  261.1 5.7 %all-to-all-start.3 = ((bf16[128,8,1536]{2,1,0:T(8,128)(2,1)}), bf16[128,8,1536]{2,1,0:T(8,128)(2,1)}, u32[]{:S(2)}, u32[]{:S(2)}) async-start(bf16[128,8,1536]{2,1,0:T(8,128)(2,1)} %bitcast.184), calls=%async_computation.3 | async-start | bytes 6291456 | tf_op jit(solution)/shard_map/all_to_all | solution.py:29
  266.8 9.2 %convert_bitcast_fusion = bf16[128,8,3072]{2,1,0:T(8,128)(2,1)} fusion(bf16[1024,768]{1,0:T(8,128)(2,1)} %get-tuple-element.14, bf16[768,4096]{1,0:T(8,128)(2,1)} %bitcast.183), kind=kOutput, calls=%fused_computation.8 | convolution fusion | flops 4834983936 | bytes 12582912 | tf_op jit(solution)/shard_map/dot_general | solution.py:122
  276.0 31.8 %all-to-all-done.3 = bf16[128,8,1536]{2,1,0:T(8,128)(2,1)} async-done(((bf16[128,8,1536]{2,1,0:T(8,128)(2,1)}), bf16[128,8,1536]{2,1,0:T(8,128)(2,1)}, u32[]{:S(2)}, u32[]{:S(2)}) %all-to-all-start.3) | async-done | bytes 3145760 | tf_op jit(solution)/shard_map/all_to_all | solution.py:29
  307.8 6.0 %all-to-all-start.4 = ((bf16[128,8,3072]{2,1,0:T(8,128)(2,1)}), bf16[128,8,3072]{2,1,0:T(8,128)(2,1)}, u32[]{:S(2)}, u32[]{:S(2)}) async-start(bf16[128,8,3072]{2,1,0:T(8,128)(2,1)} %convert_bitcast_fusion), calls=%async_computation.4 | async-start | bytes 12582912 | tf_op jit(solution)/shard_map/all_to_all | solution.py:29
  336.4 54.0 %all-to-all-done.4 = bf16[128,8,3072]{2,1,0:T(8,128)(2,1)} async-done(((bf16[128,8,3072]{2,1,0:T(8,128)(2,1)}), bf16[128,8,3072]{2,1,0:T(8,128)(2,1)}, u32[]{:S(2)}, u32[]{:S(2)}) %all-to-all-start.4) | async-done | bytes 6291488 | tf_op jit(solution)/shard_map/all_to_all | solution.py:29
  390.4 8.3 %shard_map.112 = bf16[128,4096]{1,0:T(8,128)(2,1)} custom-call(f32[128,4096]{1,0:T(8,128)} %pad_maximum_fusion.base_ref, bf16[256,1024]{1,0:T(8,128)(2,1)} %pad_maximum_fusion.1.split_ref, bf16[1024,3072]{1,0:T(8,128)(2,1)} %bitcast.42.back_ref), custom_call_target="tpu_custom_call" | custom-call | flops 2147483648 | bytes 8388608 | tf_op jit(solution)/shard_map/pallas_call | solution.py:326
  (115 shorter events, 64.8 us)
Async XLA Ops:
  0.0 4.7 %copy-start.7 = (bf16[1,128,256]{2,1,0:T(8,128)(2,1)S(1)}, bf16[1,128,256]{2,1,0:T(8,128)(2,1)}, u32[]{:S(2)}) copy-start(bf16[1,128,256]{2,1,0:T(8,128)(2,1)} %param.14) | copy-start | bytes 196612
  0.0 4.7 %copy-start.8 = (bf16[1,128,256]{2,1,0:T(8,128)(2,1)S(1)}, bf16[1,128,256]{2,1,0:T(8,128)(2,1)}, u32[]{:S(2)}) copy-start(bf16[1,128,256]{2,1,0:T(8,128)(2,1)} %param.13) | copy-start | bytes 196612
  1.8 8.8 %copy-start.11 = (s32[1,128,8]{1,2,0:T(8,128)S(1)}, s32[1,128,8]{1,2,0:T(8,128)}, u32[]{:S(2)}) copy-start(s32[1,128,8]{1,2,0:T(8,128)} %param.17) | copy-start | bytes 12292
  1.8 8.9 %copy-start.10 = (f32[1,128,8]{1,2,0:T(8,128)S(1)}, f32[1,128,8]{1,2,0:T(8,128)}, u32[]{:S(2)}) copy-start(f32[1,128,8]{1,2,0:T(8,128)} %param.18) | copy-start | bytes 12292
  1.8 59.9 %collective-permute-start = (bf16[2048,512]{1,0:T(8,128)(2,1)S(1)}, bf16[2048,512]{1,0:T(8,128)(2,1)}, u32[]{:S(2)}, u32[]{:S(2)}) collective-permute-start(bf16[2048,512]{1,0:T(8,128)(2,1)S(1)} %constant_dynamic-slice_fusion), channel_id=1, source_target_pairs={{0,20},{1,21},{2,22},{3,23},{4,16},{5,17},{6,18},{7,19},{8,28},{9,... | collective-permute-start | bytes 6291464 | tf_op jit(solution)/shard_map/ppermute | solution.py:87
  4.8 9.2 %copy-start.2 = (bf16[1,128,4096]{2,1,0:T(8,128)(2,1)S(1)}, bf16[1,128,4096]{2,1,0:T(8,128)(2,1)}, u32[]{:S(2)}) copy-start(bf16[1,128,4096]{2,1,0:T(8,128)(2,1)} %param.12) | copy-start | bytes 3145732
  5.8 20.4 %all-to-all-start = ((bf16[8,128,512]{2,1,0:T(8,128)(2,1)}), bf16[8,128,512]{2,1,0:T(8,128)(2,1)}, u32[]{:S(2)}, u32[]{:S(2)}) async-start(bf16[8,128,512]{2,1,0:T(8,128)(2,1)} %broadcast_in_dim.77), calls=%async_computation | async-start | bytes 2097152 | tf_op jit(solution)/shard_map/all_to_all | solution.py:29
  36.9 26.8 %collective-permute-start.6 = (bf16[128,2048]{0,1:T(8,128)(2,1)}, bf16[128,2048]{0,1:T(8,128)(2,1)S(1)}, u32[]{:S(2)}, u32[]{:S(2)}) collective-permute-start(bf16[128,2048]{0,1:T(8,128)(2,1)} %bitcast.18), channel_id=1, source_target_pairs={{0,3},{1,0},{2,1},{3,2},{4,7},{5,4},{6,5},{7,6},{8,11},{9,8},{10,9... | collective-permute-start | bytes 1572872 | tf_op jit(solution)/shard_map/ppermute | solution.py:46
  38.9 28.2 %collective-permute-start.3 = (bf16[128,2048]{0,1:T(8,128)(2,1)}, bf16[128,2048]{0,1:T(8,128)(2,1)S(1)}, u32[]{:S(2)}, u32[]{:S(2)}) collective-permute-start(bf16[128,2048]{0,1:T(8,128)(2,1)} %bitcast.18), channel_id=1, source_target_pairs={{0,1},{1,2},{2,3},{3,0},{4,5},{5,6},{6,7},{7,4},{8,9},{9,10},{10,1... | collective-permute-start | bytes 1572872 | tf_op jit(solution)/shard_map/ppermute | solution.py:46
  46.0 15.7 %copy-start = (bf16[4096,512]{1,0:T(8,128)(2,1)S(1)}, bf16[4096,512]{1,0:T(8,128)(2,1)}, u32[]{:S(2)}) copy-start(bf16[4096,512]{1,0:T(8,128)(2,1)} %param.15) | copy-start | bytes 12582916
  49.2 17.9 %collective-permute-start.2 = (bf16[128,2048]{0,1:T(8,128)(2,1)S(1)}, bf16[128,2048]{0,1:T(8,128)(2,1)S(1)}, u32[]{:S(2)}, u32[]{:S(2)}) collective-permute-start(bf16[128,2048]{0,1:T(8,128)(2,1)S(1)} %bitcast.185), channel_id=1, source_target_pairs={{0,1},{1,2},{2,3},{3,0},{4,5},{5,6},{6,7},{7,4},{8,9},{9,10},{10,1... | collective-permute-start | bytes 1572872 | tf_op jit(solution)/shard_map/ppermute | solution.py:46
  50.0 18.5 %collective-permute-start.9 = (bf16[128,2048]{0,1:T(8,128)(2,1)S(1)}, bf16[128,2048]{0,1:T(8,128)(2,1)S(1)}, u32[]{:S(2)}, u32[]{:S(2)}) collective-permute-start(bf16[128,2048]{0,1:T(8,128)(2,1)S(1)} %bitcast.186), channel_id=1, source_target_pairs={{0,3},{1,0},{2,1},{3,2},{4,7},{5,4},{6,5},{7,6},{8,11},{9,8},{10,9... | collective-permute-start | bytes 1572872 | tf_op jit(solution)/shard_map/ppermute | solution.py:46
  61.7 21.1 %collective-permute-start.1 = (bf16[2048,512]{1,0:T(8,128)(2,1)}, bf16[2048,512]{1,0:T(8,128)(2,1)S(1)}, u32[]{:S(2)}, u32[]{:S(2)}) collective-permute-start(bf16[2048,512]{1,0:T(8,128)(2,1)} %collective-permute-done), channel_id=1, source_target_pairs={{0,8},{8,0},{1,9},{9,1},{2,10},{10,2},{3,11},{11,3},{4,12},{12,4},... | collective-permute-start | bytes 6291464 | tf_op jit(solution)/shard_map/ppermute | solution.py:92
  63.7 15.1 %collective-permute-start.7 = (bf16[128,2048]{0,1:T(8,128)(2,1)S(1)}, bf16[128,2048]{0,1:T(8,128)(2,1)S(1)}, u32[]{:S(2)}, u32[]{:S(2)}) collective-permute-start(bf16[128,2048]{0,1:T(8,128)(2,1)S(1)} %collective-permute-done.6), channel_id=1, source_target_pairs={{0,3},{1,0},{2,1},{3,2},{4,7},{5,4},{6,5},{7,6},{8,11},{9,8},{10,9... | collective-permute-start | bytes 1572872 | tf_op jit(solution)/shard_map/ppermute | solution.py:46
  67.0 15.3 %collective-permute-start.5 = (bf16[128,2048]{0,1:T(8,128)(2,1)S(1)}, bf16[128,2048]{0,1:T(8,128)(2,1)S(1)}, u32[]{:S(2)}, u32[]{:S(2)}) collective-permute-start(bf16[128,2048]{0,1:T(8,128)(2,1)S(1)} %collective-permute-done.2), channel_id=1, source_target_pairs={{0,1},{1,2},{2,3},{3,0},{4,5},{5,6},{6,7},{7,4},{8,9},{9,10},{10,1... | collective-permute-start | bytes 1572872 | tf_op jit(solution)/shard_map/ppermute | solution.py:46
  87.2 10.6 %collective-permute-start.8 = (bf16[128,1024]{1,0:T(8,128)(2,1)S(1)}, bf16[128,1024]{1,0:T(8,128)(2,1)S(1)}, u32[]{:S(2)}, u32[]{:S(2)}) collective-permute-start(bf16[128,1024]{1,0:T(8,128)(2,1)S(1)} %pad_maximum_fusion.4), channel_id=1, source_target_pairs={{0,2},{1,3},{2,0},{3,1},{4,6},{5,7},{6,4},{7,5},{8,10},{9,11},{10,... | collective-permute-start | bytes 786440 | tf_op jit(solution)/shard_map/ppermute | solution.py:46
  88.3 12.1 %collective-permute-start.4 = (bf16[128,1024]{1,0:T(8,128)(2,1)S(1)}, bf16[128,1024]{1,0:T(8,128)(2,1)S(1)}, u32[]{:S(2)}, u32[]{:S(2)}) collective-permute-start(bf16[128,1024]{1,0:T(8,128)(2,1)S(1)} %pad_maximum_fusion.3), channel_id=1, source_target_pairs={{0,3},{1,0},{2,1},{3,2},{4,7},{5,4},{6,5},{7,6},{8,11},{9,8},{10,9... | collective-permute-start | bytes 786440 | tf_op jit(solution)/shard_map/ppermute | solution.py:46
  91.6 10.4 %collective-permute-start.10 = (bf16[128,1024]{1,0:T(8,128)(2,1)S(1)}, bf16[128,1024]{1,0:T(8,128)(2,1)S(1)}, u32[]{:S(2)}, u32[]{:S(2)}) collective-permute-start(bf16[128,1024]{1,0:T(8,128)(2,1)S(1)} %pad_maximum_fusion.5), channel_id=1, source_target_pairs={{0,1},{1,2},{2,3},{3,0},{4,5},{5,6},{6,7},{7,4},{8,9},{9,10},{10,1... | collective-permute-start | bytes 786440 | tf_op jit(solution)/shard_map/ppermute | solution.py:46
  113.7 99.0 %all-to-all-start.2 = ((bf16[128,8,3584]{2,1,0:T(8,128)(2,1)}), bf16[128,8,3584]{2,1,0:T(8,128)(2,1)}, u32[]{:S(2)}, u32[]{:S(2)}) async-start(bf16[128,8,3584]{2,1,0:T(8,128)(2,1)} %bitcast.175), calls=%async_computation.2 | async-start | bytes 14680064 | tf_op jit(solution)/shard_map/all_to_all | solution.py:29
  212.7 36.0 %all-to-all-start.1 = ((bf16[128,8,1024]{2,1,0:T(8,128)(2,1)}), bf16[128,8,1024]{2,1,0:T(8,128)(2,1)}, u32[]{:S(2)}, u32[]{:S(2)}) async-start(bf16[128,8,1024]{2,1,0:T(8,128)(2,1)} %convert_bitcast_fusion.1), calls=%async_computation.1 | async-start | bytes 4194304 | tf_op jit(solution)/shard_map/all_to_all | solution.py:29
  261.1 46.7 %all-to-all-start.3 = ((bf16[128,8,1536]{2,1,0:T(8,128)(2,1)}), bf16[128,8,1536]{2,1,0:T(8,128)(2,1)}, u32[]{:S(2)}, u32[]{:S(2)}) async-start(bf16[128,8,1536]{2,1,0:T(8,128)(2,1)} %bitcast.184), calls=%async_computation.3 | async-start | bytes 6291456 | tf_op jit(solution)/shard_map/all_to_all | solution.py:29
  307.8 82.6 %all-to-all-start.4 = ((bf16[128,8,3072]{2,1,0:T(8,128)(2,1)}), bf16[128,8,3072]{2,1,0:T(8,128)(2,1)}, u32[]{:S(2)}, u32[]{:S(2)}) async-start(bf16[128,8,3072]{2,1,0:T(8,128)(2,1)} %convert_bitcast_fusion), calls=%async_computation.4 | async-start | bytes 12582912 | tf_op jit(solution)/shard_map/all_to_all | solution.py:29
  324.5 4.6 %copy-start.5 = (bf16[128,128]{1,0:T(8,128)(2,1)S(1)}, bf16[128,128]{1,0:T(8,128)(2,1)}, u32[]{:S(2)}) copy-start(bf16[128,128]{1,0:T(8,128)(2,1)} %fusion.98) | copy-start | bytes 98308
  324.5 4.6 %copy-start.6 = (bf16[128,128]{1,0:T(8,128)(2,1)S(1)}, bf16[128,128]{1,0:T(8,128)(2,1)}, u32[]{:S(2)}) copy-start(bf16[128,128]{1,0:T(8,128)(2,1)} %get-tuple-element.21) | copy-start | bytes 98308
  (4 other events, 4.3 us)

commit v3 on v2

v3 whole, which is shorter than its diff:
```python
import jax
import jax.numpy as jnp
from jax import lax
from jax.experimental import pallas as pl
from jax.experimental.pallas import tpu as pltpu
from jax.sharding import Mesh, PartitionSpec as P


KVH = 2
DH = 128
EXPERTS = 128
FULL = 8
SLOTS = EXPERTS * FULL
WIDTH = 4096
PACK = WIDTH // 8
OUT_FIRST = 3072
BACK_FIRST = 1024
TILE = 256
FINISH = 1024

DP = ("z", "xl", "core")
CTX = ("xh", "y")
ALL = DP + CTX
BF = jnp.bfloat16
F32 = jnp.float32


def exchange(blocks, axes):
    return lax.all_to_all(blocks, axes, split_axis=0, concat_axis=0, tiled=True)


def neighbour_pairs():
    pairs = []
    for z in range(4):
        for xl in range(2):
            for core in range(2):
                for xh in range(2):
                    for y in range(4):
                        src = (((z * 2 + xl) * 2 + core) * 2 + xh) * 4 + y
                        dst = (((z * 2 + 1 - xl) * 2 + core) * 2 + 1 - xh) * 4 + y
                        pairs.append((src, dst))
    return pairs


def shift(block, step):
    return lax.ppermute(block, "y", [(i, (i + step) % 4) for i in range(4)])


def gather_pair(keys, values):
    pair = jnp.concatenate([keys, values], axis=1)
    gathered = exchange(jnp.broadcast_to(pair[None], (8,) + pair.shape), CTX)
    return gathered.reshape(8 * pair.shape[0], pair.shape[1])


def attend_kernel(place_ref, query_ref, key_ref, value_ref, out_ref, bias):
    tok = query_ref.shape[0]
    heads = query_ref.shape[1] // DH

    @pl.when(pl.program_id(0) == 0)
    def _():
        query_pos = place_ref[0] * tok + lax.broadcasted_iota(jnp.int32, bias.shape, 0)
        key_pos = lax.broadcasted_iota(jnp.int32, bias.shape, 1)
        bias[...] = jnp.where(key_pos <= query_pos, 0.0, -1e30)

    for head in range(heads):
        at = slice(head * DH, (head + 1) * DH)
        scores = lax.dot_general(
            query_ref[:, at], key_ref[...], (((1,), (1,)), ((), ())), preferred_element_type=F32
        )
        scores = scores * DH ** (-0.5) + bias[...]
        weights = jnp.exp(scores - jnp.max(scores, axis=1, keepdims=True))
        total = jnp.sum(weights, axis=1, keepdims=True)
        out_ref[:, at] = (product(weights.astype(BF), value_ref[...]) / total).astype(BF)


def attend(place, queries, gathered, head):
    tok = queries.shape[0]
    keys = gathered.shape[0]
    half = queries.shape[1] // KVH
    block = 4 * DH
    steps = half // block
    return pl.pallas_call(
        attend_kernel,
        grid_spec=pltpu.PrefetchScalarGridSpec(
            num_scalar_prefetch=1,
            grid=(steps,),
            in_specs=[
                pl.BlockSpec((tok, block), lambda i, p: (0, head * steps + i)),
                pl.BlockSpec((keys, DH), lambda i, p: (0, head)),
                pl.BlockSpec((keys, DH), lambda i, p: (0, KVH + head)),
            ],
            out_specs=pl.BlockSpec((tok, block), lambda i, p: (0, i)),
            scratch_shapes=[pltpu.VMEM((tok, keys), F32)],
        ),
        out_shape=jax.ShapeDtypeStruct((tok, half), BF),
        cost_estimate=pl.CostEstimate(
            flops=4 * tok * half * keys, bytes_accessed=4 * tok * half, transcendentals=tok * half * 8
        ),
    )(place, queries, gathered, gathered)


def own_kernel(*refs):
    *row_refs, weight_ref, out_ref = refs
    half = row_refs[0].shape[1]
    left = jnp.concatenate([ref[...] for ref in row_refs[0::2]], axis=0)
    right = jnp.concatenate([ref[...] for ref in row_refs[1::2]], axis=0)
    out = product(left, weight_ref[:half]) + product(right, weight_ref[half:])
    out_ref[...] = out.astype(BF)


def pair_kernel(core_ref, *refs):
    *row_refs, fetched_ref, other_ref, out_ref = refs
    left = jnp.concatenate([ref[...] for ref in row_refs[0::2]], axis=0)
    right = jnp.concatenate([ref[...] for ref in row_refs[1::2]], axis=0)
    swap = core_ref[0] == 1
    out = product(jnp.where(swap, right, left), fetched_ref[...])
    out = out + product(jnp.where(swap, left, right), other_ref[...])
    out_ref[...] = out.astype(BF)


def columns(rows, weight, core=None):
    flat = [part for pair in rows for part in pair]
    tok, half = flat[0].shape
    wide = weight[0].shape[1]
    count = len(rows) * tok
    body = own_kernel if core is None else pair_kernel
    vmem = pl.BlockSpec(memory_space=pltpu.VMEM)
    scalars = [] if core is None else [core]
    return pl.pallas_call(
        body,
        in_specs=[pl.BlockSpec(memory_space=pltpu.SMEM)] * len(scalars) + [vmem] * (len(flat) + len(weight)),
        out_specs=vmem,
        out_shape=jax.ShapeDtypeStruct((count, wide), BF),
        compiler_params=pltpu.CompilerParams(vmem_limit_bytes=32 * 1024 * 1024),
        cost_estimate=pl.CostEstimate(
            flops=4 * count * half * wide, bytes_accessed=4 * half * wide + 4 * count * half, transcendentals=0
        ),
    )(*scalars, *flat, *weight)


def project(attended, out_weight):
    first, second = attended
    tok, half = first.shape
    core = lax.axis_index("core")
    mine = lax.dynamic_slice_in_dim(out_weight, core * half, half, axis=0)
    fetched = lax.ppermute(mine, ALL, neighbour_pairs())
    below_a, above_a = shift(first, 1), shift(first, -1)
    below_b, above_b = shift(second, 1), shift(second, -1)
    far_a = shift(below_a, 1)
    far_b = shift(above_b, -1)
    other = lax.ppermute(fetched, "core", [(0, 1), (1, 0)])
    near = [(first, second), (below_a, below_b), (above_a, above_b)]
    far = [(far_a, far_b)]
    which = core.reshape(1)
    near_own = columns(near, [out_weight])
    near_pair = columns(near, [fetched, other], which)
    near = jnp.concatenate([near_own, near_pair], axis=1)
    from_above = shift(near[tok : 2 * tok], -1)
    from_below = shift(near[2 * tok :], 1)
    far_own = columns(far, [out_weight])
    far_pair = columns(far, [fetched, other], which)
    from_far = shift(jnp.concatenate([far_own, far_pair], axis=1), 2)
    return [near[:tok], from_above, from_far, from_below]


def product(left, right):
    return jnp.dot(left, right, preferred_element_type=F32)


def shuffle(packing):
    by_row = lax.broadcasted_iota(jnp.int32, (128, 128), 0 if packing else 1)
    by_piece = lax.broadcasted_iota(jnp.int32, (128, 128), 1 if packing else 0)
    return (lax.rem(by_row, 8) * 16 + lax.div(by_row, 8) == by_piece).astype(F32).astype(BF)


def packed_rows(rows):
    pieces = [rows[:, PACK * s : PACK * (s + 1)] for s in range(8)]
    return product(shuffle(True), jnp.concatenate(pieces, axis=0)).astype(BF)


def unpack(packed, rows, start):
    pieces = product(shuffle(False), packed).astype(BF)
    for s in range(8):
        rows[pl.ds(start, 16), PACK * s : PACK * (s + 1)] = pieces[16 * s : 16 * s + 16]


def make_kernel(
    place_ref, here_ref, above_ref, far_ref, below_ref, hidden_ref, gain_ref, pick_ref, last_ref,
    out_ref, rest_ref, residual_ref, normed,
):
    step = pl.program_id(0)

    @pl.when(step == 0)
    def _():
        for ahead, ref in enumerate((here_ref, above_ref, far_ref, below_ref)):
            y = lax.rem(place_ref[2] + ahead, 4)
            for part in range(2):
                high = place_ref[1] if part == 0 else 1 - place_ref[1]
                at = pl.ds(pl.multiple_of((high * 4 + y) * PACK, PACK), PACK)
                projected = ref[:, part * PACK : (part + 1) * PACK].astype(F32)
                residual_ref[:, at] = hidden_ref[:, at].astype(F32) + projected
        residual = residual_ref[...]
        mean = jnp.mean(residual * residual, axis=1, keepdims=True)
        normed[...] = (residual * lax.rsqrt(mean + 1e-06) * gain_ref[...]).astype(BF)

    picked = pick_ref[...]
    out_ref[:, :OUT_FIRST] = product(picked, normed[:, :OUT_FIRST]).astype(BF)
    out_ref[:, OUT_FIRST:] = packed_rows(product(last_ref[...], normed[...]).astype(BF))

    @pl.when(step == 0)
    def _():
        rest_ref[...] = normed[:, OUT_FIRST:]


def silu_product(gated, lifted):
    return (gated / (1.0 + jnp.exp(-gated)) * lifted).astype(BF)


def first_kernel(got_ref, gate_ref, up_ref, down_ref, gated_ref, lifted_ref, last_ref, rows):
    step = pl.program_id(0)
    x = got_ref[:, :OUT_FIRST]
    gated_ref[...] = product(x, gate_ref[:OUT_FIRST])
    lifted_ref[...] = product(x, up_ref[:OUT_FIRST])
    for i in range(TILE // 128):
        start = pl.multiple_of(step * (TILE // 8) + 16 * i, 16)
        unpack(got_ref[128 * i : 128 * (i + 1), OUT_FIRST:], rows, start)

    @pl.when(step == pl.num_programs(0) - 1)
    def _():
        x = rows[...]
        activated = silu_product(product(x, gate_ref[...]), product(x, up_ref[...]))
        served = product(activated, down_ref[...]).astype(BF)
        for i in range(EXPERTS // 16):
            last_ref[128 * i : 128 * (i + 1)] = packed_rows(served[16 * i : 16 * (i + 1)])


def second_kernel(got_ref, gate_ref, up_ref, down_ref, gated_ref, lifted_ref, last_ref, act_ref, out_ref):
    x = got_ref[...]
    gated = gated_ref[...] + product(x, gate_ref[...])
    lifted = lifted_ref[...] + product(x, up_ref[...])
    activated = silu_product(gated, lifted)
    act_ref[...] = activated
    out_ref[:, :BACK_FIRST] = product(activated, down_ref[...]).astype(BF)
    out_ref[:, BACK_FIRST:] = last_ref[...]


def finish_kernel(base_ref, split_ref, back_ref, out_ref):
    fixed = BACK_FIRST // FINISH

    @pl.when(pl.program_id(0) < fixed)
    def _():
        out_ref[...] = base_ref[...].astype(BF)

    @pl.when(pl.program_id(0) >= fixed)
    def _():
        sums = product(split_ref[...], back_ref[...])
        tok = base_ref.shape[0]
        out_ref[...] = (base_ref[...] + (sums[:tok] + sums[tok:])).astype(BF)


def whole(shape, index=(0, 0)):
    return pl.BlockSpec(shape, lambda i: index)


def tiled(shape):
    return pl.BlockSpec(shape, lambda i: (i, 0))


def call(body, grid, in_specs, out_specs, out_shape, scratch=(), flops=0, moved=0):
    return pl.pallas_call(
        body,
        grid=grid,
        in_specs=in_specs,
        out_specs=out_specs,
        out_shape=out_shape,
        scratch_shapes=scratch,
        compiler_params=pltpu.CompilerParams(vmem_limit_bytes=56 * 1024 * 1024),
        cost_estimate=pl.CostEstimate(flops=flops, bytes_accessed=moved, transcendentals=0),
    )


def two_terms(weigh):
    high = weigh.astype(BF)
    low = (weigh - high.astype(F32)).astype(BF)
    return jnp.concatenate([high, low], axis=0)


def slots_of(routes, slot_gates):
    tok = routes.shape[0]
    named = routes[:, :, None] == jnp.arange(EXPERTS, dtype=jnp.int32)[None, None, :]
    hit = jnp.any(named, axis=1)
    gate = jnp.sum(jnp.where(named, slot_gates[:, :, None], 0.0), axis=1)
    before = jnp.arange(tok)[None, :] < jnp.arange(tok)[:, None]
    rank = jnp.dot(before.astype(BF), hit.astype(BF), preferred_element_type=F32)
    return hit, jnp.where(hit, rank, -1.0), gate


def layer(
    hidden,
    queries,
    keys,
    values,
    out_weight,
    norm_gain,
    routes,
    slot_scores,
    gate_weight,
    up_weight,
    down_weight,
):
    tok, _ = hidden.shape[1:]
    place = jnp.stack([lax.axis_index(CTX), lax.axis_index("xh"), lax.axis_index("y")])
    gathered = gather_pair(keys[0], values[0])
    first = attend(place, queries[0], gathered, 0)
    second = attend(place, queries[0], gathered, 1)

    score_rows = slot_scores[0]
    slot_gates = score_rows / jnp.sum(score_rows, axis=1, keepdims=True)
    _, rank, gate = slots_of(routes[0], slot_gates)
    places = jnp.arange(FULL, dtype=F32)
    pick = (rank.T[:, None, :] == places[None, :, None]).astype(BF).reshape(EXPERTS * FULL, tok)
    pick_last = (rank.T == float(FULL)).astype(BF)
    weigh = jnp.where(rank[:, :, None] == places, gate[:, :, None], 0.0).reshape(tok, EXPERTS * FULL)
    weigh_last = jnp.where(rank == float(FULL), gate, 0.0)
    split, split_last = two_terms(weigh), two_terms(weigh_last)

    columns_home = project((first, second), out_weight)

    hid = gate_weight.shape[2]
    w_gate, w_up, w_down = gate_weight[0], up_weight[0], down_weight[0]
    shape = jax.ShapeDtypeStruct
    rest = WIDTH - OUT_FIRST
    send_first = OUT_FIRST + PACK
    back_first = BACK_FIRST + PACK
    nine = pltpu.VMEM((EXPERTS, WIDTH), BF)

    sent, normed_rest, residual = pl.pallas_call(
        make_kernel,
        name="make",
        grid_spec=pltpu.PrefetchScalarGridSpec(
            num_scalar_prefetch=1,
            grid=(SLOTS // 128,),
            in_specs=[pl.BlockSpec((tok, 2 * PACK), lambda i, p: (0, 0))] * 4
            + [
                pl.BlockSpec((tok, WIDTH), lambda i, p: (0, 0)),
                pl.BlockSpec((1, WIDTH), lambda i, p: (0, 0)),
                pl.BlockSpec((128, tok), lambda i, p: (i, 0)),
                pl.BlockSpec((16, tok), lambda i, p: (i, 0)),
            ],
            out_specs=[
                pl.BlockSpec((128, send_first), lambda i, p: (i, 0)),
                pl.BlockSpec((tok, rest), lambda i, p: (0, 0)),
                pl.BlockSpec((tok, WIDTH), lambda i, p: (0, 0)),
            ],
            scratch_shapes=[pltpu.VMEM((tok, WIDTH), BF)],
        ),
        out_shape=[
            shape((SLOTS, send_first), BF), shape((tok, rest), BF), shape((tok, WIDTH), F32)
        ],
        compiler_params=pltpu.CompilerParams(vmem_limit_bytes=32 * 1024 * 1024),
        cost_estimate=pl.CostEstimate(
            flops=2 * SLOTS * tok * send_first, bytes_accessed=SLOTS * send_first * 2, transcendentals=0
        ),
    )(place, *columns_home, hidden[0], norm_gain.reshape(1, WIDTH), pick, pick_last)
    got = exchange(sent.reshape(EXPERTS, FULL, send_first), ALL).reshape(SLOTS, send_first)
    sent_rest = product(pick, normed_rest).astype(BF)
    got_rest = exchange(sent_rest.reshape(EXPERTS, FULL, rest), ALL).reshape(SLOTS, rest)
    gated, lifted, last = call(
        first_kernel, (SLOTS // TILE,),
        [
            tiled((TILE, send_first)), whole((WIDTH, hid)), whole((WIDTH, hid)), whole((hid, WIDTH)),
        ],
        [tiled((TILE, hid)), tiled((TILE, hid)), whole((SLOTS, PACK))],
        [shape((SLOTS, hid), F32), shape((SLOTS, hid), F32), shape((SLOTS, PACK), BF)], [nine],
        flops=4 * SLOTS * OUT_FIRST * hid, moved=SLOTS * (send_first + 4 * hid) * 2 + WIDTH * hid * 6,
    )(got, w_gate, w_up, w_down)
    activated, served = call(
        second_kernel, (SLOTS // TILE,),
        [
            tiled((TILE, rest)), whole((rest, hid), (OUT_FIRST // rest, 0)),
            whole((rest, hid), (OUT_FIRST // rest, 0)), whole((hid, BACK_FIRST)),
            tiled((TILE, hid)), tiled((TILE, hid)), tiled((TILE, PACK)),
        ],
        [tiled((TILE, hid)), tiled((TILE, back_first))],
        [shape((SLOTS, hid), BF), shape((SLOTS, back_first), BF)],
        flops=6 * SLOTS * rest * hid, moved=SLOTS * (rest + back_first + 4 * hid) * 2 + rest * hid * 6,
    )(got_rest, w_gate, w_up, w_down, gated, lifted, last)
    back = exchange(served.reshape(EXPERTS, FULL, back_first), ALL).reshape(SLOTS, back_first)
    served_rest = product(activated, w_down[:, BACK_FIRST:]).astype(BF)
    back_rest = exchange(
        served_rest.reshape(EXPERTS, FULL, WIDTH - BACK_FIRST), ALL
    ).reshape(SLOTS, WIDTH - BACK_FIRST)

    sums = product(split, back[:, :BACK_FIRST])
    nines = product(split_last, back[:, BACK_FIRST:].reshape(EXPERTS, WIDTH))
    base = residual + (nines[:tok] + nines[tok:])
    base = jnp.concatenate(
        [base[:, :BACK_FIRST] + (sums[:tok] + sums[tok:]), base[:, BACK_FIRST:]], axis=1
    )
    fixed = BACK_FIRST // FINISH
    out = call(
        finish_kernel, (WIDTH // FINISH,),
        [
            pl.BlockSpec((tok, FINISH), lambda i: (0, i)),
            whole((2 * tok, SLOTS)),
            pl.BlockSpec((SLOTS, FINISH), lambda i: (0, jnp.maximum(i - fixed, 0))),
        ],
        pl.BlockSpec((tok, FINISH), lambda i: (0, i)), shape((tok, WIDTH), BF),
        flops=4 * tok * SLOTS * WIDTH, moved=SLOTS * WIDTH * 2,
    )(base, split, back_rest)
    return out[None]


def solution(mesh):
    fine = Mesh(mesh.devices.reshape(4, 2, 2, 2, 4), ALL)
    return jax.shard_map(
        layer,
        mesh=fine,
        in_specs=(
            P(DP, CTX, None),
            P(DP, CTX, None),
            P(DP, CTX, None),
            P(DP, CTX, None),
            P(None, CTX),
            P(),
            P(DP, CTX, None),
            P(DP, CTX, None),
            P(ALL, None, None),
            P(ALL, None, None),
            P(ALL, None, None),
        ),
        out_specs=P(DP, CTX, None),
        check_vma=False,
    )
```

time: 406 us -> 437 us (1.076)
  the two profiles are of different devices: /device:TPU:0 before, /device:TPU:91 now
where the time goes in v3:
time: 437 us; the launch traced here: 432 us
  waiting for transfers between devices  258 us (59%)
  Pallas kernels  74.9 us (17%)
  starting transfers between devices  56.5 us (13%)
  local copies, waits for them, and re-layouts  19.7 us (5%)
  matrix products  16.2 us (4%)
  other arithmetic  6.22 us (1%)
    all_to_all x5, waiting for transfers between devices, exchange(): return lax.all_to_all(blocks, axes, split_axis=0, concat_axis=0, tiled=True)  175 us
    ppermute x1, waiting for transfers between devices, project(): fetched = lax.ppermute(mine, ALL, neighbour_pairs())  51 us
    all_to_all x5, starting transfers between devices, exchange(): return lax.all_to_all(blocks, axes, split_axis=0, concat_axis=0, tiled=True)  47.2 us
    ppermute x9, waiting for transfers between devices, shift(): return lax.ppermute(block, 'y', [(i, (i + step) % 4) for i in range(4)])  32.1 us
    pallas_call x1, Pallas kernels, layer(): call(first_kernel, (SLOTS // TILE,), [tiled((TILE, send_first)), whole((W...  22.3 us
    pallas_call x2, Pallas kernels, attend(): pl.pallas_call(attend_kernel, grid_spec=pltpu.PrefetchScalarGridSpec(num_...  17.7 us
    dot_general x4, matrix products, product(): return jnp.dot(left, right, preferred_element_type=F32)  15.5 us
    pallas_call x4, Pallas kernels, columns(): pl.pallas_call(body, in_specs=[pl.BlockSpec(memory_space=pltpu.SMEM)] * l...  10.7 us
  transfers between devices with their start and end apart: 16, of which 12 were waited for; matrix products, arithmetic and copies ran while one was open for 7% of the time, Pallas kernels for 11%

profile of v3, /device:TPU:91, one launch (start us, length us, event | category | flops | bytes accessed | tf_op | source)
XLA Modules:
  0.0 432.2 jit_solution(929910683729730380)
XLA Ops:
  0.0 3.1 constant_dynamic-slice_fusion
  5.4 4.7 %all-to-all-start = ((bf16[8,128,512]{2,1,0:T(8,128)(2,1)}), bf16[8,128,512]{2,1,0:T(8,128)(2,1)S(1)}, u32[]{:S(2)}, u32[]{:S(2)}) async-start(bf16[8,128,512]{2,1,0:T(8,128)(2,1)} %broadcast_in_dim.52), calls=%async_computation | async-start | bytes 2097152 | tf_op jit(solution)/shard_map/all_to_all | solution.py:29
  10.1 51.0 %collective-permute-done.4.refs_6_.refs_2_ = bf16[2048,512]{1,0:T(8,128)(2,1)S(1)} collective-permute-done((bf16[2048,512]{1,0:T(8,128)(2,1)}, bf16[2048,512]{1,0:T(8,128)(2,1)S(1)}, u32[]{:S(2)}, u32[]{:S(2)}) %collective-permute-start.4) | collective-permute-done | bytes 2097184 | tf_op jit(solution)/shard_map/ppermute | solution.py:146
  64.2 8.8 %shard_map.109.refs_0_ = bf16[128,2048]{1,0:T(8,128)(2,1)} custom-call(s32[3]{0:T(128)} %pad_add_fusion.place_ref, bf16[128,4096]{1,0:T(8,128)(2,1)} %bitcast.60, bf16[1024,512]{1,0:T(8,128)(2,1)} %bitcast.52, bf16[1024,512]{1,0:T(8,128)(2,1)} %bitcast.53), custom_call_target="tpu_custom_call" | custom-call | flops 1073741824 | bytes 1048576 | tf_op jit(solution)/shard_map/pallas_call | solution.py:82
  73.0 8.9 %shard_map.110.refs_1_ = bf16[128,2048]{1,0:T(8,128)(2,1)} custom-call(s32[3]{0:T(128)} %pad_add_fusion.place_ref, bf16[128,4096]{1,0:T(8,128)(2,1)} %bitcast.61, bf16[1024,512]{1,0:T(8,128)(2,1)} %bitcast.54, bf16[1024,512]{1,0:T(8,128)(2,1)} %bitcast.55), custom_call_target="tpu_custom_call" | custom-call | flops 1073741824 | bytes 1048576 | tf_op jit(solution)/shard_map/pallas_call | solution.py:82
  88.1 8.8 %collective-permute-done.3.refs_5_ = bf16[128,2048]{1,0:T(8,128)(2,1)} collective-permute-done((bf16[128,2048]{1,0:T(8,128)(2,1)}, bf16[128,2048]{1,0:T(8,128)(2,1)}, u32[]{:S(2)}, u32[]{:S(2)}) %collective-permute-start.3) | collective-permute-done | bytes 524320 | tf_op jit(solution)/shard_map/ppermute | solution.py:46
  99.0 9.1 %collective-permute-done.2.refs_4_ = bf16[128,2048]{1,0:T(8,128)(2,1)} collective-permute-done((bf16[128,2048]{1,0:T(8,128)(2,1)}, bf16[128,2048]{1,0:T(8,128)(2,1)}, u32[]{:S(2)}, u32[]{:S(2)}) %collective-permute-start.2) | collective-permute-done | bytes 524320 | tf_op jit(solution)/shard_map/ppermute | solution.py:46
  111.3 3.4 shard_map.111
  114.8 4.4 %collective-permute-done.8.refs_1_ = bf16[128,2048]{1,0:T(8,128)(2,1)S(1)} collective-permute-done((bf16[128,2048]{1,0:T(8,128)(2,1)}, bf16[128,2048]{1,0:T(8,128)(2,1)S(1)}, u32[]{:S(2)}, u32[]{:S(2)}) %collective-permute-start.8) | collective-permute-done | bytes 524320 | tf_op jit(solution)/shard_map/ppermute | solution.py:46
  120.0 4.2 shard_map.112
  133.6 5.4 %collective-permute-done.9.far_ref = bf16[128,1024]{1,0:T(8,128)(2,1)S(1)} collective-permute-done((bf16[128,1024]{1,0:T(8,128)(2,1)S(1)}, bf16[128,1024]{1,0:T(8,128)(2,1)S(1)}, u32[]{:S(2)}, u32[]{:S(2)}) %collective-permute-start.9) | collective-permute-done | bytes 262176 | tf_op jit(solution)/shard_map/ppermute | solution.py:46
  140.2 7.6 %make.1 = (bf16[1024,3584]{1,0:T(8,128)(2,1)S(1)}, bf16[128,1024]{1,0:T(8,128)(2,1)S(1)}, f32[128,4096]{1,0:T(8,128)S(1)}) custom-call(s32[3]{0:T(128)S(1)} %copy-done.3, bf16[128,1024]{1,0:T(8,128)(2,1)S(1)} %get-tuple-element.22.here_ref, bf16[128,1024]{1,0:T(8,128)(2,1)} %collective-permute-done.6.above_ref, ...), custom_call_target="tpu_custom_call" | custom-call | flops 939524096 | bytes 7340032 | tf_op jit(solution)/shard_map/make/pallas_call | solution.py:337
  147.8 3.0 copy-done.1
  150.8 12.7 %all-to-all-start.2 = ((bf16[128,8,3584]{2,1,0:T(8,128)(2,1)}), bf16[128,8,3584]{2,1,0:T(8,128)(2,1)}, u32[]{:S(2)}, u32[]{:S(2)}) async-start(bf16[128,8,3584]{2,1,0:T(8,128)(2,1)} %bitcast.41), calls=%async_computation.2 | async-start | bytes 14680064 | tf_op jit(solution)/shard_map/all_to_all | solution.py:29
  165.6 84.7 %all-to-all-done.2 = bf16[128,8,3584]{2,1,0:T(8,128)(2,1)} async-done(((bf16[128,8,3584]{2,1,0:T(8,128)(2,1)}), bf16[128,8,3584]{2,1,0:T(8,128)(2,1)}, u32[]{:S(2)}, u32[]{:S(2)}) %all-to-all-start.2) | async-done | bytes 7340064 | tf_op jit(solution)/shard_map/all_to_all | solution.py:29
  250.4 8.8 %all-to-all-start.1 = ((bf16[128,8,1024]{2,1,0:T(8,128)(2,1)}), bf16[128,8,1024]{2,1,0:T(8,128)(2,1)}, u32[]{:S(2)}, u32[]{:S(2)}) async-start(bf16[128,8,1024]{2,1,0:T(8,128)(2,1)} %convert_bitcast_fusion.1), calls=%async_computation.1 | async-start | bytes 4194304 | tf_op jit(solution)/shard_map/all_to_all | solution.py:29
  259.2 22.3 %shard_map.115 = (f32[1024,768]{1,0:T(8,128)}, f32[1024,768]{1,0:T(8,128)}, bf16[1024,512]{1,0:T(8,128)(2,1)}) custom-call(bf16[1024,3584]{1,0:T(8,128)(2,1)} %bitcast.20.got_ref, bf16[4096,768]{1,0:T(8,128)(2,1)} %bitcast.44, bf16[4096,768]{1,0:T(8,128)(2,1)} %bitcast.46, bf16[768,4096]{1,0:T(8,128)(2,1)} %bitcast.48), custom_call_target="tpu_custom_call" | custom-call | flops 9663676416 | bytes 32505856 | tf_op jit(solution)/shard_map/pallas_call | solution.py:368
  283.9 10.4 %shard_map.116 = (bf16[1024,768]{1,0:T(8,128)(2,1)}, bf16[1024,1536]{1,0:T(8,128)(2,1)}) custom-call(bf16[1024,1024]{1,0:T(8,128)(2,1)} %bitcast.15.got_ref, bf16[4096,768]{1,0:T(8,128)(2,1)} %bitcast.45, bf16[4096,768]{1,0:T(8,128)(2,1)} %bitcast.47, bf16[768,4096]{1,0:T(8,128)(2,1)} %bitcast.49, f32[1024,768]{1,0:T(8,128)} %get-tuple-element.16.gated_ref, ...), custom_call_target="tpu_custom_call" | custom-call | flops 4831838208 | bytes 16252928 | tf_op jit(solution)/shard_map/pallas_call | solution.py:377
  294.3 10.8 %all-to-all-start.3 = ((bf16[128,8,1536]{2,1,0:T(8,128)(2,1)}), bf16[128,8,1536]{2,1,0:T(8,128)(2,1)}, u32[]{:S(2)}, u32[]{:S(2)}) async-start(bf16[128,8,1536]{2,1,0:T(8,128)(2,1)} %bitcast.51), calls=%async_computation.3 | async-start | bytes 6291456 | tf_op jit(solution)/shard_map/all_to_all | solution.py:29
  305.1 9.2 %convert_bitcast_fusion = bf16[128,8,3072]{2,1,0:T(8,128)(2,1)} fusion(bf16[1024,768]{1,0:T(8,128)(2,1)} %get-tuple-element.20, bf16[768,4096]{1,0:T(8,128)(2,1)} %bitcast.50), kind=kOutput, calls=%fused_computation | convolution fusion | flops 4834983936 | bytes 12582912 | tf_op jit(solution)/shard_map/dot_general | solution.py:167
  314.2 27.5 %all-to-all-done.3 = bf16[128,8,1536]{2,1,0:T(8,128)(2,1)} async-done(((bf16[128,8,1536]{2,1,0:T(8,128)(2,1)}), bf16[128,8,1536]{2,1,0:T(8,128)(2,1)}, u32[]{:S(2)}, u32[]{:S(2)}) %all-to-all-start.3) | async-done | bytes 3145760 | tf_op jit(solution)/shard_map/all_to_all | solution.py:29
  341.7 10.3 %all-to-all-start.4 = ((bf16[128,8,3072]{2,1,0:T(8,128)(2,1)}), bf16[128,8,3072]{2,1,0:T(8,128)(2,1)}, u32[]{:S(2)}, u32[]{:S(2)}) async-start(bf16[128,8,3072]{2,1,0:T(8,128)(2,1)} %convert_bitcast_fusion), calls=%async_computation.4 | async-start | bytes 12582912 | tf_op jit(solution)/shard_map/all_to_all | solution.py:29
  365.4 60.6 %all-to-all-done.4 = bf16[128,8,3072]{2,1,0:T(8,128)(2,1)} async-done(((bf16[128,8,3072]{2,1,0:T(8,128)(2,1)}), bf16[128,8,3072]{2,1,0:T(8,128)(2,1)}, u32[]{:S(2)}, u32[]{:S(2)}) %all-to-all-start.4) | async-done | bytes 6291488 | tf_op jit(solution)/shard_map/all_to_all | solution.py:29
  426.0 6.2 %shard_map.117 = bf16[128,4096]{1,0:T(8,128)(2,1)} custom-call(f32[128,4096]{1,0:T(8,128)} %pad_maximum_fusion.base_ref, bf16[256,1024]{1,0:T(8,128)(2,1)} %pad_maximum_fusion.1.split_ref, bf16[1024,3072]{1,0:T(8,128)(2,1)} %bitcast.26.back_ref), custom_call_target="tpu_custom_call" | custom-call | flops 2147483648 | bytes 8388608 | tf_op jit(solution)/shard_map/pallas_call | solution.py:401
  (94 shorter events, 45.9 us)
Async XLA Ops:
  3.1 58.0 %collective-permute-start.4 = (bf16[2048,512]{1,0:T(8,128)(2,1)}, bf16[2048,512]{1,0:T(8,128)(2,1)S(1)}, u32[]{:S(2)}, u32[]{:S(2)}) collective-permute-start(bf16[2048,512]{1,0:T(8,128)(2,1)} %constant_dynamic-slice_fusion), channel_id=1, source_target_pairs={{0,20},{1,21},{2,22},{3,23},{4,16},{5,17},{6,18},{7,19},{8,28},{9,... | collective-permute-start | bytes 6291464 | tf_op jit(solution)/shard_map/ppermute | solution.py:146
  5.4 57.8 %all-to-all-start = ((bf16[8,128,512]{2,1,0:T(8,128)(2,1)}), bf16[8,128,512]{2,1,0:T(8,128)(2,1)S(1)}, u32[]{:S(2)}, u32[]{:S(2)}) async-start(bf16[8,128,512]{2,1,0:T(8,128)(2,1)} %broadcast_in_dim.52), calls=%async_computation | async-start | bytes 2097152 | tf_op jit(solution)/shard_map/all_to_all | solution.py:29
  61.1 58.9 %collective-permute-start.5 = (bf16[2048,512]{1,0:T(8,128)(2,1)S(1)}, bf16[2048,512]{1,0:T(8,128)(2,1)}, u32[]{:S(2)}, u32[]{:S(2)}) collective-permute-start(bf16[2048,512]{1,0:T(8,128)(2,1)S(1)} %collective-permute-done.4.refs_6_.refs_2_), channel_id=1, source_target_pairs={{0,8},{8,0},{1,9},{9,1},{2,10},{10,2},{3,11},{11,3},{4,12},{12,4},... | collective-permute-start | bytes 6291464 | tf_op jit(solution)/shard_map/ppermute | solution.py:151
  73.0 10.3 %copy-start.18 = (s32[1,128,8]{1,2,0:T(8,128)S(1)}, s32[1,128,8]{1,2,0:T(8,128)}, u32[]{:S(2)}) copy-start(s32[1,128,8]{1,2,0:T(8,128)} %param.17) | copy-start | bytes 12292
  73.0 10.4 %copy-start.17 = (f32[1,128,8]{1,2,0:T(8,128)S(1)}, f32[1,128,8]{1,2,0:T(8,128)}, u32[]{:S(2)}) copy-start(f32[1,128,8]{1,2,0:T(8,128)} %param.18) | copy-start | bytes 12292
  73.0 13.8 %collective-permute-start = (bf16[128,2048]{1,0:T(8,128)(2,1)}, bf16[128,2048]{1,0:T(8,128)(2,1)}, u32[]{:S(2)}, u32[]{:S(2)}) collective-permute-start(bf16[128,2048]{1,0:T(8,128)(2,1)} %shard_map.109.refs_0_), channel_id=1, source_target_pairs={{0,1},{1,2},{2,3},{3,0},{4,5},{5,6},{6,7},{7,4},{8,9},{9,10},{10,1... | collective-permute-start | bytes 1572872 | tf_op jit(solution)/shard_map/ppermute | solution.py:46
  81.9 14.9 %collective-permute-start.3 = (bf16[128,2048]{1,0:T(8,128)(2,1)}, bf16[128,2048]{1,0:T(8,128)(2,1)}, u32[]{:S(2)}, u32[]{:S(2)}) collective-permute-start(bf16[128,2048]{1,0:T(8,128)(2,1)} %shard_map.110.refs_1_), channel_id=1, source_target_pairs={{0,3},{1,0},{2,1},{3,2},{4,7},{5,4},{6,5},{7,6},{8,11},{9,8},{10,9... | collective-permute-start | bytes 1572872 | tf_op jit(solution)/shard_map/ppermute | solution.py:46
  83.5 15.5 %collective-permute-start.1 = (bf16[128,2048]{1,0:T(8,128)(2,1)}, bf16[128,2048]{1,0:T(8,128)(2,1)}, u32[]{:S(2)}, u32[]{:S(2)}) collective-permute-start(bf16[128,2048]{1,0:T(8,128)(2,1)} %shard_map.110.refs_1_), channel_id=1, source_target_pairs={{0,1},{1,2},{2,3},{3,0},{4,5},{5,6},{6,7},{7,4},{8,9},{9,10},{10,1... | collective-permute-start | bytes 1572872 | tf_op jit(solution)/shard_map/ppermute | solution.py:46
  84.9 23.2 %collective-permute-start.2 = (bf16[128,2048]{1,0:T(8,128)(2,1)}, bf16[128,2048]{1,0:T(8,128)(2,1)}, u32[]{:S(2)}, u32[]{:S(2)}) collective-permute-start(bf16[128,2048]{1,0:T(8,128)(2,1)} %shard_map.109.refs_0_), channel_id=1, source_target_pairs={{0,3},{1,0},{2,1},{3,2},{4,7},{5,4},{6,5},{7,6},{8,11},{9,8},{10,9... | collective-permute-start | bytes 1572872 | tf_op jit(solution)/shard_map/ppermute | solution.py:46
  86.8 28.0 %collective-permute-start.7 = (bf16[128,2048]{1,0:T(8,128)(2,1)}, bf16[128,2048]{1,0:T(8,128)(2,1)S(1)}, u32[]{:S(2)}, u32[]{:S(2)}) collective-permute-start(bf16[128,2048]{1,0:T(8,128)(2,1)} %collective-permute-done.refs_2_), channel_id=1, source_target_pairs={{0,1},{1,2},{2,3},{3,0},{4,5},{5,6},{6,7},{7,4},{8,9},{9,10},{10,1... | collective-permute-start | bytes 1572872 | tf_op jit(solution)/shard_map/ppermute | solution.py:46
  96.9 22.4 %collective-permute-start.8 = (bf16[128,2048]{1,0:T(8,128)(2,1)}, bf16[128,2048]{1,0:T(8,128)(2,1)S(1)}, u32[]{:S(2)}, u32[]{:S(2)}) collective-permute-start(bf16[128,2048]{1,0:T(8,128)(2,1)} %collective-permute-done.3.refs_5_), channel_id=1, source_target_pairs={{0,3},{1,0},{2,1},{3,2},{4,7},{5,4},{6,5},{7,6},{8,11},{9,8},{10,9... | collective-permute-start | bytes 1572872 | tf_op jit(solution)/shard_map/ppermute | solution.py:46
  98.3 16.6 %copy-start.11 = (f32[128,128]{1,0:T(8,128)}, f32[128,128]{1,0:T(8,128)S(1)}, u32[]{:S(2)}) copy-start(f32[128,128]{1,0:T(8,128)S(1)} %get-tuple-element.25) | copy-start | bytes 196612
  125.1 7.3 %collective-permute-start.10 = (bf16[128,1024]{1,0:T(8,128)(2,1)}, bf16[128,1024]{1,0:T(8,128)(2,1)}, u32[]{:S(2)}, u32[]{:S(2)}) collective-permute-start(bf16[128,1024]{1,0:T(8,128)(2,1)} %get-tuple-element.21), channel_id=1, source_target_pairs={{0,1},{1,2},{2,3},{3,0},{4,5},{5,6},{6,7},{7,4},{8,9},{9,10},{10,1... | collective-permute-start | bytes 786440 | tf_op jit(solution)/shard_map/ppermute | solution.py:46
  125.1 4.8 %copy-start.9 = (f32[128,128]{1,0:T(8,128)S(1)}, f32[128,128]{1,0:T(8,128)}, u32[]{:S(2)}) copy-start(f32[128,128]{1,0:T(8,128)} %copy.25) | copy-start | bytes 196612
  125.1 13.9 %copy-start.3 = (s32[3]{0:T(128)S(1)}, s32[3]{0:T(128)}, u32[]{:S(2)}) copy-start(s32[3]{0:T(128)} %pad_add_fusion.place_ref) | copy-start | bytes 40
  125.1 13.9 %copy-start.5 = (f32[4096]{0:T(1024)S(1)}, f32[4096]{0:T(1024)}, u32[]{:S(2)}) copy-start(f32[4096]{0:T(1024)} %param.16) | copy-start | bytes 49156
  125.1 8.5 %collective-permute-start.6 = (bf16[128,1024]{1,0:T(8,128)(2,1)}, bf16[128,1024]{1,0:T(8,128)(2,1)}, u32[]{:S(2)}, u32[]{:S(2)}) collective-permute-start(bf16[128,1024]{1,0:T(8,128)(2,1)} %get-tuple-element.23), channel_id=1, source_target_pairs={{0,3},{1,0},{2,1},{3,2},{4,7},{5,4},{6,5},{7,6},{8,11},{9,8},{10,9... | collective-permute-start | bytes 786440 | tf_op jit(solution)/shard_map/ppermute | solution.py:46
  128.9 10.1 %collective-permute-start.9 = (bf16[128,1024]{1,0:T(8,128)(2,1)S(1)}, bf16[128,1024]{1,0:T(8,128)(2,1)S(1)}, u32[]{:S(2)}, u32[]{:S(2)}) collective-permute-start(bf16[128,1024]{1,0:T(8,128)(2,1)S(1)} %pad_maximum_fusion.3), channel_id=1, source_target_pairs={{0,2},{1,3},{2,0},{3,1},{4,6},{5,7},{6,4},{7,5},{8,10},{9,11},{10,... | collective-permute-start | bytes 786440 | tf_op jit(solution)/shard_map/ppermute | solution.py:46
  150.8 12.7 %copy-start.10 = (f32[128,128]{1,0:T(8,128)S(1)}, f32[128,128]{1,0:T(8,128)}, u32[]{:S(2)}) copy-start(f32[128,128]{1,0:T(8,128)} %copy.25) | copy-start | bytes 196612
  150.8 99.5 %all-to-all-start.2 = ((bf16[128,8,3584]{2,1,0:T(8,128)(2,1)}), bf16[128,8,3584]{2,1,0:T(8,128)(2,1)}, u32[]{:S(2)}, u32[]{:S(2)}) async-start(bf16[128,8,3584]{2,1,0:T(8,128)(2,1)} %bitcast.41), calls=%async_computation.2 | async-start | bytes 14680064 | tf_op jit(solution)/shard_map/all_to_all | solution.py:29
  250.4 33.5 %all-to-all-start.1 = ((bf16[128,8,1024]{2,1,0:T(8,128)(2,1)}), bf16[128,8,1024]{2,1,0:T(8,128)(2,1)}, u32[]{:S(2)}, u32[]{:S(2)}) async-start(bf16[128,8,1024]{2,1,0:T(8,128)(2,1)} %convert_bitcast_fusion.1), calls=%async_computation.1 | async-start | bytes 4194304 | tf_op jit(solution)/shard_map/all_to_all | solution.py:29
  294.3 47.4 %all-to-all-start.3 = ((bf16[128,8,1536]{2,1,0:T(8,128)(2,1)}), bf16[128,8,1536]{2,1,0:T(8,128)(2,1)}, u32[]{:S(2)}, u32[]{:S(2)}) async-start(bf16[128,8,1536]{2,1,0:T(8,128)(2,1)} %bitcast.51), calls=%async_computation.3 | async-start | bytes 6291456 | tf_op jit(solution)/shard_map/all_to_all | solution.py:29
  314.2 37.8 %copy-start.12 = (f32[128,128]{1,0:T(8,128)S(1)}, f32[128,128]{1,0:T(8,128)}, u32[]{:S(2)}) copy-start(f32[128,128]{1,0:T(8,128)} %copy-done.11) | copy-start | bytes 196612
  341.7 84.3 %all-to-all-start.4 = ((bf16[128,8,3072]{2,1,0:T(8,128)(2,1)}), bf16[128,8,3072]{2,1,0:T(8,128)(2,1)}, u32[]{:S(2)}, u32[]{:S(2)}) async-start(bf16[128,8,3072]{2,1,0:T(8,128)(2,1)} %convert_bitcast_fusion), calls=%async_computation.4 | async-start | bytes 12582912 | tf_op jit(solution)/shard_map/all_to_all | solution.py:29
  (11 other events, 22.6 us)

commit v4 on v3

v4 whole, which is shorter than its diff:
```python
import jax
import jax.numpy as jnp
from jax import lax
from jax.experimental import pallas as pl
from jax.experimental.pallas import tpu as pltpu
from jax.sharding import Mesh, PartitionSpec as P


KVH = 2
DH = 128
EXPERTS = 128
FULL = 8
SLOTS = EXPERTS * FULL
WIDTH = 4096
PACK = WIDTH // 8
FOUR = 4
HALF = WIDTH // 2
FIRST = HALF + PACK
TILE = 512

DP = ("z", "xl", "core")
CTX = ("xh", "y")
ALL = DP + CTX
BF = jnp.bfloat16
F32 = jnp.float32


def exchange(blocks, axes):
    return lax.all_to_all(blocks, axes, split_axis=0, concat_axis=0, tiled=True)


def neighbour_pairs():
    pairs = []
    for z in range(4):
        for xl in range(2):
            for core in range(2):
                for xh in range(2):
                    for y in range(4):
                        src = (((z * 2 + xl) * 2 + core) * 2 + xh) * 4 + y
                        dst = (((z * 2 + 1 - xl) * 2 + core) * 2 + 1 - xh) * 4 + y
                        pairs.append((src, dst))
    return pairs


def shift(block, step):
    return lax.ppermute(block, "y", [(i, (i + step) % 4) for i in range(4)])


def gather_pair(keys, values):
    pair = jnp.concatenate([keys, values], axis=1)
    gathered = exchange(jnp.broadcast_to(pair[None], (8,) + pair.shape), CTX)
    return gathered.reshape(8 * pair.shape[0], pair.shape[1])


def attend_kernel(place_ref, query_ref, key_ref, value_ref, out_ref, bias, flipped):
    tok = query_ref.shape[0]
    heads = query_ref.shape[1] // DH

    @pl.when(pl.program_id(0) == 0)
    def _():
        query_pos = place_ref[0] * tok + lax.broadcasted_iota(jnp.int32, bias.shape, 0)
        key_pos = lax.broadcasted_iota(jnp.int32, bias.shape, 1)
        bias[...] = jnp.where(key_pos <= query_pos, 0.0, -1e30)
        flipped[...] = key_ref[...].T

    for head in range(0, heads, 2):
        pair = [slice((head + i) * DH, (head + i + 1) * DH) for i in range(2)]
        rows = jnp.concatenate([query_ref[:, at] for at in pair], axis=0)
        scores = product(rows, flipped[...]) * DH ** (-0.5)
        scores = scores + jnp.concatenate([bias[...], bias[...]], axis=0)
        weights = jnp.exp(scores - jnp.max(scores, axis=1, keepdims=True))
        total = jnp.sum(weights, axis=1, keepdims=True)
        out = (product(weights.astype(BF), value_ref[...]) / total).astype(BF)
        for i, at in enumerate(pair):
            out_ref[:, at] = out[i * tok : (i + 1) * tok]


def attend(place, queries, gathered, head):
    tok = queries.shape[0]
    keys = gathered.shape[0]
    half = queries.shape[1] // KVH
    block = 4 * DH
    steps = half // block
    return pl.pallas_call(
        attend_kernel,
        grid_spec=pltpu.PrefetchScalarGridSpec(
            num_scalar_prefetch=1,
            grid=(steps,),
            in_specs=[
                pl.BlockSpec((tok, block), lambda i, p: (0, head * steps + i)),
                pl.BlockSpec((keys, DH), lambda i, p: (0, head)),
                pl.BlockSpec((keys, DH), lambda i, p: (0, KVH + head)),
            ],
            out_specs=pl.BlockSpec((tok, block), lambda i, p: (0, i)),
            scratch_shapes=[pltpu.VMEM((tok, keys), F32), pltpu.VMEM((DH, keys), BF)],
        ),
        out_shape=jax.ShapeDtypeStruct((tok, half), BF),
        compiler_params=pltpu.CompilerParams(vmem_limit_bytes=16 * 1024 * 1024),
        cost_estimate=pl.CostEstimate(
            flops=4 * tok * half * keys, bytes_accessed=4 * tok * half, transcendentals=tok * half * 8
        ),
    )(place, queries, gathered, gathered)


def own_kernel(*refs):
    *row_refs, weight_ref, out_ref = refs
    half = row_refs[0].shape[1]
    left = jnp.concatenate([ref[...] for ref in row_refs[0::2]], axis=0)
    right = jnp.concatenate([ref[...] for ref in row_refs[1::2]], axis=0)
    out = product(left, weight_ref[:half]) + product(right, weight_ref[half:])
    out_ref[...] = out.astype(BF)


def pair_kernel(core_ref, *refs):
    *row_refs, fetched_ref, other_ref, out_ref = refs
    left = jnp.concatenate([ref[...] for ref in row_refs[0::2]], axis=0)
    right = jnp.concatenate([ref[...] for ref in row_refs[1::2]], axis=0)
    swap = core_ref[0] == 1
    out = product(jnp.where(swap, right, left), fetched_ref[...])
    out = out + product(jnp.where(swap, left, right), other_ref[...])
    out_ref[...] = out.astype(BF)


def columns(rows, weight, core=None):
    flat = [part for pair in rows for part in pair]
    tok, half = flat[0].shape
    wide = weight[0].shape[1]
    count = len(rows) * tok
    body = own_kernel if core is None else pair_kernel
    scalars = [] if core is None else [core]
    block = 256
    return pl.pallas_call(
        body,
        grid=(wide // block,),
        in_specs=[pl.BlockSpec(memory_space=pltpu.SMEM)] * len(scalars)
        + [whole((tok, half))] * len(flat)
        + [pl.BlockSpec((w.shape[0], block), lambda i: (0, i)) for w in weight],
        out_specs=pl.BlockSpec((count, block), lambda i: (0, i)),
        out_shape=jax.ShapeDtypeStruct((count, wide), BF),
        compiler_params=pltpu.CompilerParams(vmem_limit_bytes=24 * 1024 * 1024),
        cost_estimate=pl.CostEstimate(
            flops=4 * count * half * wide, bytes_accessed=4 * half * wide + 4 * count * half, transcendentals=0
        ),
    )(*scalars, *flat, *weight)


def project(attended, out_weight):
    first, second = attended
    tok, half = first.shape
    core = lax.axis_index("core")
    mine = lax.dynamic_slice_in_dim(out_weight, core * half, half, axis=0)
    fetched = lax.ppermute(mine, ALL, neighbour_pairs())
    below_a, above_a = shift(first, 1), shift(first, -1)
    below_b, above_b = shift(second, 1), shift(second, -1)
    far_a = shift(below_a, 1)
    far_b = shift(above_b, -1)
    other = lax.ppermute(fetched, "core", [(0, 1), (1, 0)])
    near = [(first, second), (below_a, below_b), (above_a, above_b)]
    far = [(far_a, far_b)]
    which = core.reshape(1)
    near_own = columns(near, [out_weight])
    near_pair = columns(near, [fetched, other], which)
    near = jnp.concatenate([near_own, near_pair], axis=1)
    from_above = shift(near[tok : 2 * tok], -1)
    from_below = shift(near[2 * tok :], 1)
    far_own = columns(far, [out_weight])
    far_pair = columns(far, [fetched, other], which)
    from_far = shift(jnp.concatenate([far_own, far_pair], axis=1), 2)
    return [near[:tok], from_above, from_far, from_below]


def product(left, right):
    return jnp.dot(left, right, preferred_element_type=F32)


def shuffle(pieces, slots, packing):
    cut = lax.broadcasted_iota(jnp.int32, (128, 128), 0 if packing else 1)
    held = lax.broadcasted_iota(jnp.int32, (128, 128), 1 if packing else 0)
    expert, piece, slot = lax.div(cut, 8), lax.rem(lax.div(cut, slots), pieces), lax.rem(cut, slots)
    return ((piece * 16 + expert) * slots + slot == held).astype(F32).astype(BF)


def packed_rows(rows, pieces, slots):
    wide = WIDTH // pieces
    cut = jnp.concatenate([rows[:, wide * s : wide * (s + 1)] for s in range(pieces)], axis=0)
    return product(shuffle(pieces, slots, True), cut).astype(BF)


def whole_rows(packed, pieces, slots):
    cut = product(shuffle(pieces, slots, False), packed).astype(BF)
    return [cut[16 * slots * s : 16 * slots * (s + 1)] for s in range(pieces)]


def make_kernel(
    place_ref, here_ref, above_ref, far_ref, below_ref, hidden_ref, gain_ref, pick_ref, last_ref,
    out_ref, halves_ref, residual_ref, normed,
):
    step = pl.program_id(0)

    @pl.when(step == 0)
    def _():
        for ahead, ref in enumerate((here_ref, above_ref, far_ref, below_ref)):
            y = lax.rem(place_ref[2] + ahead, 4)
            for part in range(2):
                high = place_ref[1] if part == 0 else 1 - place_ref[1]
                at = pl.ds(pl.multiple_of((high * 4 + y) * PACK, PACK), PACK)
                projected = ref[:, part * PACK : (part + 1) * PACK].astype(F32)
                residual_ref[:, at] = hidden_ref[:, at].astype(F32) + projected
        residual = residual_ref[...]
        mean = jnp.mean(residual * residual, axis=1, keepdims=True)
        normed[...] = (residual * lax.rsqrt(mean + 1e-06) * gain_ref[...]).astype(BF)

        halves_ref[...] = jnp.concatenate([normed[:, :HALF], normed[:, HALF:]], axis=0)

    out_ref[:, :HALF] = product(pick_ref[...], halves_ref[...]).astype(BF)
    out_ref[:, HALF:] = packed_rows(product(last_ref[...], normed[...]).astype(BF), 8, 1)


def silu_product(gated, lifted):
    return (gated / (1.0 + jnp.exp(-gated)) * lifted).astype(BF)


def expert_kernel(got_ref, gate_ref, up_ref, down_ref, out_ref):
    groups = got_ref.shape[0] // 128
    with_last = got_ref.shape[1] > HALF
    low, high = [], []
    for g in range(groups):
        pieces = whole_rows(got_ref[128 * g : 128 * (g + 1), :HALF], 2, FOUR)
        low.append(pieces[0])
        high.append(pieces[1])
    if with_last:
        for g in range(groups):
            pieces = whole_rows(got_ref[128 * g : 128 * (g + 1), HALF:], 8, 1)
            low.append(jnp.concatenate(pieces[:4], axis=1))
            high.append(jnp.concatenate(pieces[4:], axis=1))
    low, high = jnp.concatenate(low, axis=0), jnp.concatenate(high, axis=0)
    gated = product(low, gate_ref[:HALF]) + product(high, gate_ref[HALF:])
    lifted = product(low, up_ref[:HALF]) + product(high, up_ref[HALF:])
    served = product(silu_product(gated, lifted), down_ref[...]).astype(BF)
    for g in range(groups):
        out_ref[128 * g : 128 * (g + 1), :HALF] = packed_rows(served[64 * g : 64 * (g + 1)], 2, FOUR)
    if with_last:
        for g in range(groups):
            at = 64 * groups + 16 * g
            out_ref[128 * g : 128 * (g + 1), HALF:] = packed_rows(served[at : at + 16], 8, 1)


def experts(got, w_gate, w_up, w_down):
    wide = got.shape[1]
    hid = w_gate.shape[1]
    rows = SLOTS * wide // WIDTH
    return pl.pallas_call(
        expert_kernel,
        grid=(SLOTS // TILE,),
        in_specs=[tiled((TILE, wide))]
        + [pl.BlockSpec(w.shape, lambda i: (0, 0), pipeline_mode=pl.Buffered(1)) for w in (w_gate, w_up, w_down)],
        out_specs=tiled((TILE, wide)),
        out_shape=jax.ShapeDtypeStruct((SLOTS, wide), BF),
        compiler_params=pltpu.CompilerParams(vmem_limit_bytes=60 * 1024 * 1024),
        cost_estimate=pl.CostEstimate(
            flops=6 * rows * WIDTH * hid, bytes_accessed=4 * SLOTS * wide + 6 * WIDTH * hid, transcendentals=rows * hid
        ),
    )(got, w_gate, w_up, w_down)


def finish_kernel(low_ref, high_ref, split_ref, back_ref, out_ref):
    step = pl.program_id(0)
    tok, wide = low_ref.shape
    sums = product(split_ref[...], back_ref[...])
    for piece, ref in enumerate((low_ref, high_ref)):
        part = sums[2 * tok * piece : 2 * tok * (piece + 1)]
        at = pl.ds(pl.multiple_of(piece * HALF + step * wide, wide), wide)
        out_ref[:, at] = (ref[...] + (part[:tok] + part[tok:])).astype(BF)


def whole(shape, index=(0, 0)):
    return pl.BlockSpec(shape, lambda i: index)


def tiled(shape):
    return pl.BlockSpec(shape, lambda i: (i, 0))


def two_terms(weigh):
    high = weigh.astype(BF)
    low = (weigh - high.astype(F32)).astype(BF)
    return jnp.concatenate([high, low], axis=0)


def slots_of(routes, slot_gates):
    tok = routes.shape[0]
    named = routes[:, :, None] == jnp.arange(EXPERTS, dtype=jnp.int32)[None, None, :]
    hit = jnp.any(named, axis=1)
    gate = jnp.sum(jnp.where(named, slot_gates[:, :, None], 0.0), axis=1)
    before = jnp.arange(tok)[None, :] < jnp.arange(tok)[:, None]
    rank = jnp.dot(before.astype(BF), hit.astype(BF), preferred_element_type=F32)
    return hit, jnp.where(hit, rank, -1.0), gate


def layer(
    hidden,
    queries,
    keys,
    values,
    out_weight,
    norm_gain,
    routes,
    slot_scores,
    gate_weight,
    up_weight,
    down_weight,
):
    tok, _ = hidden.shape[1:]
    place = jnp.stack([lax.axis_index(CTX), lax.axis_index("xh"), lax.axis_index("y")])
    gathered = gather_pair(keys[0], values[0])
    first = attend(place, queries[0], gathered, 0)
    second = attend(place, queries[0], gathered, 1)

    score_rows = slot_scores[0]
    slot_gates = score_rows / jnp.sum(score_rows, axis=1, keepdims=True)
    _, rank, gate = slots_of(routes[0], slot_gates)
    order = jnp.arange(8)
    piece, slot = order // FOUR, (order % FOUR).astype(F32)
    placed = rank.T[:, None, :]

    def picks(start):
        taken = placed == (slot + start)[None, :, None]
        parts = [taken & (piece == p)[None, :, None] for p in range(2)]
        return jnp.concatenate(parts, axis=2).astype(BF).reshape(SLOTS, 2 * tok)

    def weighs(start):
        taken = jnp.where(rank[:, :, None] == slot + start, gate[:, :, None], 0.0)
        parts = [jnp.where(piece == p, taken, 0.0).reshape(tok, SLOTS) for p in range(2)]
        return jnp.concatenate([two_terms(part) for part in parts], axis=0)

    pick, pick_rest, pick_last = picks(0.0), picks(4.0), (rank.T == float(FULL)).astype(BF)
    split, split_rest = weighs(0.0), weighs(4.0)
    split_last = two_terms(jnp.where(rank == float(FULL), gate, 0.0))

    columns_home = project((first, second), out_weight)

    shape = jax.ShapeDtypeStruct
    weights = gate_weight[0], up_weight[0], down_weight[0]

    def swap(rows):
        wide = rows.shape[1]
        return exchange(rows.reshape(EXPERTS, 8, wide), ALL).reshape(SLOTS, wide)

    sent, halves, residual = pl.pallas_call(
        make_kernel,
        name="make",
        grid_spec=pltpu.PrefetchScalarGridSpec(
            num_scalar_prefetch=1,
            grid=(SLOTS // 128,),
            in_specs=[pl.BlockSpec((tok, 2 * PACK), lambda i, p: (0, 0))] * 4
            + [
                pl.BlockSpec((tok, WIDTH), lambda i, p: (0, 0)),
                pl.BlockSpec((1, WIDTH), lambda i, p: (0, 0)),
                pl.BlockSpec((128, 2 * tok), lambda i, p: (i, 0)),
                pl.BlockSpec((16, tok), lambda i, p: (i, 0)),
            ],
            out_specs=[
                pl.BlockSpec((128, FIRST), lambda i, p: (i, 0)),
                pl.BlockSpec((2 * tok, HALF), lambda i, p: (0, 0)),
                pl.BlockSpec((tok, WIDTH), lambda i, p: (0, 0)),
            ],
            scratch_shapes=[pltpu.VMEM((tok, WIDTH), BF)],
        ),
        out_shape=[shape((SLOTS, FIRST), BF), shape((2 * tok, HALF), BF), shape((tok, WIDTH), F32)],
        compiler_params=pltpu.CompilerParams(vmem_limit_bytes=60 * 1024 * 1024),
        cost_estimate=pl.CostEstimate(
            flops=4 * SLOTS * tok * HALF, bytes_accessed=SLOTS * FIRST * 2, transcendentals=0
        ),
    )(place, *columns_home, hidden[0], norm_gain.reshape(1, WIDTH), pick, pick_last)
    got = swap(sent)
    got_rest = swap(product(pick_rest, halves).astype(BF))
    back = swap(experts(got, *weights))
    back_rest = swap(experts(got_rest, *weights))

    sums = product(split, back[:, :HALF])
    sums = sums.reshape(2, 2, tok, HALF)
    nines = product(split_last, back[:, HALF:].reshape(EXPERTS, WIDTH))
    base = residual + (nines[:tok] + nines[tok:])
    base = base + jnp.concatenate([sums[0, 0] + sums[0, 1], sums[1, 0] + sums[1, 1]], axis=1)
    steps = HALF // PACK
    out = pl.pallas_call(
        finish_kernel,
        name="finish",
        grid=(steps,),
        in_specs=[
            pl.BlockSpec((tok, PACK), lambda i: (0, i)),
            pl.BlockSpec((tok, PACK), lambda i: (0, i + steps)),
            whole((4 * tok, SLOTS)),
            pl.BlockSpec((SLOTS, PACK), lambda i: (0, i)),
        ],
        out_specs=whole((tok, WIDTH)),
        out_shape=shape((tok, WIDTH), BF),
        compiler_params=pltpu.CompilerParams(vmem_limit_bytes=24 * 1024 * 1024),
        cost_estimate=pl.CostEstimate(
            flops=8 * tok * SLOTS * HALF, bytes_accessed=SLOTS * HALF * 2 + tok * WIDTH * 6, transcendentals=0
        ),
    )(base, base, split_rest, back_rest)
    return out[None]


def solution(mesh):
    fine = Mesh(mesh.devices.reshape(4, 2, 2, 2, 4), ALL)
    return jax.shard_map(
        layer,
        mesh=fine,
        in_specs=(
            P(DP, CTX, None),
            P(DP, CTX, None),
            P(DP, CTX, None),
            P(DP, CTX, None),
            P(None, CTX),
            P(),
            P(DP, CTX, None),
            P(DP, CTX, None),
            P(ALL, None, None),
            P(ALL, None, None),
            P(ALL, None, None),
        ),
        out_specs=P(DP, CTX, None),
        check_vma=False,
    )
```

time: 437 us -> 417 us (0.954)
  waiting for transfers between devices: 258 us -> 237 us
  Pallas kernels: 74.9 us -> 84.9 us
  matrix products: 16.2 us -> 9.19 us
  local copies, waits for them, and re-layouts: 19.7 us -> 13.2 us
    all_to_all x5, waiting for transfers between devices: 175 us -> 157 us  [exchange(): return lax.all_to_all(blocks, axes, split_axis=0, concat_axis=0, tiled=True)]
    pallas_call x7, Pallas kernels: 49.6 us -> 62.2 us  [the longest x2 44.7 us: experts(): pl.pallas_call(expert_kernel, grid=(SLOTS // TILE,), in_specs=[tiled((TIL...]
    dot_general x4 -> x3, matrix products: 15.5 us -> 8.43 us  [product(): return jnp.dot(left, right, preferred_element_type=F32)]
    pallas_call x2, Pallas kernels: 17.7 us -> 12.2 us  [attend(): pl.pallas_call(attend_kernel, grid_spec=pltpu.PrefetchScalarGridSpec(num_...]
    unnamed x38 -> x36, local copies, waits for them, and re-layouts: 9.27 us -> 5.87 us
  transfers between devices with their start and end apart: 16 -> 16, of which waited for: 12 -> 12; matrix products, arithmetic and copies ran while one was open for 7% -> 5% of each run, Pallas kernels for 11% -> 16%
where the time goes in v4:
time: 417 us; the launch traced here: 411 us
  waiting for transfers between devices  237 us (57%)
  Pallas kernels  84.9 us (20%)
  starting transfers between devices  57.9 us (14%)
  local copies, waits for them, and re-layouts  13.2 us (3%)
  matrix products  9.19 us (2%)
  other arithmetic  8.12 us (2%)
    all_to_all x5, waiting for transfers between devices, exchange(): return lax.all_to_all(blocks, axes, split_axis=0, concat_axis=0, tiled=True)  157 us
    ppermute x1, waiting for transfers between devices, project(): fetched = lax.ppermute(mine, ALL, neighbour_pairs())  51 us
    all_to_all x5, starting transfers between devices, exchange(): return lax.all_to_all(blocks, axes, split_axis=0, concat_axis=0, tiled=True)  46.8 us
    pallas_call x2, Pallas kernels, experts(): pl.pallas_call(expert_kernel, grid=(SLOTS // TILE,), in_specs=[tiled((TIL...  44.7 us
    ppermute x9, waiting for transfers between devices, shift(): return lax.ppermute(block, 'y', [(i, (i + step) % 4) for i in range(4)])  29.1 us
    pallas_call x2, Pallas kernels, attend(): pl.pallas_call(attend_kernel, grid_spec=pltpu.PrefetchScalarGridSpec(num_...  12.2 us
    pallas_call x4, Pallas kernels, columns(): pl.pallas_call(body, grid=(wide // block,), in_specs=[pl.BlockSpec(memory...  11.7 us
    pallas_call x1, Pallas kernels, layer(): pl.pallas_call(make_kernel, name='make', grid_spec=pltpu.PrefetchScalarGr...  10.5 us
  transfers between devices with their start and end apart: 16, of which 12 were waited for; matrix products, arithmetic and copies ran while one was open for 5% of the time, Pallas kernels for 16%

profile of v4, /device:TPU:91, one launch (start us, length us, event | category | flops | bytes accessed | tf_op | source)
XLA Modules:
  0.0 411.2 jit_solution(11213047097295328894)
XLA Ops:
  5.4 4.7 %all-to-all-start = ((bf16[8,128,512]{2,1,0:T(8,128)(2,1)}), bf16[8,128,512]{2,1,0:T(8,128)(2,1)S(1)}, u32[]{:S(2)}, u32[]{:S(2)}) async-start(bf16[8,128,512]{2,1,0:T(8,128)(2,1)} %broadcast_in_dim.82), calls=%async_computation | async-start | bytes 2097152 | tf_op jit(solution)/shard_map/all_to_all | solution.py:29
  10.1 51.0 %collective-permute-done.4.refs_6_.refs_2_ = bf16[2048,512]{1,0:T(8,128)(2,1)S(1)} collective-permute-done((bf16[2048,512]{1,0:T(8,128)(2,1)}, bf16[2048,512]{1,0:T(8,128)(2,1)S(1)}, u32[]{:S(2)}, u32[]{:S(2)}) %collective-permute-start.4) | collective-permute-done | bytes 2097184 | tf_op jit(solution)/shard_map/ppermute | solution.py:152
  64.2 6.1 %shard_map.109.refs_0_ = bf16[128,2048]{1,0:T(8,128)(2,1)} custom-call(s32[3]{0:T(128)S(1)} %pad_add_fusion.place_ref, bf16[128,4096]{1,0:T(8,128)(2,1)S(1)} %bitcast.54, bf16[1024,512]{1,0:T(8,128)(2,1)S(1)} %bitcast.50, bf16[1024,512]{1,0:T(8,128)(2,1)S(1)} %bitcast.51), custom_call_target="tpu_custom_call" | custom-call | flops 1073741824 | bytes 1048576 | tf_op jit(solution)/shard_map/pallas_call | solution.py:84
  70.3 6.1 %shard_map.110.refs_1_ = bf16[128,2048]{1,0:T(8,128)(2,1)} custom-call(s32[3]{0:T(128)S(1)} %pad_add_fusion.place_ref, bf16[128,4096]{1,0:T(8,128)(2,1)S(1)} %bitcast.55, bf16[1024,512]{1,0:T(8,128)(2,1)S(1)} %bitcast.52, bf16[1024,512]{1,0:T(8,128)(2,1)S(1)} %bitcast.53), custom_call_target="tpu_custom_call" | custom-call | flops 1073741824 | bytes 1048576 | tf_op jit(solution)/shard_map/pallas_call | solution.py:84
  85.4 5.9 %collective-permute-done.3.refs_5_ = bf16[128,2048]{1,0:T(8,128)(2,1)} collective-permute-done((bf16[128,2048]{1,0:T(8,128)(2,1)}, bf16[128,2048]{1,0:T(8,128)(2,1)}, u32[]{:S(2)}, u32[]{:S(2)}) %collective-permute-start.3) | collective-permute-done | bytes 524320 | tf_op jit(solution)/shard_map/ppermute | solution.py:46
  93.9 8.6 %collective-permute-done.2.refs_4_ = bf16[128,2048]{1,0:T(8,128)(2,1)} collective-permute-done((bf16[128,2048]{1,0:T(8,128)(2,1)}, bf16[128,2048]{1,0:T(8,128)(2,1)}, u32[]{:S(2)}, u32[]{:S(2)}) %collective-permute-start.2) | collective-permute-done | bytes 524320 | tf_op jit(solution)/shard_map/ppermute | solution.py:46
  104.7 4.0 shard_map.111
  108.7 4.9 %collective-permute-done.8.refs_1_ = bf16[128,2048]{1,0:T(8,128)(2,1)S(1)} collective-permute-done((bf16[128,2048]{1,0:T(8,128)(2,1)}, bf16[128,2048]{1,0:T(8,128)(2,1)S(1)}, u32[]{:S(2)}, u32[]{:S(2)}) %collective-permute-start.8) | collective-permute-done | bytes 524320 | tf_op jit(solution)/shard_map/ppermute | solution.py:46
  114.9 4.3 %shard_map.112 = bf16[384,512]{1,0:T(8,128)(2,1)S(1)} custom-call(s32[1]{0:T(128)} %bitcast.7.core_ref, bf16[128,2048]{1,0:T(8,128)(2,1)} %shard_map.109.refs_0_, bf16[128,2048]{1,0:T(8,128)(2,1)} %shard_map.110.refs_1_, bf16[128,2048]{1,0:T(8,128)(2,1)} %collective-permute-done.refs_2_, bf16[128,2048]{1,0:T(8,128)(2,1)} %collective-permute-done.1.refs_3_, ...), custom_call_target="tpu_custom_call" | custom-call | flops 1610612736 | bytes 7340032 | tf_op jit(solution)/shard_map/pallas_call | solution.py:132
  127.6 6.2 %collective-permute-done.9.far_ref = bf16[128,1024]{1,0:T(8,128)(2,1)S(1)} collective-permute-done((bf16[128,1024]{1,0:T(8,128)(2,1)S(1)}, bf16[128,1024]{1,0:T(8,128)(2,1)S(1)}, u32[]{:S(2)}, u32[]{:S(2)}) %collective-permute-start.9) | collective-permute-done | bytes 262176 | tf_op jit(solution)/shard_map/ppermute | solution.py:46
  134.5 10.5 %make.1 = (bf16[1024,2560]{1,0:T(8,128)(2,1)}, bf16[256,2048]{1,0:T(8,128)(2,1)}, f32[128,4096]{1,0:T(8,128)}) custom-call(s32[3]{0:T(128)} %copy-done.1, bf16[128,1024]{1,0:T(8,128)(2,1)} %get-tuple-element.20.here_ref, bf16[128,1024]{1,0:T(8,128)(2,1)} %copy-done.15, bf16[128,1024]{1,0:T(8,128)(2,1)} %copy-done.16, bf16[128,1024]{1,0:T(8,128)(2,1)} %copy-done.14, ...), custom_call_target="tpu_custom_call" | custom-call | flops 1073741824 | bytes 5242880 | tf_op jit(solution)/shard_map/make/pallas_call | solution.py:349
  145.0 12.5 %all-to-all-start.1 = ((bf16[128,8,2560]{2,1,0:T(8,128)(2,1)}), bf16[128,8,2560]{2,1,0:T(8,128)(2,1)}, u32[]{:S(2)}, u32[]{:S(2)}) async-start(bf16[128,8,2560]{2,1,0:T(8,128)(2,1)} %bitcast.56), calls=%async_computation.1 | async-start | bytes 10485760 | tf_op jit(solution)/shard_map/all_to_all | solution.py:29
  157.4 3.2 convert_bitcast_fusion
  160.7 57.1 %all-to-all-done.1 = bf16[128,8,2560]{2,1,0:T(8,128)(2,1)} async-done(((bf16[128,8,2560]{2,1,0:T(8,128)(2,1)}), bf16[128,8,2560]{2,1,0:T(8,128)(2,1)}, u32[]{:S(2)}, u32[]{:S(2)}) %all-to-all-start.1) | async-done | bytes 5242912 | tf_op jit(solution)/shard_map/all_to_all | solution.py:29
  217.8 10.1 %all-to-all-start.3 = ((bf16[128,8,2048]{2,1,0:T(8,128)(2,1)}), bf16[128,8,2048]{2,1,0:T(8,128)(2,1)}, u32[]{:S(2)}, u32[]{:S(2)}) async-start(bf16[128,8,2048]{2,1,0:T(8,128)(2,1)} %convert_bitcast_fusion), calls=%async_computation.3 | async-start | bytes 8388608 | tf_op jit(solution)/shard_map/all_to_all | solution.py:29
  227.9 24.0 %shard_map.115 = bf16[1024,2560]{1,0:T(8,128)(2,1)} custom-call(bf16[1024,2560]{1,0:T(8,128)(2,1)} %bitcast.15.got_ref, bf16[4096,768]{1,0:T(8,128)(2,1)} %bitcast.64, bf16[4096,768]{1,0:T(8,128)(2,1)} %bitcast.66, bf16[768,4096]{1,0:T(8,128)(2,1)} %bitcast.68), custom_call_target="tpu_custom_call" | custom-call | flops 12079595520 | bytes 29360128 | tf_op jit(solution)/shard_map/pallas_call | solution.py:252
  251.9 24.8 %all-to-all-done.3 = bf16[128,8,2048]{2,1,0:T(8,128)(2,1)} async-done(((bf16[128,8,2048]{2,1,0:T(8,128)(2,1)}), bf16[128,8,2048]{2,1,0:T(8,128)(2,1)}, u32[]{:S(2)}, u32[]{:S(2)}) %all-to-all-start.3) | async-done | bytes 4194336 | tf_op jit(solution)/shard_map/all_to_all | solution.py:29
  276.7 9.4 %all-to-all-start.2 = ((bf16[128,8,2560]{2,1,0:T(8,128)(2,1)}), bf16[128,8,2560]{2,1,0:T(8,128)(2,1)}, u32[]{:S(2)}, u32[]{:S(2)}) async-start(bf16[128,8,2560]{2,1,0:T(8,128)(2,1)} %bitcast.57), calls=%async_computation.2 | async-start | bytes 10485760 | tf_op jit(solution)/shard_map/all_to_all | solution.py:29
  286.3 20.7 %shard_map.116 = bf16[1024,2048]{1,0:T(8,128)(2,1)} custom-call(bf16[1024,2048]{1,0:T(8,128)(2,1)} %bitcast.27.got_ref, bf16[4096,768]{1,0:T(8,128)(2,1)} %bitcast.65, bf16[4096,768]{1,0:T(8,128)(2,1)} %bitcast.67, bf16[768,4096]{1,0:T(8,128)(2,1)} %bitcast.69), custom_call_target="tpu_custom_call" | custom-call | flops 9663676416 | bytes 27262976 | tf_op jit(solution)/shard_map/pallas_call | solution.py:252
  307.0 39.4 %all-to-all-done.2 = bf16[128,8,2560]{2,1,0:T(8,128)(2,1)} async-done(((bf16[128,8,2560]{2,1,0:T(8,128)(2,1)}), bf16[128,8,2560]{2,1,0:T(8,128)(2,1)}, u32[]{:S(2)}, u32[]{:S(2)}) %all-to-all-start.2) | async-done | bytes 5242912 | tf_op jit(solution)/shard_map/all_to_all | solution.py:29
  346.5 10.1 %all-to-all-start.4 = ((bf16[128,8,2048]{2,1,0:T(8,128)(2,1)}), bf16[128,8,2048]{2,1,0:T(8,128)(2,1)}, u32[]{:S(2)}, u32[]{:S(2)}) async-start(bf16[128,8,2048]{2,1,0:T(8,128)(2,1)} %bitcast.59), calls=%async_computation.4 | async-start | bytes 8388608 | tf_op jit(solution)/shard_map/all_to_all | solution.py:29
  362.8 4.5 %fusion = f32[512,2048]{1,0:T(8,128)S(1)} fusion(bf16[1024,2560]{1,0:T(8,128)(2,1)} %bitcast.20, bf16[128,1024]{1,0:T(8,128)(2,1)S(1)} %copy-done.5, bf16[128,1024]{1,0:T(8,128)(2,1)S(1)} %copy-done.6, bf16[128,1024]{1,0:T(8,128)(2,1)S(1)} %copy-done.4, bf16[128,1024]{1,0:T(8,128)(2,1)S(1)} %get-tuple-element.17), kind=kOutput, calls=%fused_computation | convolution fusion | flops 2151677952 | bytes 9437184 | tf_op jit(solution)/shard_map/dot_general | solution.py:173
  369.4 36.0 %all-to-all-done.4 = bf16[128,8,2048]{2,1,0:T(8,128)(2,1)} async-done(((bf16[128,8,2048]{2,1,0:T(8,128)(2,1)}), bf16[128,8,2048]{2,1,0:T(8,128)(2,1)}, u32[]{:S(2)}, u32[]{:S(2)}) %all-to-all-start.4) | async-done | bytes 4194336 | tf_op jit(solution)/shard_map/all_to_all | solution.py:29
  405.4 5.8 %finish.1 = bf16[128,4096]{1,0:T(8,128)(2,1)} custom-call(f32[128,4096]{1,0:T(8,128)S(1)} %fusion.3.low_ref.high_ref, f32[128,4096]{1,0:T(8,128)S(1)} %fusion.3.low_ref.high_ref, bf16[512,1024]{1,0:T(8,128)(2,1)S(1)} %pad_maximum_fusion.split_ref, bf16[1024,2048]{1,0:T(8,128)(2,1)} %bitcast.29.back_ref), custom_call_target="tpu_custom_call" | custom-call | flops 2147483648 | bytes 7340032 | tf_op jit(solution)/shard_map/finish/pallas_call | solution.py:386
  (101 shorter events, 40.9 us)
Async XLA Ops:
  0.0 4.4 %copy-start.11 = (bf16[1,128,256]{2,1,0:T(8,128)(2,1)S(1)}, bf16[1,128,256]{2,1,0:T(8,128)(2,1)}, u32[]{:S(2)}) copy-start(bf16[1,128,256]{2,1,0:T(8,128)(2,1)} %param.13) | copy-start | bytes 196612
  3.1 59.5 %copy-start.12 = (f32[1,128,8]{1,2,0:T(8,128)S(1)}, f32[1,128,8]{1,2,0:T(8,128)}, u32[]{:S(2)}) copy-start(f32[1,128,8]{1,2,0:T(8,128)} %param.18) | copy-start | bytes 12292
  3.1 59.6 %copy-start.13 = (s32[1,128,8]{1,2,0:T(8,128)S(1)}, s32[1,128,8]{1,2,0:T(8,128)}, u32[]{:S(2)}) copy-start(s32[1,128,8]{1,2,0:T(8,128)} %param.17) | copy-start | bytes 12292
  3.1 58.0 %collective-permute-start.4 = (bf16[2048,512]{1,0:T(8,128)(2,1)}, bf16[2048,512]{1,0:T(8,128)(2,1)S(1)}, u32[]{:S(2)}, u32[]{:S(2)}) collective-permute-start(bf16[2048,512]{1,0:T(8,128)(2,1)} %constant_dynamic-slice_fusion), channel_id=1, source_target_pairs={{0,20},{1,21},{2,22},{3,23},{4,16},{5,17},{6,18},{7,19},{8,28},{9,... | collective-permute-start | bytes 6291464 | tf_op jit(solution)/shard_map/ppermute | solution.py:152
  5.4 57.6 %all-to-all-start = ((bf16[8,128,512]{2,1,0:T(8,128)(2,1)}), bf16[8,128,512]{2,1,0:T(8,128)(2,1)S(1)}, u32[]{:S(2)}, u32[]{:S(2)}) async-start(bf16[8,128,512]{2,1,0:T(8,128)(2,1)} %broadcast_in_dim.82), calls=%async_computation | async-start | bytes 2097152 | tf_op jit(solution)/shard_map/all_to_all | solution.py:29
  61.1 53.8 %collective-permute-start.5 = (bf16[2048,512]{1,0:T(8,128)(2,1)S(1)}, bf16[2048,512]{1,0:T(8,128)(2,1)}, u32[]{:S(2)}, u32[]{:S(2)}) collective-permute-start(bf16[2048,512]{1,0:T(8,128)(2,1)S(1)} %collective-permute-done.4.refs_6_.refs_2_), channel_id=1, source_target_pairs={{0,8},{8,0},{1,9},{9,1},{2,10},{10,2},{3,11},{11,3},{4,12},{12,4},... | collective-permute-start | bytes 6291464 | tf_op jit(solution)/shard_map/ppermute | solution.py:157
  63.0 13.5 %copy-start.1 = (s32[3]{0:T(128)}, s32[3]{0:T(128)S(1)}, u32[]{:S(2)}) copy-start(s32[3]{0:T(128)S(1)} %pad_add_fusion.place_ref) | copy-start | bytes 40
  70.3 13.8 %collective-permute-start = (bf16[128,2048]{1,0:T(8,128)(2,1)}, bf16[128,2048]{1,0:T(8,128)(2,1)}, u32[]{:S(2)}, u32[]{:S(2)}) collective-permute-start(bf16[128,2048]{1,0:T(8,128)(2,1)} %shard_map.109.refs_0_), channel_id=1, source_target_pairs={{0,1},{1,2},{2,3},{3,0},{4,5},{5,6},{6,7},{7,4},{8,9},{9,10},{10,1... | collective-permute-start | bytes 1572872 | tf_op jit(solution)/shard_map/ppermute | solution.py:46
  76.5 14.8 %collective-permute-start.3 = (bf16[128,2048]{1,0:T(8,128)(2,1)}, bf16[128,2048]{1,0:T(8,128)(2,1)}, u32[]{:S(2)}, u32[]{:S(2)}) collective-permute-start(bf16[128,2048]{1,0:T(8,128)(2,1)} %shard_map.110.refs_1_), channel_id=1, source_target_pairs={{0,3},{1,0},{2,1},{3,2},{4,7},{5,4},{6,5},{7,6},{8,11},{9,8},{10,9... | collective-permute-start | bytes 1572872 | tf_op jit(solution)/shard_map/ppermute | solution.py:46
  78.5 23.9 %collective-permute-start.2 = (bf16[128,2048]{1,0:T(8,128)(2,1)}, bf16[128,2048]{1,0:T(8,128)(2,1)}, u32[]{:S(2)}, u32[]{:S(2)}) collective-permute-start(bf16[128,2048]{1,0:T(8,128)(2,1)} %shard_map.109.refs_0_), channel_id=1, source_target_pairs={{0,3},{1,0},{2,1},{3,2},{4,7},{5,4},{6,5},{7,6},{8,11},{9,8},{10,9... | collective-permute-start | bytes 1572872 | tf_op jit(solution)/shard_map/ppermute | solution.py:46
  79.1 23.4 %collective-permute-start.1 = (bf16[128,2048]{1,0:T(8,128)(2,1)}, bf16[128,2048]{1,0:T(8,128)(2,1)}, u32[]{:S(2)}, u32[]{:S(2)}) collective-permute-start(bf16[128,2048]{1,0:T(8,128)(2,1)} %shard_map.110.refs_1_), channel_id=1, source_target_pairs={{0,1},{1,2},{2,3},{3,0},{4,5},{5,6},{6,7},{7,4},{8,9},{9,10},{10,1... | collective-permute-start | bytes 1572872 | tf_op jit(solution)/shard_map/ppermute | solution.py:46
  84.1 24.6 %collective-permute-start.7 = (bf16[128,2048]{1,0:T(8,128)(2,1)}, bf16[128,2048]{1,0:T(8,128)(2,1)S(1)}, u32[]{:S(2)}, u32[]{:S(2)}) collective-permute-start(bf16[128,2048]{1,0:T(8,128)(2,1)} %collective-permute-done.refs_2_), channel_id=1, source_target_pairs={{0,1},{1,2},{2,3},{3,0},{4,5},{5,6},{6,7},{7,4},{8,9},{9,10},{10,1... | collective-permute-start | bytes 1572872 | tf_op jit(solution)/shard_map/ppermute | solution.py:46
  91.2 22.4 %collective-permute-start.8 = (bf16[128,2048]{1,0:T(8,128)(2,1)}, bf16[128,2048]{1,0:T(8,128)(2,1)S(1)}, u32[]{:S(2)}, u32[]{:S(2)}) collective-permute-start(bf16[128,2048]{1,0:T(8,128)(2,1)} %collective-permute-done.3.refs_5_), channel_id=1, source_target_pairs={{0,3},{1,0},{2,1},{3,2},{4,7},{5,4},{6,5},{7,6},{8,11},{9,8},{10,9... | collective-permute-start | bytes 1572872 | tf_op jit(solution)/shard_map/ppermute | solution.py:46
  119.9 6.8 %collective-permute-start.10 = (bf16[128,1024]{1,0:T(8,128)(2,1)S(1)}, bf16[128,1024]{1,0:T(8,128)(2,1)S(1)}, u32[]{:S(2)}, u32[]{:S(2)}) collective-permute-start(bf16[128,1024]{1,0:T(8,128)(2,1)S(1)} %get-tuple-element.19), channel_id=1, source_target_pairs={{0,1},{1,2},{2,3},{3,0},{4,5},{5,6},{6,7},{7,4},{8,9},{9,10},{10,1... | collective-permute-start | bytes 786440 | tf_op jit(solution)/shard_map/ppermute | solution.py:46
  119.9 7.7 %collective-permute-start.6 = (bf16[128,1024]{1,0:T(8,128)(2,1)S(1)}, bf16[128,1024]{1,0:T(8,128)(2,1)S(1)}, u32[]{:S(2)}, u32[]{:S(2)}) collective-permute-start(bf16[128,1024]{1,0:T(8,128)(2,1)S(1)} %get-tuple-element.21), channel_id=1, source_target_pairs={{0,3},{1,0},{2,1},{3,2},{4,7},{5,4},{6,5},{7,6},{8,11},{9,8},{10,9... | collective-permute-start | bytes 786440 | tf_op jit(solution)/shard_map/ppermute | solution.py:46
  123.6 10.1 %collective-permute-start.9 = (bf16[128,1024]{1,0:T(8,128)(2,1)S(1)}, bf16[128,1024]{1,0:T(8,128)(2,1)S(1)}, u32[]{:S(2)}, u32[]{:S(2)}) collective-permute-start(bf16[128,1024]{1,0:T(8,128)(2,1)S(1)} %pad_maximum_fusion.2), channel_id=1, source_target_pairs={{0,2},{1,3},{2,0},{3,1},{4,6},{5,7},{6,4},{7,5},{8,10},{9,11},{10,... | collective-permute-start | bytes 786440 | tf_op jit(solution)/shard_map/ppermute | solution.py:46
  126.7 7.1 %copy-start.14 = (bf16[128,1024]{1,0:T(8,128)(2,1)}, bf16[128,1024]{1,0:T(8,128)(2,1)S(1)}, u32[]{:S(2)}) copy-start(bf16[128,1024]{1,0:T(8,128)(2,1)S(1)} %collective-permute-done.10.below_ref) | copy-start | bytes 786436
  127.6 6.2 %copy-start.15 = (bf16[128,1024]{1,0:T(8,128)(2,1)}, bf16[128,1024]{1,0:T(8,128)(2,1)S(1)}, u32[]{:S(2)}) copy-start(bf16[128,1024]{1,0:T(8,128)(2,1)S(1)} %collective-permute-done.6.above_ref) | copy-start | bytes 786436
  144.9 12.5 %copy-start.7 = (pred[1024,128]{1,0:T(32,128)(4,1)S(1)}, pred[1024,128]{1,0:T(32,128)(4,1)}, u32[]{:S(2)}) copy-start(pred[1024,128]{1,0:T(32,128)(4,1)} %get-tuple-element.31) | copy-start | bytes 393220
  144.9 12.5 %copy-start.17 = (bf16[256,2048]{1,0:T(8,128)(2,1)S(1)}, bf16[256,2048]{1,0:T(8,128)(2,1)}, u32[]{:S(2)}) copy-start(bf16[256,2048]{1,0:T(8,128)(2,1)} %get-tuple-element.10) | copy-start | bytes 3145732
  145.0 72.8 %all-to-all-start.1 = ((bf16[128,8,2560]{2,1,0:T(8,128)(2,1)}), bf16[128,8,2560]{2,1,0:T(8,128)(2,1)}, u32[]{:S(2)}, u32[]{:S(2)}) async-start(bf16[128,8,2560]{2,1,0:T(8,128)(2,1)} %bitcast.56), calls=%async_computation.1 | async-start | bytes 10485760 | tf_op jit(solution)/shard_map/all_to_all | solution.py:29
  217.8 58.9 %all-to-all-start.3 = ((bf16[128,8,2048]{2,1,0:T(8,128)(2,1)}), bf16[128,8,2048]{2,1,0:T(8,128)(2,1)}, u32[]{:S(2)}, u32[]{:S(2)}) async-start(bf16[128,8,2048]{2,1,0:T(8,128)(2,1)} %convert_bitcast_fusion), calls=%async_computation.3 | async-start | bytes 8388608 | tf_op jit(solution)/shard_map/all_to_all | solution.py:29
  276.7 69.8 %all-to-all-start.2 = ((bf16[128,8,2560]{2,1,0:T(8,128)(2,1)}), bf16[128,8,2560]{2,1,0:T(8,128)(2,1)}, u32[]{:S(2)}, u32[]{:S(2)}) async-start(bf16[128,8,2560]{2,1,0:T(8,128)(2,1)} %bitcast.57), calls=%async_computation.2 | async-start | bytes 10485760 | tf_op jit(solution)/shard_map/all_to_all | solution.py:29
  346.5 58.9 %all-to-all-start.4 = ((bf16[128,8,2048]{2,1,0:T(8,128)(2,1)}), bf16[128,8,2048]{2,1,0:T(8,128)(2,1)}, u32[]{:S(2)}, u32[]{:S(2)}) async-start(bf16[128,8,2048]{2,1,0:T(8,128)(2,1)} %bitcast.59), calls=%async_computation.4 | async-start | bytes 8388608 | tf_op jit(solution)/shard_map/all_to_all | solution.py:29
  (10 other events, 16.8 us)

commit v5 on v4

--- a/solution.py
+++ b/solution.py
@@ -48,20 +48,32 @@
 
 def gather_pair(keys, values):
     pair = jnp.concatenate([keys, values], axis=1)
-    gathered = exchange(jnp.broadcast_to(pair[None], (8,) + pair.shape), CTX)
-    return gathered.reshape(8 * pair.shape[0], pair.shape[1])
-
-
-def attend_kernel(place_ref, query_ref, key_ref, value_ref, out_ref, bias, flipped):
+    blocks = [pair]
+    for ahead in range(1, 8):
+        pairs = []
+        for index in range(8):
+            xh, y = index // 4, index % 4
+            pairs.append(((xh ^ (ahead // 4)) * 4 + (y + ahead) % 4, index))
+        blocks.append(lax.ppermute(pair, CTX, pairs))
+    return blocks
+
+
+def attend_kernel(place_ref, query_ref, *refs):
+    *block_refs, out_ref, bias, flipped, held = refs
     tok = query_ref.shape[0]
     heads = query_ref.shape[1] // DH
 
     @pl.when(pl.program_id(0) == 0)
     def _():
-        query_pos = place_ref[0] * tok + lax.broadcasted_iota(jnp.int32, bias.shape, 0)
-        key_pos = lax.broadcasted_iota(jnp.int32, bias.shape, 1)
-        bias[...] = jnp.where(key_pos <= query_pos, 0.0, -1e30)
-        flipped[...] = key_ref[...].T
+        query_pos = place_ref[0] * tok + lax.broadcasted_iota(jnp.int32, (tok, tok), 0)
+        for ahead in range(8):
+            high = place_ref[1] if ahead < 4 else 1 - place_ref[1]
+            source = high * 4 + lax.rem(place_ref[2] + ahead, 4)
+            key_pos = source * tok + lax.broadcasted_iota(jnp.int32, (tok, tok), 1)
+            at = slice(ahead * tok, (ahead + 1) * tok)
+            bias[:, at] = jnp.where(key_pos <= query_pos, 0.0, -1e30)
+            flipped[:, at] = block_refs[2 * ahead][...].T
+            held[at] = block_refs[2 * ahead + 1][...]
 
     for head in range(0, heads, 2):
         pair = [slice((head + i) * DH, (head + i + 1) * DH) for i in range(2)]
@@ -70,36 +82,38 @@
         scores = scores + jnp.concatenate([bias[...], bias[...]], axis=0)
         weights = jnp.exp(scores - jnp.max(scores, axis=1, keepdims=True))
         total = jnp.sum(weights, axis=1, keepdims=True)
-        out = (product(weights.astype(BF), value_ref[...]) / total).astype(BF)
+        out = (product(weights.astype(BF), held[...]) / total).astype(BF)
         for i, at in enumerate(pair):
             out_ref[:, at] = out[i * tok : (i + 1) * tok]
 
 
-def attend(place, queries, gathered, head):
+def attend(place, queries, blocks, head):
     tok = queries.shape[0]
-    keys = gathered.shape[0]
+    keys = len(blocks) * tok
     half = queries.shape[1] // KVH
     block = 4 * DH
     steps = half // block
+    specs = [
+        pl.BlockSpec((tok, DH), lambda i, p: (0, head)),
+        pl.BlockSpec((tok, DH), lambda i, p: (0, KVH + head)),
+    ]
     return pl.pallas_call(
         attend_kernel,
         grid_spec=pltpu.PrefetchScalarGridSpec(
             num_scalar_prefetch=1,
             grid=(steps,),
-            in_specs=[
-                pl.BlockSpec((tok, block), lambda i, p: (0, head * steps + i)),
-                pl.BlockSpec((keys, DH), lambda i, p: (0, head)),
-                pl.BlockSpec((keys, DH), lambda i, p: (0, KVH + head)),
+            in_specs=[pl.BlockSpec((tok, block), lambda i, p: (0, head * steps + i))] + specs * len(blocks),
+            out_specs=pl.BlockSpec((tok, block), lambda i, p: (0, i)),
+            scratch_shapes=[
+                pltpu.VMEM((tok, keys), F32), pltpu.VMEM((DH, keys), BF), pltpu.VMEM((keys, DH), BF)
             ],
-            out_specs=pl.BlockSpec((tok, block), lambda i, p: (0, i)),
-            scratch_shapes=[pltpu.VMEM((tok, keys), F32), pltpu.VMEM((DH, keys), BF)],
         ),
         out_shape=jax.ShapeDtypeStruct((tok, half), BF),
         compiler_params=pltpu.CompilerParams(vmem_limit_bytes=16 * 1024 * 1024),
         cost_estimate=pl.CostEstimate(
             flops=4 * tok * half * keys, bytes_accessed=4 * tok * half, transcendentals=tok * half * 8
         ),
-    )(place, queries, gathered, gathered)
+    )(place, queries, *[block for block in blocks for _ in range(2)])
 
 
 def own_kernel(*refs):
@@ -158,12 +172,13 @@
     near = [(first, second), (below_a, below_b), (above_a, above_b)]
     far = [(far_a, far_b)]
     which = core.reshape(1)
-    near_own = columns(near, [out_weight])
+    weight = out_weight
+    near_own = columns(near, [weight])
     near_pair = columns(near, [fetched, other], which)
     near = jnp.concatenate([near_own, near_pair], axis=1)
     from_above = shift(near[tok : 2 * tok], -1)
     from_below = shift(near[2 * tok :], 1)
-    far_own = columns(far, [out_weight])
+    far_own = columns(far, [weight])
     far_pair = columns(far, [fetched, other], which)
     from_far = shift(jnp.concatenate([far_own, far_pair], axis=1), 2)
     return [near[:tok], from_above, from_far, from_below]
@@ -193,7 +208,7 @@
 
 def make_kernel(
     place_ref, here_ref, above_ref, far_ref, below_ref, hidden_ref, gain_ref, pick_ref, last_ref,
-    out_ref, halves_ref, residual_ref, normed,
+    out_ref, halves_ref, residual_ref, normed, last_rows,
 ):
     step = pl.program_id(0)
 
@@ -211,9 +226,12 @@
         normed[...] = (residual * lax.rsqrt(mean + 1e-06) * gain_ref[...]).astype(BF)
 
         halves_ref[...] = jnp.concatenate([normed[:, :HALF], normed[:, HALF:]], axis=0)
+        last_rows[...] = product(last_ref[...], normed[...]).astype(BF)
 
     out_ref[:, :HALF] = product(pick_ref[...], halves_ref[...]).astype(BF)
-    out_ref[:, HALF:] = packed_rows(product(last_ref[...], normed[...]).astype(BF), 8, 1)
+    for i in range(2):
+        rows = last_rows[pl.ds(pl.multiple_of(step * 32 + 16 * i, 16), 16), :]
+        out_ref[128 * i : 128 * (i + 1), HALF:] = packed_rows(rows, 8, 1)
 
 
 def silu_product(gated, lifted):
@@ -351,23 +369,23 @@
         name="make",
         grid_spec=pltpu.PrefetchScalarGridSpec(
             num_scalar_prefetch=1,
-            grid=(SLOTS // 128,),
+            grid=(SLOTS // 256,),
             in_specs=[pl.BlockSpec((tok, 2 * PACK), lambda i, p: (0, 0))] * 4
             + [
                 pl.BlockSpec((tok, WIDTH), lambda i, p: (0, 0)),
                 pl.BlockSpec((1, WIDTH), lambda i, p: (0, 0)),
-                pl.BlockSpec((128, 2 * tok), lambda i, p: (i, 0)),
-                pl.BlockSpec((16, tok), lambda i, p: (i, 0)),
+                pl.BlockSpec((256, 2 * tok), lambda i, p: (i, 0)),
+                pl.BlockSpec((EXPERTS, tok), lambda i, p: (0, 0)),
             ],
             out_specs=[
-                pl.BlockSpec((128, FIRST), lambda i, p: (i, 0)),
+                pl.BlockSpec((256, FIRST), lambda i, p: (i, 0)),
                 pl.BlockSpec((2 * tok, HALF), lambda i, p: (0, 0)),
                 pl.BlockSpec((tok, WIDTH), lambda i, p: (0, 0)),
             ],
-            scratch_shapes=[pltpu.VMEM((tok, WIDTH), BF)],
+            scratch_shapes=[pltpu.VMEM((tok, WIDTH), BF), pltpu.VMEM((EXPERTS, WIDTH), BF)],
         ),
         out_shape=[shape((SLOTS, FIRST), BF), shape((2 * tok, HALF), BF), shape((tok, WIDTH), F32)],
-        compiler_params=pltpu.CompilerParams(vmem_limit_bytes=60 * 1024 * 1024),
+        compiler_params=pltpu.CompilerParams(vmem_limit_bytes=57 * 1024 * 1024),
         cost_estimate=pl.CostEstimate(
             flops=4 * SLOTS * tok * HALF, bytes_accessed=SLOTS * FIRST * 2, transcendentals=0
         ),

time: 417 us -> 420 us (level)
  starting transfers between devices: 57.9 us -> 66.5 us
    ppermute x0 -> x7, starting transfers between devices: none -> 13.3 us  [gather_pair(): blocks.append(lax.ppermute(pair, CTX, pairs))]
    ppermute x0 -> x7, waiting for transfers between devices: none -> 7.66 us  [gather_pair(): blocks.append(lax.ppermute(pair, CTX, pairs))]
    ppermute x1, waiting for transfers between devices: 51 us -> 45.3 us  [project(): fetched = lax.ppermute(mine, ALL, neighbour_pairs())]
    all_to_all x5 -> x4, starting transfers between devices: 46.8 us -> 41.5 us  [exchange(): return lax.all_to_all(blocks, axes, split_axis=0, concat_axis=0, tiled=True)]
    all_to_all x5 -> x4, waiting for transfers between devices: 157 us -> 157 us  [exchange(): return lax.all_to_all(blocks, axes, split_axis=0, concat_axis=0, tiled=True)]
  transfers between devices with their start and end apart: 16 -> 22, of which waited for: 12 -> 15; matrix products, arithmetic and copies ran while one was open for 5% -> 5% of each run, Pallas kernels for 16% -> 16%
where the time goes in v5:
time: 420 us; the launch traced here: 415 us
  waiting for transfers between devices  237 us (56%)
  Pallas kernels  82.9 us (20%)
  starting transfers between devices  66.5 us (16%)
  local copies, waits for them, and re-layouts  10.8 us (3%)
  matrix products  9.18 us (2%)
  other arithmetic  8.11 us (2%)
    all_to_all x4, waiting for transfers between devices, exchange(): return lax.all_to_all(blocks, axes, split_axis=0, concat_axis=0, tiled=True)  157 us
    ppermute x1, waiting for transfers between devices, project(): fetched = lax.ppermute(mine, ALL, neighbour_pairs())  45.3 us
    pallas_call x2, Pallas kernels, experts(): pl.pallas_call(expert_kernel, grid=(SLOTS // TILE,), in_specs=[tiled((TIL...  44.7 us
    all_to_all x4, starting transfers between devices, exchange(): return lax.all_to_all(blocks, axes, split_axis=0, concat_axis=0, tiled=True)  41.5 us
    ppermute x9, waiting for transfers between devices, shift(): return lax.ppermute(block, 'y', [(i, (i + step) % 4) for i in range(4)])  26.9 us
    ppermute x7, starting transfers between devices, gather_pair(): blocks.append(lax.ppermute(pair, CTX, pairs))  13.3 us
    pallas_call x2, Pallas kernels, attend(): pl.pallas_call(attend_kernel, grid_spec=pltpu.PrefetchScalarGridSpec(num_...  12.7 us
    pallas_call x4, Pallas kernels, columns(): pl.pallas_call(body, grid=(wide // block,), in_specs=[pl.BlockSpec(memory...  11.7 us
  transfers between devices with their start and end apart: 22, of which 15 were waited for; matrix products, arithmetic and copies ran while one was open for 5% of the time, Pallas kernels for 16%

profile of v5, /device:TPU:91, one launch (start us, length us, event | category | flops | bytes accessed | tf_op | source)
XLA Modules:
  0.0 415.2 jit_solution(462482684135011216)
XLA Ops:
  3.1 45.3 %collective-permute-done.11.refs_6_.refs_2_ = bf16[2048,512]{1,0:T(8,128)(2,1)S(1)} collective-permute-done((bf16[2048,512]{1,0:T(8,128)(2,1)S(1)}, bf16[2048,512]{1,0:T(8,128)(2,1)S(1)}, u32[]{:S(2)}, u32[]{:S(2)}) %collective-permute-start.11) | collective-permute-done | bytes 2097184 | tf_op jit(solution)/shard_map/ppermute | solution.py:166
  67.3 4.0 collective-permute-done.refs_2_.refs_3_
  72.4 6.3 %shard_map.109.refs_0_ = bf16[128,2048]{1,0:T(8,128)(2,1)} custom-call(s32[3]{0:T(128)S(1)} %pad_add_fusion.place_ref, bf16[128,4096]{1,0:T(8,128)(2,1)S(1)} %bitcast.49, bf16[128,512]{1,0:T(8,128)(2,1)S(1)} %pad_maximum_fusion.3.refs_0_.refs_1_, bf16[128,512]{1,0:T(8,128)(2,1)S(1)} %pad_maximum_fusion.3.refs_0_.refs_1_, ...), custom_call_target="tpu_custom_call" | custom-call | flops 1073741824 | bytes 1048576 | tf_op jit(solution)/shard_map/pallas_call | solution.py:100
  78.8 6.4 %shard_map.110.refs_1_ = bf16[128,2048]{1,0:T(8,128)(2,1)} custom-call(s32[3]{0:T(128)S(1)} %pad_add_fusion.place_ref, bf16[128,4096]{1,0:T(8,128)(2,1)S(1)} %bitcast.50, bf16[128,512]{1,0:T(8,128)(2,1)S(1)} %pad_maximum_fusion.3.refs_0_.refs_1_, bf16[128,512]{1,0:T(8,128)(2,1)S(1)} %pad_maximum_fusion.3.refs_0_.refs_1_, ...), custom_call_target="tpu_custom_call" | custom-call | flops 1073741824 | bytes 1048576 | tf_op jit(solution)/shard_map/pallas_call | solution.py:100
  91.6 6.0 %collective-permute-done.10.refs_5_ = bf16[128,2048]{1,0:T(8,128)(2,1)} collective-permute-done((bf16[128,2048]{1,0:T(8,128)(2,1)}, bf16[128,2048]{1,0:T(8,128)(2,1)}, u32[]{:S(2)}, u32[]{:S(2)}) %collective-permute-start.10) | collective-permute-done | bytes 524320 | tf_op jit(solution)/shard_map/ppermute | solution.py:46
  100.1 8.8 %collective-permute-done.9.refs_4_ = bf16[128,2048]{1,0:T(8,128)(2,1)} collective-permute-done((bf16[128,2048]{1,0:T(8,128)(2,1)}, bf16[128,2048]{1,0:T(8,128)(2,1)}, u32[]{:S(2)}, u32[]{:S(2)}) %collective-permute-start.9) | collective-permute-done | bytes 524320 | tf_op jit(solution)/shard_map/ppermute | solution.py:46
  111.1 4.0 shard_map.111
  115.1 4.9 %collective-permute-done.15.refs_1_ = bf16[128,2048]{1,0:T(8,128)(2,1)S(1)} collective-permute-done((bf16[128,2048]{1,0:T(8,128)(2,1)}, bf16[128,2048]{1,0:T(8,128)(2,1)S(1)}, u32[]{:S(2)}, u32[]{:S(2)}) %collective-permute-start.15) | collective-permute-done | bytes 524320 | tf_op jit(solution)/shard_map/ppermute | solution.py:46
  121.3 4.3 %shard_map.112 = bf16[384,512]{1,0:T(8,128)(2,1)S(1)} custom-call(s32[1]{0:T(128)} %bitcast.6.core_ref, bf16[128,2048]{1,0:T(8,128)(2,1)} %shard_map.109.refs_0_, bf16[128,2048]{1,0:T(8,128)(2,1)} %shard_map.110.refs_1_, bf16[128,2048]{1,0:T(8,128)(2,1)} %collective-permute-done.7.refs_2_, bf16[128,2048]{1,0:T(8,128)(2,1)} %collective-permute-done.8.refs_3_, ...), custom_call_target="tpu_custom_call" | custom-call | flops 1610612736 | bytes 7340032 | tf_op jit(solution)/shard_map/pallas_call | solution.py:146
  135.2 5.6 %collective-permute-done.16.far_ref = bf16[128,1024]{1,0:T(8,128)(2,1)S(1)} collective-permute-done((bf16[128,1024]{1,0:T(8,128)(2,1)S(1)}, bf16[128,1024]{1,0:T(8,128)(2,1)S(1)}, u32[]{:S(2)}, u32[]{:S(2)}) %collective-permute-start.16) | collective-permute-done | bytes 262176 | tf_op jit(solution)/shard_map/ppermute | solution.py:46
  141.5 8.1 %make.1 = (bf16[1024,2560]{1,0:T(8,128)(2,1)}, bf16[256,2048]{1,0:T(8,128)(2,1)}, f32[128,4096]{1,0:T(8,128)}) custom-call(s32[3]{0:T(128)} %copy-done.1, bf16[128,1024]{1,0:T(8,128)(2,1)} %get-tuple-element.20.here_ref, bf16[128,1024]{1,0:T(8,128)(2,1)} %copy-done.15, bf16[128,1024]{1,0:T(8,128)(2,1)} %copy-done.16, bf16[128,1024]{1,0:T(8,128)(2,1)} %copy-done.14, ...), custom_call_target="tpu_custom_call" | custom-call | flops 1073741824 | bytes 5242880 | tf_op jit(solution)/shard_map/make/pallas_call | solution.py:367
  149.6 11.8 %all-to-all-start = ((bf16[128,8,2560]{2,1,0:T(8,128)(2,1)}), bf16[128,8,2560]{2,1,0:T(8,128)(2,1)}, u32[]{:S(2)}, u32[]{:S(2)}) async-start(bf16[128,8,2560]{2,1,0:T(8,128)(2,1)} %bitcast.51), calls=%async_computation | async-start | bytes 10485760 | tf_op jit(solution)/shard_map/all_to_all | solution.py:29
  161.4 3.2 convert_bitcast_fusion
  164.7 57.1 %all-to-all-done = bf16[128,8,2560]{2,1,0:T(8,128)(2,1)} async-done(((bf16[128,8,2560]{2,1,0:T(8,128)(2,1)}), bf16[128,8,2560]{2,1,0:T(8,128)(2,1)}, u32[]{:S(2)}, u32[]{:S(2)}) %all-to-all-start) | async-done | bytes 5242912 | tf_op jit(solution)/shard_map/all_to_all | solution.py:29
  221.8 10.1 %all-to-all-start.2 = ((bf16[128,8,2048]{2,1,0:T(8,128)(2,1)}), bf16[128,8,2048]{2,1,0:T(8,128)(2,1)}, u32[]{:S(2)}, u32[]{:S(2)}) async-start(bf16[128,8,2048]{2,1,0:T(8,128)(2,1)} %convert_bitcast_fusion), calls=%async_computation.2 | async-start | bytes 8388608 | tf_op jit(solution)/shard_map/all_to_all | solution.py:29
  231.9 24.0 %shard_map.115 = bf16[1024,2560]{1,0:T(8,128)(2,1)} custom-call(bf16[1024,2560]{1,0:T(8,128)(2,1)} %bitcast.14.got_ref, bf16[4096,768]{1,0:T(8,128)(2,1)} %bitcast.59, bf16[4096,768]{1,0:T(8,128)(2,1)} %bitcast.61, bf16[768,4096]{1,0:T(8,128)(2,1)} %bitcast.63), custom_call_target="tpu_custom_call" | custom-call | flops 12079595520 | bytes 29360128 | tf_op jit(solution)/shard_map/pallas_call | solution.py:270
  255.9 24.8 %all-to-all-done.2 = bf16[128,8,2048]{2,1,0:T(8,128)(2,1)} async-done(((bf16[128,8,2048]{2,1,0:T(8,128)(2,1)}), bf16[128,8,2048]{2,1,0:T(8,128)(2,1)}, u32[]{:S(2)}, u32[]{:S(2)}) %all-to-all-start.2) | async-done | bytes 4194336 | tf_op jit(solution)/shard_map/all_to_all | solution.py:29
  280.7 9.4 %all-to-all-start.1 = ((bf16[128,8,2560]{2,1,0:T(8,128)(2,1)}), bf16[128,8,2560]{2,1,0:T(8,128)(2,1)}, u32[]{:S(2)}, u32[]{:S(2)}) async-start(bf16[128,8,2560]{2,1,0:T(8,128)(2,1)} %bitcast.52), calls=%async_computation.1 | async-start | bytes 10485760 | tf_op jit(solution)/shard_map/all_to_all | solution.py:29
  290.3 20.7 %shard_map.116 = bf16[1024,2048]{1,0:T(8,128)(2,1)} custom-call(bf16[1024,2048]{1,0:T(8,128)(2,1)} %bitcast.26.got_ref, bf16[4096,768]{1,0:T(8,128)(2,1)} %bitcast.60, bf16[4096,768]{1,0:T(8,128)(2,1)} %bitcast.62, bf16[768,4096]{1,0:T(8,128)(2,1)} %bitcast.64), custom_call_target="tpu_custom_call" | custom-call | flops 9663676416 | bytes 27262976 | tf_op jit(solution)/shard_map/pallas_call | solution.py:270
  311.0 39.5 %all-to-all-done.1 = bf16[128,8,2560]{2,1,0:T(8,128)(2,1)} async-done(((bf16[128,8,2560]{2,1,0:T(8,128)(2,1)}), bf16[128,8,2560]{2,1,0:T(8,128)(2,1)}, u32[]{:S(2)}, u32[]{:S(2)}) %all-to-all-start.1) | async-done | bytes 5242912 | tf_op jit(solution)/shard_map/all_to_all | solution.py:29
  350.5 10.1 %all-to-all-start.3 = ((bf16[128,8,2048]{2,1,0:T(8,128)(2,1)}), bf16[128,8,2048]{2,1,0:T(8,128)(2,1)}, u32[]{:S(2)}, u32[]{:S(2)}) async-start(bf16[128,8,2048]{2,1,0:T(8,128)(2,1)} %bitcast.54), calls=%async_computation.3 | async-start | bytes 8388608 | tf_op jit(solution)/shard_map/all_to_all | solution.py:29
  366.8 4.5 %fusion = f32[512,2048]{1,0:T(8,128)S(1)} fusion(bf16[1024,2560]{1,0:T(8,128)(2,1)} %bitcast.19, bf16[128,1024]{1,0:T(8,128)(2,1)S(1)} %copy-done.5, bf16[128,1024]{1,0:T(8,128)(2,1)S(1)} %copy-done.6, bf16[128,1024]{1,0:T(8,128)(2,1)S(1)} %copy-done.4, bf16[128,1024]{1,0:T(8,128)(2,1)S(1)} %get-tuple-element.17), kind=kOutput, calls=%fused_computation | convolution fusion | flops 2151677952 | bytes 9437184 | tf_op jit(solution)/shard_map/dot_general | solution.py:188
  373.4 36.0 %all-to-all-done.3 = bf16[128,8,2048]{2,1,0:T(8,128)(2,1)} async-done(((bf16[128,8,2048]{2,1,0:T(8,128)(2,1)}), bf16[128,8,2048]{2,1,0:T(8,128)(2,1)}, u32[]{:S(2)}, u32[]{:S(2)}) %all-to-all-start.3) | async-done | bytes 4194336 | tf_op jit(solution)/shard_map/all_to_all | solution.py:29
  409.4 5.8 %finish.1 = bf16[128,4096]{1,0:T(8,128)(2,1)} custom-call(f32[128,4096]{1,0:T(8,128)S(1)} %fusion.3.low_ref.high_ref, f32[128,4096]{1,0:T(8,128)S(1)} %fusion.3.low_ref.high_ref, bf16[512,1024]{1,0:T(8,128)(2,1)S(1)} %pad_maximum_fusion.split_ref, bf16[1024,2048]{1,0:T(8,128)(2,1)} %bitcast.28.back_ref), custom_call_target="tpu_custom_call" | custom-call | flops 2147483648 | bytes 7340032 | tf_op jit(solution)/shard_map/finish/pallas_call | solution.py:404
  (112 shorter events, 54.2 us)
Async XLA Ops:
  0.0 57.7 %copy-start.12 = (f32[1,128,8]{1,2,0:T(8,128)S(1)}, f32[1,128,8]{1,2,0:T(8,128)}, u32[]{:S(2)}) copy-start(f32[1,128,8]{1,2,0:T(8,128)} %param.18) | copy-start | bytes 12292
  0.0 65.3 %copy-start.13 = (s32[1,128,8]{1,2,0:T(8,128)S(1)}, s32[1,128,8]{1,2,0:T(8,128)}, u32[]{:S(2)}) copy-start(s32[1,128,8]{1,2,0:T(8,128)} %param.17) | copy-start | bytes 12292
  1.8 46.6 %collective-permute-start.11 = (bf16[2048,512]{1,0:T(8,128)(2,1)S(1)}, bf16[2048,512]{1,0:T(8,128)(2,1)S(1)}, u32[]{:S(2)}, u32[]{:S(2)}) collective-permute-start(bf16[2048,512]{1,0:T(8,128)(2,1)S(1)} %constant_dynamic-slice_fusion), channel_id=1, source_target_pairs={{0,20},{1,21},{2,22},{3,23},{4,16},{5,17},{6,18},{7,19},{8,28},{9,... | collective-permute-start | bytes 6291464 | tf_op jit(solution)/shard_map/ppermute | solution.py:166
  48.4 72.9 %collective-permute-start.12 = (bf16[2048,512]{1,0:T(8,128)(2,1)S(1)}, bf16[2048,512]{1,0:T(8,128)(2,1)}, u32[]{:S(2)}, u32[]{:S(2)}) collective-permute-start(bf16[2048,512]{1,0:T(8,128)(2,1)S(1)} %collective-permute-done.11.refs_6_.refs_2_), channel_id=1, source_target_pairs={{0,8},{8,0},{1,9},{9,1},{2,10},{10,2},{3,11},{11,3},{4,12},{12,4},... | collective-permute-start | bytes 6291464 | tf_op jit(solution)/shard_map/ppermute | solution.py:171
  49.9 7.8 %collective-permute-start.6 = (bf16[128,512]{1,0:T(8,128)(2,1)S(1)}, bf16[128,512]{1,0:T(8,128)(2,1)S(1)}, u32[]{:S(2)}, u32[]{:S(2)}) collective-permute-start(bf16[128,512]{1,0:T(8,128)(2,1)S(1)} %pad_maximum_fusion.3.refs_0_.refs_1_), channel_id=1, source_target_pairs={{7,0},{4,1},{5,2},{6,3},{3,4},{0,5},{1,6},{2,7},{15,8},{12,9},{13,... | collective-permute-start | bytes 393224 | tf_op jit(solution)/shard_map/ppermute | solution.py:57
  52.7 8.7 %collective-permute-start.5 = (bf16[128,512]{1,0:T(8,128)(2,1)S(1)}, bf16[128,512]{1,0:T(8,128)(2,1)S(1)}, u32[]{:S(2)}, u32[]{:S(2)}) collective-permute-start(bf16[128,512]{1,0:T(8,128)(2,1)S(1)} %pad_maximum_fusion.3.refs_0_.refs_1_), channel_id=1, source_target_pairs={{6,0},{7,1},{4,2},{5,3},{2,4},{3,5},{0,6},{1,7},{14,8},{15,9},{12,... | collective-permute-start | bytes 393224 | tf_op jit(solution)/shard_map/ppermute | solution.py:57
  54.7 10.5 %collective-permute-start.4 = (bf16[128,512]{1,0:T(8,128)(2,1)S(1)}, bf16[128,512]{1,0:T(8,128)(2,1)S(1)}, u32[]{:S(2)}, u32[]{:S(2)}) collective-permute-start(bf16[128,512]{1,0:T(8,128)(2,1)S(1)} %pad_maximum_fusion.3.refs_0_.refs_1_), channel_id=1, source_target_pairs={{5,0},{6,1},{7,2},{4,3},{1,4},{2,5},{3,6},{0,7},{13,8},{14,9},{15,... | collective-permute-start | bytes 393224 | tf_op jit(solution)/shard_map/ppermute | solution.py:57
  57.0 9.8 %collective-permute-start.3 = (bf16[128,512]{1,0:T(8,128)(2,1)S(1)}, bf16[128,512]{1,0:T(8,128)(2,1)S(1)}, u32[]{:S(2)}, u32[]{:S(2)}) collective-permute-start(bf16[128,512]{1,0:T(8,128)(2,1)S(1)} %pad_maximum_fusion.3.refs_0_.refs_1_), channel_id=1, source_target_pairs={{4,0},{5,1},{6,2},{7,3},{0,4},{1,5},{2,6},{3,7},{12,8},{13,9},{14,... | collective-permute-start | bytes 393224 | tf_op jit(solution)/shard_map/ppermute | solution.py:57
  57.8 9.0 %collective-permute-start.2 = (bf16[128,512]{1,0:T(8,128)(2,1)S(1)}, bf16[128,512]{1,0:T(8,128)(2,1)S(1)}, u32[]{:S(2)}, u32[]{:S(2)}) collective-permute-start(bf16[128,512]{1,0:T(8,128)(2,1)S(1)} %pad_maximum_fusion.3.refs_0_.refs_1_), channel_id=1, source_target_pairs={{3,0},{0,1},{1,2},{2,3},{7,4},{4,5},{5,6},{6,7},{11,8},{8,9},{9,10... | collective-permute-start | bytes 393224 | tf_op jit(solution)/shard_map/ppermute | solution.py:57
  61.4 5.9 %collective-permute-start.1 = (bf16[128,512]{1,0:T(8,128)(2,1)S(1)}, bf16[128,512]{1,0:T(8,128)(2,1)S(1)}, u32[]{:S(2)}, u32[]{:S(2)}) collective-permute-start(bf16[128,512]{1,0:T(8,128)(2,1)S(1)} %pad_maximum_fusion.3.refs_0_.refs_1_), channel_id=1, source_target_pairs={{2,0},{3,1},{0,2},{1,3},{6,4},{7,5},{4,6},{5,7},{10,8},{11,9},{8,1... | collective-permute-start | bytes 393224 | tf_op jit(solution)/shard_map/ppermute | solution.py:57
  65.1 6.1 %collective-permute-start = (bf16[128,512]{1,0:T(8,128)(2,1)S(1)}, bf16[128,512]{1,0:T(8,128)(2,1)S(1)}, u32[]{:S(2)}, u32[]{:S(2)}) collective-permute-start(bf16[128,512]{1,0:T(8,128)(2,1)S(1)} %pad_maximum_fusion.3.refs_0_.refs_1_), channel_id=1, source_target_pairs={{1,0},{2,1},{3,2},{0,3},{5,4},{6,5},{7,6},{4,7},{9,8},{10,9},{11,1... | collective-permute-start | bytes 393224 | tf_op jit(solution)/shard_map/ppermute | solution.py:57
  78.8 11.7 %collective-permute-start.7 = (bf16[128,2048]{1,0:T(8,128)(2,1)}, bf16[128,2048]{1,0:T(8,128)(2,1)}, u32[]{:S(2)}, u32[]{:S(2)}) collective-permute-start(bf16[128,2048]{1,0:T(8,128)(2,1)} %shard_map.109.refs_0_), channel_id=1, source_target_pairs={{0,1},{1,2},{2,3},{3,0},{4,5},{5,6},{6,7},{7,4},{8,9},{9,10},{10,1... | collective-permute-start | bytes 1572872 | tf_op jit(solution)/shard_map/ppermute | solution.py:46
  85.1 12.5 %collective-permute-start.10 = (bf16[128,2048]{1,0:T(8,128)(2,1)}, bf16[128,2048]{1,0:T(8,128)(2,1)}, u32[]{:S(2)}, u32[]{:S(2)}) collective-permute-start(bf16[128,2048]{1,0:T(8,128)(2,1)} %shard_map.110.refs_1_), channel_id=1, source_target_pairs={{0,3},{1,0},{2,1},{3,2},{4,7},{5,4},{6,5},{7,6},{8,11},{9,8},{10,9... | collective-permute-start | bytes 1572872 | tf_op jit(solution)/shard_map/ppermute | solution.py:46
  87.2 21.7 %collective-permute-start.9 = (bf16[128,2048]{1,0:T(8,128)(2,1)}, bf16[128,2048]{1,0:T(8,128)(2,1)}, u32[]{:S(2)}, u32[]{:S(2)}) collective-permute-start(bf16[128,2048]{1,0:T(8,128)(2,1)} %shard_map.109.refs_0_), channel_id=1, source_target_pairs={{0,3},{1,0},{2,1},{3,2},{4,7},{5,4},{6,5},{7,6},{8,11},{9,8},{10,9... | collective-permute-start | bytes 1572872 | tf_op jit(solution)/shard_map/ppermute | solution.py:46
  87.7 21.2 %collective-permute-start.8 = (bf16[128,2048]{1,0:T(8,128)(2,1)}, bf16[128,2048]{1,0:T(8,128)(2,1)}, u32[]{:S(2)}, u32[]{:S(2)}) collective-permute-start(bf16[128,2048]{1,0:T(8,128)(2,1)} %shard_map.110.refs_1_), channel_id=1, source_target_pairs={{0,1},{1,2},{2,3},{3,0},{4,5},{5,6},{6,7},{7,4},{8,9},{9,10},{10,1... | collective-permute-start | bytes 1572872 | tf_op jit(solution)/shard_map/ppermute | solution.py:46
  90.4 24.7 %collective-permute-start.14 = (bf16[128,2048]{1,0:T(8,128)(2,1)}, bf16[128,2048]{1,0:T(8,128)(2,1)S(1)}, u32[]{:S(2)}, u32[]{:S(2)}) collective-permute-start(bf16[128,2048]{1,0:T(8,128)(2,1)} %collective-permute-done.7.refs_2_), channel_id=1, source_target_pairs={{0,1},{1,2},{2,3},{3,0},{4,5},{5,6},{6,7},{7,4},{8,9},{9,10},{10,1... | collective-permute-start | bytes 1572872 | tf_op jit(solution)/shard_map/ppermute | solution.py:46
  97.7 22.4 %collective-permute-start.15 = (bf16[128,2048]{1,0:T(8,128)(2,1)}, bf16[128,2048]{1,0:T(8,128)(2,1)S(1)}, u32[]{:S(2)}, u32[]{:S(2)}) collective-permute-start(bf16[128,2048]{1,0:T(8,128)(2,1)} %collective-permute-done.10.refs_5_), channel_id=1, source_target_pairs={{0,3},{1,0},{2,1},{3,2},{4,7},{5,4},{6,5},{7,6},{8,11},{9,8},{10,9... | collective-permute-start | bytes 1572872 | tf_op jit(solution)/shard_map/ppermute | solution.py:46
  126.4 7.3 %collective-permute-start.17 = (bf16[128,1024]{1,0:T(8,128)(2,1)S(1)}, bf16[128,1024]{1,0:T(8,128)(2,1)S(1)}, u32[]{:S(2)}, u32[]{:S(2)}) collective-permute-start(bf16[128,1024]{1,0:T(8,128)(2,1)S(1)} %get-tuple-element.19), channel_id=1, source_target_pairs={{0,1},{1,2},{2,3},{3,0},{4,5},{5,6},{6,7},{7,4},{8,9},{9,10},{10,1... | collective-permute-start | bytes 786440 | tf_op jit(solution)/shard_map/ppermute | solution.py:46
  128.6 6.6 %collective-permute-start.13 = (bf16[128,1024]{1,0:T(8,128)(2,1)S(1)}, bf16[128,1024]{1,0:T(8,128)(2,1)S(1)}, u32[]{:S(2)}, u32[]{:S(2)}) collective-permute-start(bf16[128,1024]{1,0:T(8,128)(2,1)S(1)} %get-tuple-element.21), channel_id=1, source_target_pairs={{0,3},{1,0},{2,1},{3,2},{4,7},{5,4},{6,5},{7,6},{8,11},{9,8},{10,9... | collective-permute-start | bytes 786440 | tf_op jit(solution)/shard_map/ppermute | solution.py:46
  130.9 9.9 %collective-permute-start.16 = (bf16[128,1024]{1,0:T(8,128)(2,1)S(1)}, bf16[128,1024]{1,0:T(8,128)(2,1)S(1)}, u32[]{:S(2)}, u32[]{:S(2)}) collective-permute-start(bf16[128,1024]{1,0:T(8,128)(2,1)S(1)} %pad_maximum_fusion.2), channel_id=1, source_target_pairs={{0,2},{1,3},{2,0},{3,1},{4,6},{5,7},{6,4},{7,5},{8,10},{9,11},{10,... | collective-permute-start | bytes 786440 | tf_op jit(solution)/shard_map/ppermute | solution.py:46
  149.6 72.2 %all-to-all-start = ((bf16[128,8,2560]{2,1,0:T(8,128)(2,1)}), bf16[128,8,2560]{2,1,0:T(8,128)(2,1)}, u32[]{:S(2)}, u32[]{:S(2)}) async-start(bf16[128,8,2560]{2,1,0:T(8,128)(2,1)} %bitcast.51), calls=%async_computation | async-start | bytes 10485760 | tf_op jit(solution)/shard_map/all_to_all | solution.py:29
  221.8 58.9 %all-to-all-start.2 = ((bf16[128,8,2048]{2,1,0:T(8,128)(2,1)}), bf16[128,8,2048]{2,1,0:T(8,128)(2,1)}, u32[]{:S(2)}, u32[]{:S(2)}) async-start(bf16[128,8,2048]{2,1,0:T(8,128)(2,1)} %convert_bitcast_fusion), calls=%async_computation.2 | async-start | bytes 8388608 | tf_op jit(solution)/shard_map/all_to_all | solution.py:29
  280.7 69.8 %all-to-all-start.1 = ((bf16[128,8,2560]{2,1,0:T(8,128)(2,1)}), bf16[128,8,2560]{2,1,0:T(8,128)(2,1)}, u32[]{:S(2)}, u32[]{:S(2)}) async-start(bf16[128,8,2560]{2,1,0:T(8,128)(2,1)} %bitcast.52), calls=%async_computation.1 | async-start | bytes 10485760 | tf_op jit(solution)/shard_map/all_to_all | solution.py:29
  350.5 58.9 %all-to-all-start.3 = ((bf16[128,8,2048]{2,1,0:T(8,128)(2,1)}), bf16[128,8,2048]{2,1,0:T(8,128)(2,1)}, u32[]{:S(2)}, u32[]{:S(2)}) async-start(bf16[128,8,2048]{2,1,0:T(8,128)(2,1)} %bitcast.54), calls=%async_computation.3 | async-start | bytes 8388608 | tf_op jit(solution)/shard_map/all_to_all | solution.py:29
  (16 other events, 168.4 us)

commit v6 on v5

--- a/solution.py
+++ b/solution.py
@@ -8,6 +8,7 @@
 
 KVH = 2
 DH = 128
+TOP = 8
 EXPERTS = 128
 FULL = 8
 SLOTS = EXPERTS * FULL
@@ -299,20 +300,62 @@
     return pl.BlockSpec(shape, lambda i: (i, 0))
 
 
-def two_terms(weigh):
-    high = weigh.astype(BF)
-    low = (weigh - high.astype(F32)).astype(BF)
-    return jnp.concatenate([high, low], axis=0)
-
-
-def slots_of(routes, slot_gates):
+def prep_kernel(routes_ref, scores_ref, pick_ref, pick_rest_ref, pick_last_ref, split_ref, split_rest_ref, split_last_ref):
+    tok = routes_ref.shape[0]
+    scores = scores_ref[...]
+    gates = scores / jnp.sum(scores, axis=1, keepdims=True)
+    expert = lax.broadcasted_iota(jnp.int32, (tok, EXPERTS), 1)
+    hit = jnp.zeros((tok, EXPERTS), F32)
+    gate = jnp.zeros((tok, EXPERTS), F32)
+    for k in range(TOP):
+        named = routes_ref[:, k : k + 1] == expert
+        hit = hit + jnp.where(named, 1.0, 0.0)
+        gate = gate + jnp.where(named, gates[:, k : k + 1], 0.0)
+    row = lax.broadcasted_iota(jnp.int32, (tok, tok), 0)
+    col = lax.broadcasted_iota(jnp.int32, (tok, tok), 1)
+    earlier = product(jnp.where(col < row, 1.0, 0.0).astype(BF), hit.astype(BF))
+    rank = jnp.where(hit > 0.0, earlier, -1.0)
+
+    placed = jnp.broadcast_to(rank.T[:, None, :], (EXPERTS, 8, tok))
+    order = lax.broadcasted_iota(jnp.int32, (EXPERTS, 8, tok), 1)
+    for start, ref in ((0, pick_ref), (FOUR, pick_rest_ref)):
+        taken = placed == (lax.rem(order, FOUR) + start).astype(F32)
+        for p in range(2):
+            part = jnp.where(taken & (lax.div(order, FOUR) == p), 1.0, 0.0)
+            ref[:, p * tok : (p + 1) * tok] = part.reshape(SLOTS, tok).astype(BF)
+    pick_last_ref[...] = jnp.where(rank.T == float(FULL), 1.0, 0.0).astype(BF)
+
+    lane = lax.broadcasted_iota(jnp.int32, (EXPERTS, SLOTS), 1)
+    own = lax.broadcasted_iota(jnp.int32, (EXPERTS, SLOTS), 0)
+    spread = jnp.where(lax.div(lane, 8) == own, 1.0, 0.0).astype(BF)
+    high = gate.astype(BF)
+    terms = jnp.concatenate([high, (gate - high.astype(F32)).astype(BF)], axis=0)
+    weigh = product(terms, spread)
+    ranks = product(rank.astype(BF), spread)
+    ranks = jnp.concatenate([ranks, ranks], axis=0)
+    order = lax.rem(lax.broadcasted_iota(jnp.int32, (2 * tok, SLOTS), 1), 8)
+    for start, ref in ((0, split_ref), (FOUR, split_rest_ref)):
+        taken = ranks == (lax.rem(order, FOUR) + start).astype(F32)
+        for p in range(2):
+            part = jnp.where(taken & (lax.div(order, FOUR) == p), weigh, 0.0)
+            ref[2 * tok * p : 2 * tok * (p + 1)] = part.astype(BF)
+    last = jnp.concatenate([rank, rank], axis=0) == float(FULL)
+    split_last_ref[...] = jnp.where(last, terms.astype(F32), 0.0).astype(BF)
+
+
+def prep(routes, scores):
     tok = routes.shape[0]
-    named = routes[:, :, None] == jnp.arange(EXPERTS, dtype=jnp.int32)[None, None, :]
-    hit = jnp.any(named, axis=1)
-    gate = jnp.sum(jnp.where(named, slot_gates[:, :, None], 0.0), axis=1)
-    before = jnp.arange(tok)[None, :] < jnp.arange(tok)[:, None]
-    rank = jnp.dot(before.astype(BF), hit.astype(BF), preferred_element_type=F32)
-    return hit, jnp.where(hit, rank, -1.0), gate
+    shapes = [(SLOTS, 2 * tok), (SLOTS, 2 * tok), (EXPERTS, tok), (4 * tok, SLOTS), (4 * tok, SLOTS), (2 * tok, EXPERTS)]
+    vmem = pl.BlockSpec(memory_space=pltpu.VMEM)
+    return pl.pallas_call(
+        prep_kernel,
+        name="prep",
+        in_specs=[vmem] * 2,
+        out_specs=[vmem] * len(shapes),
+        out_shape=[jax.ShapeDtypeStruct(shape, BF) for shape in shapes],
+        compiler_params=pltpu.CompilerParams(vmem_limit_bytes=24 * 1024 * 1024),
+        cost_estimate=pl.CostEstimate(flops=2 * 10**8, bytes_accessed=3 * 10**6, transcendentals=0),
+    )(routes, scores)
 
 
 def layer(
@@ -334,26 +377,7 @@
     first = attend(place, queries[0], gathered, 0)
     second = attend(place, queries[0], gathered, 1)
 
-    score_rows = slot_scores[0]
-    slot_gates = score_rows / jnp.sum(score_rows, axis=1, keepdims=True)
-    _, rank, gate = slots_of(routes[0], slot_gates)
-    order = jnp.arange(8)
-    piece, slot = order // FOUR, (order % FOUR).astype(F32)
-    placed = rank.T[:, None, :]
-
-    def picks(start):
-        taken = placed == (slot + start)[None, :, None]
-        parts = [taken & (piece == p)[None, :, None] for p in range(2)]
-        return jnp.concatenate(parts, axis=2).astype(BF).reshape(SLOTS, 2 * tok)
-
-    def weighs(start):
-        taken = jnp.where(rank[:, :, None] == slot + start, gate[:, :, None], 0.0)
-        parts = [jnp.where(piece == p, taken, 0.0).reshape(tok, SLOTS) for p in range(2)]
-        return jnp.concatenate([two_terms(part) for part in parts], axis=0)
-
-    pick, pick_rest, pick_last = picks(0.0), picks(4.0), (rank.T == float(FULL)).astype(BF)
-    split, split_rest = weighs(0.0), weighs(4.0)
-    split_last = two_terms(jnp.where(rank == float(FULL), gate, 0.0))
+    pick, pick_rest, pick_last, split, split_rest, split_last = prep(routes[0], slot_scores[0])
 
     columns_home = project((first, second), out_weight)
 

time: 420 us -> 417 us (level)
  other arithmetic: 8.11 us -> 1.76 us
  waiting for transfers between devices: 237 us -> 243 us
    ppermute x9, waiting for transfers between devices: 26.9 us -> 32.2 us  [shift(): return lax.ppermute(block, 'y', [(i, (i + step) % 4) for i in range(4)])]
  transfers between devices with their start and end apart: 22 -> 22, of which waited for: 15 -> 16; matrix products, arithmetic and copies ran while one was open for 5% -> 4% of each run, Pallas kernels for 16% -> 15%
where the time goes in v6:
time: 417 us; the launch traced here: 412 us
  waiting for transfers between devices  243 us (58%)
  Pallas kernels  80.4 us (19%)
  starting transfers between devices  67 us (16%)
  matrix products  10.9 us (3%)
  local copies, waits for them, and re-layouts  8.52 us (2%)
    all_to_all x4, waiting for transfers between devices, exchange(): return lax.all_to_all(blocks, axes, split_axis=0, concat_axis=0, tiled=True)  158 us
    ppermute x1, waiting for transfers between devices, project(): fetched = lax.ppermute(mine, ALL, neighbour_pairs())  45.3 us
    pallas_call x2, Pallas kernels, experts(): pl.pallas_call(expert_kernel, grid=(SLOTS // TILE,), in_specs=[tiled((TIL...  44.7 us
    all_to_all x4, starting transfers between devices, exchange(): return lax.all_to_all(blocks, axes, split_axis=0, concat_axis=0, tiled=True)  41.6 us
    ppermute x9, waiting for transfers between devices, shift(): return lax.ppermute(block, 'y', [(i, (i + step) % 4) for i in range(4)])  32.2 us
    ppermute x7, starting transfers between devices, gather_pair(): blocks.append(lax.ppermute(pair, CTX, pairs))  13.2 us
    pallas_call x2, Pallas kernels, attend(): pl.pallas_call(attend_kernel, grid_spec=pltpu.PrefetchScalarGridSpec(num_...  11.4 us
    dot_general x3, matrix products, product(): return jnp.dot(left, right, preferred_element_type=F32)  10.9 us
  transfers between devices with their start and end apart: 22, of which 16 were waited for; matrix products, arithmetic and copies ran while one was open for 4% of the time, Pallas kernels for 15%

profile of v6, /device:TPU:91, one launch (start us, length us, event | category | flops | bytes accessed | tf_op | source)
XLA Modules:
  0.0 412.3 jit_solution(7882313895715518237)
XLA Ops:
  3.1 45.3 %collective-permute-done.11.refs_6_.refs_2_ = bf16[2048,512]{1,0:T(8,128)(2,1)S(1)} collective-permute-done((bf16[2048,512]{1,0:T(8,128)(2,1)S(1)}, bf16[2048,512]{1,0:T(8,128)(2,1)S(1)}, u32[]{:S(2)}, u32[]{:S(2)}) %collective-permute-start.11) | collective-permute-done | bytes 2097184 | tf_op jit(solution)/shard_map/ppermute | solution.py:167
  61.4 3.0 collective-permute-start.1
  67.2 4.0 collective-permute-done.refs_2_.refs_3_
  72.4 5.7 %shard_map.109.refs_0_ = bf16[128,2048]{1,0:T(8,128)(2,1)S(1)} custom-call(s32[3]{0:T(128)S(1)} %pad_add_fusion.place_ref, bf16[128,4096]{1,0:T(8,128)(2,1)S(1)} %bitcast.36, bf16[128,512]{1,0:T(8,128)(2,1)S(1)} %pad_maximum_fusion.2.refs_0_.refs_1_, bf16[128,512]{1,0:T(8,128)(2,1)S(1)} %pad_maximum_fusion.2.refs_0_.refs_1_, ...), custom_call_target="tpu_custom_call" | custom-call | flops 1073741824 | bytes 1048576 | tf_op jit(solution)/shard_map/pallas_call | solution.py:101
  78.2 5.7 %shard_map.110.refs_1_ = bf16[128,2048]{1,0:T(8,128)(2,1)S(1)} custom-call(s32[3]{0:T(128)S(1)} %pad_add_fusion.place_ref, bf16[128,4096]{1,0:T(8,128)(2,1)S(1)} %bitcast.37, bf16[128,512]{1,0:T(8,128)(2,1)S(1)} %pad_maximum_fusion.2.refs_0_.refs_1_, bf16[128,512]{1,0:T(8,128)(2,1)S(1)} %pad_maximum_fusion.2.refs_0_.refs_1_, ...), custom_call_target="tpu_custom_call" | custom-call | flops 1073741824 | bytes 1048576 | tf_op jit(solution)/shard_map/pallas_call | solution.py:101
  90.7 5.5 %collective-permute-done.10.refs_5_ = bf16[128,2048]{1,0:T(8,128)(2,1)S(1)} collective-permute-done((bf16[128,2048]{1,0:T(8,128)(2,1)S(1)}, bf16[128,2048]{1,0:T(8,128)(2,1)S(1)}, u32[]{:S(2)}, u32[]{:S(2)}) %collective-permute-start.10) | collective-permute-done | bytes 524320 | tf_op jit(solution)/shard_map/ppermute | solution.py:47
  96.2 11.2 %collective-permute-done.9.refs_4_ = bf16[128,2048]{1,0:T(8,128)(2,1)S(1)} collective-permute-done((bf16[128,2048]{1,0:T(8,128)(2,1)S(1)}, bf16[128,2048]{1,0:T(8,128)(2,1)S(1)}, u32[]{:S(2)}, u32[]{:S(2)}) %collective-permute-start.9) | collective-permute-done | bytes 524320 | tf_op jit(solution)/shard_map/ppermute | solution.py:47
  111.7 7.0 %collective-permute-done.15.refs_1_ = bf16[128,2048]{1,0:T(8,128)(2,1)S(1)} collective-permute-done((bf16[128,2048]{1,0:T(8,128)(2,1)S(1)}, bf16[128,2048]{1,0:T(8,128)(2,1)S(1)}, u32[]{:S(2)}, u32[]{:S(2)}) %collective-permute-start.15) | collective-permute-done | bytes 524320 | tf_op jit(solution)/shard_map/ppermute | solution.py:47
  120.0 3.3 shard_map.112
  133.1 5.5 %collective-permute-done.16.far_ref = bf16[128,1024]{1,0:T(8,128)(2,1)} collective-permute-done((bf16[128,1024]{1,0:T(8,128)(2,1)S(1)}, bf16[128,1024]{1,0:T(8,128)(2,1)}, u32[]{:S(2)}, u32[]{:S(2)}) %collective-permute-start.16) | collective-permute-done | bytes 262176 | tf_op jit(solution)/shard_map/ppermute | solution.py:47
  138.6 8.1 %make.1 = (bf16[1024,2560]{1,0:T(8,128)(2,1)}, bf16[256,2048]{1,0:T(8,128)(2,1)}, f32[128,4096]{1,0:T(8,128)}) custom-call(s32[3]{0:T(128)} %copy-done.1, bf16[128,1024]{1,0:T(8,128)(2,1)} %get-tuple-element.26.here_ref, bf16[128,1024]{1,0:T(8,128)(2,1)} %collective-permute-done.13.above_ref, bf16[128,1024]{1,0:T(8,128)(2,1)} %collective-permute-done.16.far_ref, ...), custom_call_target="tpu_custom_call" | custom-call | flops 1073741824 | bytes 5242880 | tf_op jit(solution)/shard_map/make/pallas_call | solution.py:391
  146.6 11.9 %all-to-all-start = ((bf16[128,8,2560]{2,1,0:T(8,128)(2,1)}), bf16[128,8,2560]{2,1,0:T(8,128)(2,1)}, u32[]{:S(2)}, u32[]{:S(2)}) async-start(bf16[128,8,2560]{2,1,0:T(8,128)(2,1)} %bitcast.38), calls=%async_computation | async-start | bytes 10485760 | tf_op jit(solution)/shard_map/all_to_all | solution.py:30
  158.5 4.5 %convert_bitcast_fusion = bf16[128,8,2048]{2,1,0:T(8,128)(2,1)} fusion(bf16[1024,256]{1,0:T(8,128)(2,1)S(1)} %get-tuple-element.21, bf16[256,2048]{1,0:T(8,128)(2,1)} %get-tuple-element.22), kind=kOutput, calls=%fused_computation.2 | convolution fusion | flops 1075838976 | bytes 5767168 | tf_op jit(solution)/shard_map/dot_general | solution.py:189
  163.0 55.9 %all-to-all-done = bf16[128,8,2560]{2,1,0:T(8,128)(2,1)} async-done(((bf16[128,8,2560]{2,1,0:T(8,128)(2,1)}), bf16[128,8,2560]{2,1,0:T(8,128)(2,1)}, u32[]{:S(2)}, u32[]{:S(2)}) %all-to-all-start) | async-done | bytes 5242912 | tf_op jit(solution)/shard_map/all_to_all | solution.py:30
  218.9 10.1 %all-to-all-start.2 = ((bf16[128,8,2048]{2,1,0:T(8,128)(2,1)}), bf16[128,8,2048]{2,1,0:T(8,128)(2,1)}, u32[]{:S(2)}, u32[]{:S(2)}) async-start(bf16[128,8,2048]{2,1,0:T(8,128)(2,1)} %convert_bitcast_fusion), calls=%async_computation.2 | async-start | bytes 8388608 | tf_op jit(solution)/shard_map/all_to_all | solution.py:30
  229.0 24.0 %shard_map.115 = bf16[1024,2560]{1,0:T(8,128)(2,1)} custom-call(bf16[1024,2560]{1,0:T(8,128)(2,1)} %bitcast.12.got_ref, bf16[4096,768]{1,0:T(8,128)(2,1)} %bitcast.44, bf16[4096,768]{1,0:T(8,128)(2,1)} %bitcast.46, bf16[768,4096]{1,0:T(8,128)(2,1)} %bitcast.48), custom_call_target="tpu_custom_call" | custom-call | flops 12079595520 | bytes 29360128 | tf_op jit(solution)/shard_map/pallas_call | solution.py:271
  253.0 24.8 %all-to-all-done.2 = bf16[128,8,2048]{2,1,0:T(8,128)(2,1)} async-done(((bf16[128,8,2048]{2,1,0:T(8,128)(2,1)}), bf16[128,8,2048]{2,1,0:T(8,128)(2,1)}, u32[]{:S(2)}, u32[]{:S(2)}) %all-to-all-start.2) | async-done | bytes 4194336 | tf_op jit(solution)/shard_map/all_to_all | solution.py:30
  277.8 9.4 %all-to-all-start.1 = ((bf16[128,8,2560]{2,1,0:T(8,128)(2,1)}), bf16[128,8,2560]{2,1,0:T(8,128)(2,1)}, u32[]{:S(2)}, u32[]{:S(2)}) async-start(bf16[128,8,2560]{2,1,0:T(8,128)(2,1)} %bitcast.39), calls=%async_computation.1 | async-start | bytes 10485760 | tf_op jit(solution)/shard_map/all_to_all | solution.py:30
  287.2 20.7 %shard_map.116 = bf16[1024,2048]{1,0:T(8,128)(2,1)} custom-call(bf16[1024,2048]{1,0:T(8,128)(2,1)} %bitcast.22.got_ref, bf16[4096,768]{1,0:T(8,128)(2,1)} %bitcast.45, bf16[4096,768]{1,0:T(8,128)(2,1)} %bitcast.47, bf16[768,4096]{1,0:T(8,128)(2,1)} %bitcast.49), custom_call_target="tpu_custom_call" | custom-call | flops 9663676416 | bytes 27262976 | tf_op jit(solution)/shard_map/pallas_call | solution.py:271
  307.9 39.7 %all-to-all-done.1 = bf16[128,8,2560]{2,1,0:T(8,128)(2,1)} async-done(((bf16[128,8,2560]{2,1,0:T(8,128)(2,1)}), bf16[128,8,2560]{2,1,0:T(8,128)(2,1)}, u32[]{:S(2)}, u32[]{:S(2)}) %all-to-all-start.1) | async-done | bytes 5242912 | tf_op jit(solution)/shard_map/all_to_all | solution.py:30
  347.6 10.1 %all-to-all-start.3 = ((bf16[128,8,2048]{2,1,0:T(8,128)(2,1)}), bf16[128,8,2048]{2,1,0:T(8,128)(2,1)}, u32[]{:S(2)}, u32[]{:S(2)}) async-start(bf16[128,8,2048]{2,1,0:T(8,128)(2,1)} %bitcast.41), calls=%async_computation.3 | async-start | bytes 8388608 | tf_op jit(solution)/shard_map/all_to_all | solution.py:30
  362.2 4.5 %fusion = f32[512,2048]{1,0:T(8,128)S(1)} fusion(bf16[512,1024]{1,0:T(8,128)(2,1)S(1)} %get-tuple-element.19, bf16[1024,2560]{1,0:T(8,128)(2,1)} %bitcast.17), kind=kOutput, calls=%fused_computation | convolution fusion | flops 2147483648 | bytes 9437184 | tf_op jit(solution)/shard_map/dot_general | solution.py:189
  368.9 37.6 %all-to-all-done.3 = bf16[128,8,2048]{2,1,0:T(8,128)(2,1)} async-done(((bf16[128,8,2048]{2,1,0:T(8,128)(2,1)}), bf16[128,8,2048]{2,1,0:T(8,128)(2,1)}, u32[]{:S(2)}, u32[]{:S(2)}) %all-to-all-start.3) | async-done | bytes 4194336 | tf_op jit(solution)/shard_map/all_to_all | solution.py:30
  406.5 5.8 %finish.1 = bf16[128,4096]{1,0:T(8,128)(2,1)} custom-call(f32[128,4096]{1,0:T(8,128)S(1)} %fusion.3.low_ref.high_ref, f32[128,4096]{1,0:T(8,128)S(1)} %fusion.3.low_ref.high_ref, bf16[512,1024]{1,0:T(8,128)(2,1)S(1)} %get-tuple-element.20.split_ref, bf16[1024,2048]{1,0:T(8,128)(2,1)} %bitcast.24.back_ref), custom_call_target="tpu_custom_call" | custom-call | flops 2147483648 | bytes 7340032 | tf_op jit(solution)/shard_map/finish/pallas_call | solution.py:428
  (65 shorter events, 48.9 us)
Async XLA Ops:
  0.0 49.9 %copy-start.6 = (bf16[1,128,256]{2,1,0:T(8,128)(2,1)S(1)}, bf16[1,128,256]{2,1,0:T(8,128)(2,1)}, u32[]{:S(2)}) copy-start(bf16[1,128,256]{2,1,0:T(8,128)(2,1)} %param.14) | copy-start | bytes 196612
  0.0 49.9 %copy-start.7 = (bf16[1,128,256]{2,1,0:T(8,128)(2,1)S(1)}, bf16[1,128,256]{2,1,0:T(8,128)(2,1)}, u32[]{:S(2)}) copy-start(bf16[1,128,256]{2,1,0:T(8,128)(2,1)} %param.13) | copy-start | bytes 196612
  1.8 46.6 %collective-permute-start.11 = (bf16[2048,512]{1,0:T(8,128)(2,1)S(1)}, bf16[2048,512]{1,0:T(8,128)(2,1)S(1)}, u32[]{:S(2)}, u32[]{:S(2)}) collective-permute-start(bf16[2048,512]{1,0:T(8,128)(2,1)S(1)} %constant_dynamic-slice_fusion), channel_id=1, source_target_pairs={{0,20},{1,21},{2,22},{3,23},{4,16},{5,17},{6,18},{7,19},{8,28},{9,... | collective-permute-start | bytes 6291464 | tf_op jit(solution)/shard_map/ppermute | solution.py:167
  48.4 71.6 %collective-permute-start.12 = (bf16[2048,512]{1,0:T(8,128)(2,1)S(1)}, bf16[2048,512]{1,0:T(8,128)(2,1)}, u32[]{:S(2)}, u32[]{:S(2)}) collective-permute-start(bf16[2048,512]{1,0:T(8,128)(2,1)S(1)} %collective-permute-done.11.refs_6_.refs_2_), channel_id=1, source_target_pairs={{0,8},{8,0},{1,9},{9,1},{2,10},{10,2},{3,11},{11,3},{4,12},{12,4},... | collective-permute-start | bytes 6291464 | tf_op jit(solution)/shard_map/ppermute | solution.py:172
  49.9 7.8 %collective-permute-start.6 = (bf16[128,512]{1,0:T(8,128)(2,1)S(1)}, bf16[128,512]{1,0:T(8,128)(2,1)S(1)}, u32[]{:S(2)}, u32[]{:S(2)}) collective-permute-start(bf16[128,512]{1,0:T(8,128)(2,1)S(1)} %pad_maximum_fusion.2.refs_0_.refs_1_), channel_id=1, source_target_pairs={{7,0},{4,1},{5,2},{6,3},{3,4},{0,5},{1,6},{2,7},{15,8},{12,9},{13,... | collective-permute-start | bytes 393224 | tf_op jit(solution)/shard_map/ppermute | solution.py:58
  52.7 8.7 %collective-permute-start.5 = (bf16[128,512]{1,0:T(8,128)(2,1)S(1)}, bf16[128,512]{1,0:T(8,128)(2,1)S(1)}, u32[]{:S(2)}, u32[]{:S(2)}) collective-permute-start(bf16[128,512]{1,0:T(8,128)(2,1)S(1)} %pad_maximum_fusion.2.refs_0_.refs_1_), channel_id=1, source_target_pairs={{6,0},{7,1},{4,2},{5,3},{2,4},{3,5},{0,6},{1,7},{14,8},{15,9},{12,... | collective-permute-start | bytes 393224 | tf_op jit(solution)/shard_map/ppermute | solution.py:58
  54.6 10.5 %collective-permute-start.4 = (bf16[128,512]{1,0:T(8,128)(2,1)S(1)}, bf16[128,512]{1,0:T(8,128)(2,1)S(1)}, u32[]{:S(2)}, u32[]{:S(2)}) collective-permute-start(bf16[128,512]{1,0:T(8,128)(2,1)S(1)} %pad_maximum_fusion.2.refs_0_.refs_1_), channel_id=1, source_target_pairs={{5,0},{6,1},{7,2},{4,3},{1,4},{2,5},{3,6},{0,7},{13,8},{14,9},{15,... | collective-permute-start | bytes 393224 | tf_op jit(solution)/shard_map/ppermute | solution.py:58
  57.0 9.8 %collective-permute-start.3 = (bf16[128,512]{1,0:T(8,128)(2,1)S(1)}, bf16[128,512]{1,0:T(8,128)(2,1)S(1)}, u32[]{:S(2)}, u32[]{:S(2)}) collective-permute-start(bf16[128,512]{1,0:T(8,128)(2,1)S(1)} %pad_maximum_fusion.2.refs_0_.refs_1_), channel_id=1, source_target_pairs={{4,0},{5,1},{6,2},{7,3},{0,4},{1,5},{2,6},{3,7},{12,8},{13,9},{14,... | collective-permute-start | bytes 393224 | tf_op jit(solution)/shard_map/ppermute | solution.py:58
  57.7 9.1 %collective-permute-start.2 = (bf16[128,512]{1,0:T(8,128)(2,1)S(1)}, bf16[128,512]{1,0:T(8,128)(2,1)S(1)}, u32[]{:S(2)}, u32[]{:S(2)}) collective-permute-start(bf16[128,512]{1,0:T(8,128)(2,1)S(1)} %pad_maximum_fusion.2.refs_0_.refs_1_), channel_id=1, source_target_pairs={{3,0},{0,1},{1,2},{2,3},{7,4},{4,5},{5,6},{6,7},{11,8},{8,9},{9,10... | collective-permute-start | bytes 393224 | tf_op jit(solution)/shard_map/ppermute | solution.py:58
  61.4 5.9 %collective-permute-start.1 = (bf16[128,512]{1,0:T(8,128)(2,1)S(1)}, bf16[128,512]{1,0:T(8,128)(2,1)S(1)}, u32[]{:S(2)}, u32[]{:S(2)}) collective-permute-start(bf16[128,512]{1,0:T(8,128)(2,1)S(1)} %pad_maximum_fusion.2.refs_0_.refs_1_), channel_id=1, source_target_pairs={{2,0},{3,1},{0,2},{1,3},{6,4},{7,5},{4,6},{5,7},{10,8},{11,9},{8,1... | collective-permute-start | bytes 393224 | tf_op jit(solution)/shard_map/ppermute | solution.py:58
  65.1 6.1 %collective-permute-start = (bf16[128,512]{1,0:T(8,128)(2,1)S(1)}, bf16[128,512]{1,0:T(8,128)(2,1)S(1)}, u32[]{:S(2)}, u32[]{:S(2)}) collective-permute-start(bf16[128,512]{1,0:T(8,128)(2,1)S(1)} %pad_maximum_fusion.2.refs_0_.refs_1_), channel_id=1, source_target_pairs={{1,0},{2,1},{3,2},{0,3},{5,4},{6,5},{7,6},{4,7},{9,8},{10,9},{11,1... | collective-permute-start | bytes 393224 | tf_op jit(solution)/shard_map/ppermute | solution.py:58
  78.1 11.1 %collective-permute-start.7 = (bf16[128,2048]{1,0:T(8,128)(2,1)S(1)}, bf16[128,2048]{1,0:T(8,128)(2,1)S(1)}, u32[]{:S(2)}, u32[]{:S(2)}) collective-permute-start(bf16[128,2048]{1,0:T(8,128)(2,1)S(1)} %shard_map.109.refs_0_), channel_id=1, source_target_pairs={{0,1},{1,2},{2,3},{3,0},{4,5},{5,6},{6,7},{7,4},{8,9},{9,10},{10,1... | collective-permute-start | bytes 1572872 | tf_op jit(solution)/shard_map/ppermute | solution.py:47
  83.9 12.3 %collective-permute-start.10 = (bf16[128,2048]{1,0:T(8,128)(2,1)S(1)}, bf16[128,2048]{1,0:T(8,128)(2,1)S(1)}, u32[]{:S(2)}, u32[]{:S(2)}) collective-permute-start(bf16[128,2048]{1,0:T(8,128)(2,1)S(1)} %shard_map.110.refs_1_), channel_id=1, source_target_pairs={{0,3},{1,0},{2,1},{3,2},{4,7},{5,4},{6,5},{7,6},{8,11},{9,8},{10,9... | collective-permute-start | bytes 1572872 | tf_op jit(solution)/shard_map/ppermute | solution.py:47
  85.4 22.0 %collective-permute-start.9 = (bf16[128,2048]{1,0:T(8,128)(2,1)S(1)}, bf16[128,2048]{1,0:T(8,128)(2,1)S(1)}, u32[]{:S(2)}, u32[]{:S(2)}) collective-permute-start(bf16[128,2048]{1,0:T(8,128)(2,1)S(1)} %shard_map.109.refs_0_), channel_id=1, source_target_pairs={{0,3},{1,0},{2,1},{3,2},{4,7},{5,4},{6,5},{7,6},{8,11},{9,8},{10,9... | collective-permute-start | bytes 1572872 | tf_op jit(solution)/shard_map/ppermute | solution.py:47
  85.9 21.6 %collective-permute-start.8 = (bf16[128,2048]{1,0:T(8,128)(2,1)S(1)}, bf16[128,2048]{1,0:T(8,128)(2,1)S(1)}, u32[]{:S(2)}, u32[]{:S(2)}) collective-permute-start(bf16[128,2048]{1,0:T(8,128)(2,1)S(1)} %shard_map.110.refs_1_), channel_id=1, source_target_pairs={{0,1},{1,2},{2,3},{3,0},{4,5},{5,6},{6,7},{7,4},{8,9},{9,10},{10,1... | collective-permute-start | bytes 1572872 | tf_op jit(solution)/shard_map/ppermute | solution.py:47
  89.2 22.5 %collective-permute-start.14 = (bf16[128,2048]{1,0:T(8,128)(2,1)S(1)}, bf16[128,2048]{1,0:T(8,128)(2,1)S(1)}, u32[]{:S(2)}, u32[]{:S(2)}) collective-permute-start(bf16[128,2048]{1,0:T(8,128)(2,1)S(1)} %collective-permute-done.7.refs_2_), channel_id=1, source_target_pairs={{0,1},{1,2},{2,3},{3,0},{4,5},{5,6},{6,7},{7,4},{8,9},{9,10},{10,1... | collective-permute-start | bytes 1572872 | tf_op jit(solution)/shard_map/ppermute | solution.py:47
  96.2 22.5 %collective-permute-start.15 = (bf16[128,2048]{1,0:T(8,128)(2,1)S(1)}, bf16[128,2048]{1,0:T(8,128)(2,1)S(1)}, u32[]{:S(2)}, u32[]{:S(2)}) collective-permute-start(bf16[128,2048]{1,0:T(8,128)(2,1)S(1)} %collective-permute-done.10.refs_5_), channel_id=1, source_target_pairs={{0,3},{1,0},{2,1},{3,2},{4,7},{5,4},{6,5},{7,6},{8,11},{9,8},{10,9... | collective-permute-start | bytes 1572872 | tf_op jit(solution)/shard_map/ppermute | solution.py:47
  124.2 8.8 %collective-permute-start.17 = (bf16[128,1024]{1,0:T(8,128)(2,1)}, bf16[128,1024]{1,0:T(8,128)(2,1)}, u32[]{:S(2)}, u32[]{:S(2)}) collective-permute-start(bf16[128,1024]{1,0:T(8,128)(2,1)} %get-tuple-element.25), channel_id=1, source_target_pairs={{0,1},{1,2},{2,3},{3,0},{4,5},{5,6},{6,7},{7,4},{8,9},{9,10},{10,1... | collective-permute-start | bytes 786440 | tf_op jit(solution)/shard_map/ppermute | solution.py:47
  126.4 6.7 %collective-permute-start.13 = (bf16[128,1024]{1,0:T(8,128)(2,1)S(1)}, bf16[128,1024]{1,0:T(8,128)(2,1)}, u32[]{:S(2)}, u32[]{:S(2)}) collective-permute-start(bf16[128,1024]{1,0:T(8,128)(2,1)S(1)} %get-tuple-element.27), channel_id=1, source_target_pairs={{0,3},{1,0},{2,1},{3,2},{4,7},{5,4},{6,5},{7,6},{8,11},{9,8},{10,9... | collective-permute-start | bytes 786440 | tf_op jit(solution)/shard_map/ppermute | solution.py:47
  128.7 9.8 %collective-permute-start.16 = (bf16[128,1024]{1,0:T(8,128)(2,1)S(1)}, bf16[128,1024]{1,0:T(8,128)(2,1)}, u32[]{:S(2)}, u32[]{:S(2)}) collective-permute-start(bf16[128,1024]{1,0:T(8,128)(2,1)S(1)} %pad_maximum_fusion.1), channel_id=1, source_target_pairs={{0,2},{1,3},{2,0},{3,1},{4,6},{5,7},{6,4},{7,5},{8,10},{9,11},{10,... | collective-permute-start | bytes 786440 | tf_op jit(solution)/shard_map/ppermute | solution.py:47
  146.6 72.2 %all-to-all-start = ((bf16[128,8,2560]{2,1,0:T(8,128)(2,1)}), bf16[128,8,2560]{2,1,0:T(8,128)(2,1)}, u32[]{:S(2)}, u32[]{:S(2)}) async-start(bf16[128,8,2560]{2,1,0:T(8,128)(2,1)} %bitcast.38), calls=%async_computation | async-start | bytes 10485760 | tf_op jit(solution)/shard_map/all_to_all | solution.py:30
  218.9 58.9 %all-to-all-start.2 = ((bf16[128,8,2048]{2,1,0:T(8,128)(2,1)}), bf16[128,8,2048]{2,1,0:T(8,128)(2,1)}, u32[]{:S(2)}, u32[]{:S(2)}) async-start(bf16[128,8,2048]{2,1,0:T(8,128)(2,1)} %convert_bitcast_fusion), calls=%async_computation.2 | async-start | bytes 8388608 | tf_op jit(solution)/shard_map/all_to_all | solution.py:30
  277.8 69.8 %all-to-all-start.1 = ((bf16[128,8,2560]{2,1,0:T(8,128)(2,1)}), bf16[128,8,2560]{2,1,0:T(8,128)(2,1)}, u32[]{:S(2)}, u32[]{:S(2)}) async-start(bf16[128,8,2560]{2,1,0:T(8,128)(2,1)} %bitcast.39), calls=%async_computation.1 | async-start | bytes 10485760 | tf_op jit(solution)/shard_map/all_to_all | solution.py:30
  347.6 58.9 %all-to-all-start.3 = ((bf16[128,8,2048]{2,1,0:T(8,128)(2,1)}), bf16[128,8,2048]{2,1,0:T(8,128)(2,1)}, u32[]{:S(2)}, u32[]{:S(2)}) async-start(bf16[128,8,2048]{2,1,0:T(8,128)(2,1)} %bitcast.41), calls=%async_computation.3 | async-start | bytes 8388608 | tf_op jit(solution)/shard_map/all_to_all | solution.py:30
  (8 other events, 104.8 us)

commit v7 on v6

--- a/solution.py
+++ b/solution.py
@@ -1,3 +1,5 @@
+import functools
+
 import jax
 import jax.numpy as jnp
 from jax import lax
@@ -18,6 +20,7 @@
 HALF = WIDTH // 2
 FIRST = HALF + PACK
 TILE = 512
+COLUMNS = 256
 
 DP = ("z", "xl", "core")
 CTX = ("xh", "y")
@@ -117,46 +120,56 @@
     )(place, queries, *[block for block in blocks for _ in range(2)])
 
 
-def own_kernel(*refs):
-    *row_refs, weight_ref, out_ref = refs
-    half = row_refs[0].shape[1]
-    left = jnp.concatenate([ref[...] for ref in row_refs[0::2]], axis=0)
-    right = jnp.concatenate([ref[...] for ref in row_refs[1::2]], axis=0)
-    out = product(left, weight_ref[:half]) + product(right, weight_ref[half:])
-    out_ref[...] = out.astype(BF)
-
-
-def pair_kernel(core_ref, *refs):
-    *row_refs, fetched_ref, other_ref, out_ref = refs
-    left = jnp.concatenate([ref[...] for ref in row_refs[0::2]], axis=0)
-    right = jnp.concatenate([ref[...] for ref in row_refs[1::2]], axis=0)
+def own_columns(left, right, weight_ref):
+    half = left.shape[1]
+    return product(left, weight_ref[:half]) + product(right, weight_ref[half:])
+
+
+def pair_columns(left, right, core_ref, fetched_ref, other_ref):
     swap = core_ref[0] == 1
     out = product(jnp.where(swap, right, left), fetched_ref[...])
-    out = out + product(jnp.where(swap, left, right), other_ref[...])
-    out_ref[...] = out.astype(BF)
-
-
-def columns(rows, weight, core=None):
+    return out + product(jnp.where(swap, left, right), other_ref[...])
+
+
+def near_kernel(core_ref, *refs, count, paired):
+    left = jnp.concatenate([ref[...] for ref in refs[0 : 2 * count : 2]], axis=0)
+    right = jnp.concatenate([ref[...] for ref in refs[1 : 2 * count : 2]], axis=0)
+    if paired:
+        out = pair_columns(left, right, core_ref, *refs[2 * count : 2 * count + 2])
+    else:
+        out = own_columns(left, right, refs[2 * count])
+    tok = refs[0].shape[0]
+    for i, ref in enumerate(refs[-count:]):
+        ref[...] = out[i * tok : (i + 1) * tok].astype(BF)
+
+
+def far_kernel(core_ref, left_ref, right_ref, weight_ref, fetched_ref, other_ref, out_ref):
+    left, right = left_ref[...], right_ref[...]
+    step, wide = pl.program_id(0), weight_ref.shape[1]
+    own = own_columns(left, right, weight_ref)
+    pair = pair_columns(left, right, core_ref, fetched_ref, other_ref)
+    for base, out in ((0, own), (PACK, pair)):
+        out_ref[:, pl.ds(pl.multiple_of(base + step * wide, wide), wide)] = out.astype(BF)
+
+
+def columns(body, core, rows, weight, out_specs, out_shape):
     flat = [part for pair in rows for part in pair]
     tok, half = flat[0].shape
     wide = weight[0].shape[1]
     count = len(rows) * tok
-    body = own_kernel if core is None else pair_kernel
-    scalars = [] if core is None else [core]
-    block = 256
     return pl.pallas_call(
         body,
-        grid=(wide // block,),
-        in_specs=[pl.BlockSpec(memory_space=pltpu.SMEM)] * len(scalars)
+        grid=(wide // COLUMNS,),
+        in_specs=[pl.BlockSpec(memory_space=pltpu.SMEM)]
         + [whole((tok, half))] * len(flat)
-        + [pl.BlockSpec((w.shape[0], block), lambda i: (0, i)) for w in weight],
-        out_specs=pl.BlockSpec((count, block), lambda i: (0, i)),
-        out_shape=jax.ShapeDtypeStruct((count, wide), BF),
+        + [pl.BlockSpec((w.shape[0], COLUMNS), lambda i: (0, i)) for w in weight],
+        out_specs=out_specs,
+        out_shape=out_shape,
         compiler_params=pltpu.CompilerParams(vmem_limit_bytes=24 * 1024 * 1024),
         cost_estimate=pl.CostEstimate(
             flops=4 * count * half * wide, bytes_accessed=4 * half * wide + 4 * count * half, transcendentals=0
         ),
-    )(*scalars, *flat, *weight)
+    )(core, *flat, *weight)
 
 
 def project(attended, out_weight):
@@ -171,18 +184,21 @@
     far_b = shift(above_b, -1)
     other = lax.ppermute(fetched, "core", [(0, 1), (1, 0)])
     near = [(first, second), (below_a, below_b), (above_a, above_b)]
-    far = [(far_a, far_b)]
     which = core.reshape(1)
-    weight = out_weight
-    near_own = columns(near, [weight])
-    near_pair = columns(near, [fetched, other], which)
-    near = jnp.concatenate([near_own, near_pair], axis=1)
-    from_above = shift(near[tok : 2 * tok], -1)
-    from_below = shift(near[2 * tok :], 1)
-    far_own = columns(far, [weight])
-    far_pair = columns(far, [fetched, other], which)
-    from_far = shift(jnp.concatenate([far_own, far_pair], axis=1), 2)
-    return [near[:tok], from_above, from_far, from_below]
+    specs = [pl.BlockSpec((tok, COLUMNS), lambda i: (0, i))] * 3
+    shapes = [jax.ShapeDtypeStruct((tok, PACK), BF)] * 3
+    own_body = functools.partial(near_kernel, count=3, paired=False)
+    pair_body = functools.partial(near_kernel, count=3, paired=True)
+    own = columns(own_body, which, near, [out_weight], specs, shapes)
+    above_own, below_own = shift(own[1], -1), shift(own[2], 1)
+    pair = columns(pair_body, which, near, [fetched, other], specs, shapes)
+    far = columns(
+        far_kernel, which, [(far_a, far_b)], [out_weight, fetched, other],
+        whole((tok, 2 * PACK)), jax.ShapeDtypeStruct((tok, 2 * PACK), BF),
+    )
+    from_far = shift(far, 2)
+    above_pair, below_pair = shift(pair[1], -1), shift(pair[2], 1)
+    return [own[0], pair[0], above_own, above_pair, from_far, below_own, below_pair]
 
 
 def product(left, right):
@@ -208,20 +224,21 @@
 
 
 def make_kernel(
-    place_ref, here_ref, above_ref, far_ref, below_ref, hidden_ref, gain_ref, pick_ref, last_ref,
+    place_ref, here_own, here_pair, above_own, above_pair, far_ref, below_own, below_pair,
+    hidden_ref, gain_ref, pick_ref, last_ref,
     out_ref, halves_ref, residual_ref, normed, last_rows,
 ):
     step = pl.program_id(0)
 
     @pl.when(step == 0)
     def _():
-        for ahead, ref in enumerate((here_ref, above_ref, far_ref, below_ref)):
+        far_parts = far_ref.at[:, :PACK], far_ref.at[:, PACK:]
+        parts = (here_own, here_pair), (above_own, above_pair), far_parts, (below_own, below_pair)
+        for ahead, refs in enumerate(parts):
             y = lax.rem(place_ref[2] + ahead, 4)
-            for part in range(2):
-                high = place_ref[1] if part == 0 else 1 - place_ref[1]
+            for high, ref in zip((place_ref[1], 1 - place_ref[1]), refs, strict=True):
                 at = pl.ds(pl.multiple_of((high * 4 + y) * PACK, PACK), PACK)
-                projected = ref[:, part * PACK : (part + 1) * PACK].astype(F32)
-                residual_ref[:, at] = hidden_ref[:, at].astype(F32) + projected
+                residual_ref[:, at] = hidden_ref[:, at].astype(F32) + ref[...].astype(F32)
         residual = residual_ref[...]
         mean = jnp.mean(residual * residual, axis=1, keepdims=True)
         normed[...] = (residual * lax.rsqrt(mean + 1e-06) * gain_ref[...]).astype(BF)
@@ -287,9 +304,9 @@
     tok, wide = low_ref.shape
     sums = product(split_ref[...], back_ref[...])
     for piece, ref in enumerate((low_ref, high_ref)):
-        part = sums[2 * tok * piece : 2 * tok * (piece + 1)]
+        part = sums[tok * piece : tok * (piece + 1)]
         at = pl.ds(pl.multiple_of(piece * HALF + step * wide, wide), wide)
-        out_ref[:, at] = (ref[...] + (part[:tok] + part[tok:])).astype(BF)
+        out_ref[:, at] = (ref[...] + part).astype(BF)
 
 
 def whole(shape, index=(0, 0)):
@@ -328,24 +345,20 @@
     lane = lax.broadcasted_iota(jnp.int32, (EXPERTS, SLOTS), 1)
     own = lax.broadcasted_iota(jnp.int32, (EXPERTS, SLOTS), 0)
     spread = jnp.where(lax.div(lane, 8) == own, 1.0, 0.0).astype(BF)
-    high = gate.astype(BF)
-    terms = jnp.concatenate([high, (gate - high.astype(F32)).astype(BF)], axis=0)
-    weigh = product(terms, spread)
+    weigh = product(gate.astype(BF), spread)
     ranks = product(rank.astype(BF), spread)
-    ranks = jnp.concatenate([ranks, ranks], axis=0)
-    order = lax.rem(lax.broadcasted_iota(jnp.int32, (2 * tok, SLOTS), 1), 8)
+    order = lax.rem(lax.broadcasted_iota(jnp.int32, (tok, SLOTS), 1), 8)
     for start, ref in ((0, split_ref), (FOUR, split_rest_ref)):
         taken = ranks == (lax.rem(order, FOUR) + start).astype(F32)
         for p in range(2):
             part = jnp.where(taken & (lax.div(order, FOUR) == p), weigh, 0.0)
-            ref[2 * tok * p : 2 * tok * (p + 1)] = part.astype(BF)
-    last = jnp.concatenate([rank, rank], axis=0) == float(FULL)
-    split_last_ref[...] = jnp.where(last, terms.astype(F32), 0.0).astype(BF)
+            ref[tok * p : tok * (p + 1)] = part.astype(BF)
+    split_last_ref[...] = jnp.where(rank == float(FULL), gate, 0.0).astype(BF)
 
 
 def prep(routes, scores):
     tok = routes.shape[0]
-    shapes = [(SLOTS, 2 * tok), (SLOTS, 2 * tok), (EXPERTS, tok), (4 * tok, SLOTS), (4 * tok, SLOTS), (2 * tok, EXPERTS)]
+    shapes = [(SLOTS, 2 * tok), (SLOTS, 2 * tok), (EXPERTS, tok), (2 * tok, SLOTS), (2 * tok, SLOTS), (tok, EXPERTS)]
     vmem = pl.BlockSpec(memory_space=pltpu.VMEM)
     return pl.pallas_call(
         prep_kernel,
@@ -394,7 +407,7 @@
         grid_spec=pltpu.PrefetchScalarGridSpec(
             num_scalar_prefetch=1,
             grid=(SLOTS // 256,),
-            in_specs=[pl.BlockSpec((tok, 2 * PACK), lambda i, p: (0, 0))] * 4
+            in_specs=[pl.BlockSpec(part.shape, lambda i, p: (0, 0)) for part in columns_home]
             + [
                 pl.BlockSpec((tok, WIDTH), lambda i, p: (0, 0)),
                 pl.BlockSpec((1, WIDTH), lambda i, p: (0, 0)),
@@ -409,7 +422,7 @@
             scratch_shapes=[pltpu.VMEM((tok, WIDTH), BF), pltpu.VMEM((EXPERTS, WIDTH), BF)],
         ),
         out_shape=[shape((SLOTS, FIRST), BF), shape((2 * tok, HALF), BF), shape((tok, WIDTH), F32)],
-        compiler_params=pltpu.CompilerParams(vmem_limit_bytes=57 * 1024 * 1024),
+        compiler_params=pltpu.CompilerParams(vmem_limit_bytes=50 * 1024 * 1024),
         cost_estimate=pl.CostEstimate(
             flops=4 * SLOTS * tok * HALF, bytes_accessed=SLOTS * FIRST * 2, transcendentals=0
         ),
@@ -420,10 +433,8 @@
     back_rest = swap(experts(got_rest, *weights))
 
     sums = product(split, back[:, :HALF])
-    sums = sums.reshape(2, 2, tok, HALF)
-    nines = product(split_last, back[:, HALF:].reshape(EXPERTS, WIDTH))
-    base = residual + (nines[:tok] + nines[tok:])
-    base = base + jnp.concatenate([sums[0, 0] + sums[0, 1], sums[1, 0] + sums[1, 1]], axis=1)
+    base = residual + product(split_last, back[:, HALF:].reshape(EXPERTS, WIDTH))
+    base = base + jnp.concatenate([sums[:tok], sums[tok:]], axis=1)
     steps = HALF // PACK
     out = pl.pallas_call(
         finish_kernel,
@@ -432,14 +443,14 @@
         in_specs=[
             pl.BlockSpec((tok, PACK), lambda i: (0, i)),
             pl.BlockSpec((tok, PACK), lambda i: (0, i + steps)),
-            whole((4 * tok, SLOTS)),
+            whole((2 * tok, SLOTS)),
             pl.BlockSpec((SLOTS, PACK), lambda i: (0, i)),
         ],
         out_specs=whole((tok, WIDTH)),
         out_shape=shape((tok, WIDTH), BF),
         compiler_params=pltpu.CompilerParams(vmem_limit_bytes=24 * 1024 * 1024),
         cost_estimate=pl.CostEstimate(
-            flops=8 * tok * SLOTS * HALF, bytes_accessed=SLOTS * HALF * 2 + tok * WIDTH * 6, transcendentals=0
+            flops=4 * tok * SLOTS * HALF, bytes_accessed=SLOTS * HALF * 2 + tok * WIDTH * 6, transcendentals=0
         ),
     )(base, base, split_rest, back_rest)
     return out[None]

time: 417 us -> 415 us (level)
  starting transfers between devices: 67 us -> 71.4 us
    ppermute x9 -> x11, waiting for transfers between devices: 32.2 us -> 26.4 us  [shift(): return lax.ppermute(block, 'y', [(i, (i + step) % 4) for i in range(4)])]
    ppermute x9 -> x11, starting transfers between devices: 9.42 us -> 12.6 us  [shift(): return lax.ppermute(block, 'y', [(i, (i + step) % 4) for i in range(4)])]
    pallas_call x4 -> x3, Pallas kernels: 9.19 us -> 9.78 us  [columns(): pl.pallas_call(body, grid=(wide // COLUMNS,), in_specs=[pl.BlockSpec(memo...]
  transfers between devices with their start and end apart: 22 -> 24, of which waited for: 16 -> 15; matrix products, arithmetic and copies ran while one was open for 4% -> 3% of each run, Pallas kernels for 15% -> 16%
where the time goes in v7:
time: 415 us; the launch traced here: 410 us
  waiting for transfers between devices  242 us (58%)
  Pallas kernels  77.7 us (19%)
  starting transfers between devices  71.4 us (17%)
  local copies, waits for them, and re-layouts  11.5 us (3%)
  matrix products  7.31 us (2%)
    all_to_all x4, waiting for transfers between devices, exchange(): return lax.all_to_all(blocks, axes, split_axis=0, concat_axis=0, tiled=True)  162 us
    ppermute x1, waiting for transfers between devices, project(): fetched = lax.ppermute(mine, ALL, neighbour_pairs())  45.3 us
    pallas_call x2, Pallas kernels, experts(): pl.pallas_call(expert_kernel, grid=(SLOTS // TILE,), in_specs=[tiled((TIL...  44.7 us
    all_to_all x4, starting transfers between devices, exchange(): return lax.all_to_all(blocks, axes, split_axis=0, concat_axis=0, tiled=True)  42.8 us
    ppermute x11, waiting for transfers between devices, shift(): return lax.ppermute(block, 'y', [(i, (i + step) % 4) for i in range(4)])  26.4 us
    ppermute x7, starting transfers between devices, gather_pair(): blocks.append(lax.ppermute(pair, CTX, pairs))  13.2 us
    ppermute x11, starting transfers between devices, shift(): return lax.ppermute(block, 'y', [(i, (i + step) % 4) for i in range(4)])  12.6 us
    pallas_call x2, Pallas kernels, attend(): pl.pallas_call(attend_kernel, grid_spec=pltpu.PrefetchScalarGridSpec(num_...  11.4 us
  transfers between devices with their start and end apart: 24, of which 15 were waited for; matrix products, arithmetic and copies ran while one was open for 3% of the time, Pallas kernels for 16%

profile of v7, /device:TPU:91, one launch (start us, length us, event | category | flops | bytes accessed | tf_op | source)
XLA Modules:
  0.0 410.2 jit_solution(16723920062452831307)
XLA Ops:
  3.1 45.3 %collective-permute-done.11.refs_6_.fetched_ref = bf16[2048,512]{1,0:T(8,128)(2,1)S(1)} collective-permute-done((bf16[2048,512]{1,0:T(8,128)(2,1)S(1)}, bf16[2048,512]{1,0:T(8,128)(2,1)S(1)}, u32[]{:S(2)}, u32[]{:S(2)}) %collective-permute-start.11) | collective-permute-done | bytes 2097184 | tf_op jit(solution)/shard_map/ppermute | solution.py:180
  61.4 3.0 collective-permute-start.1
  67.2 4.0 collective-permute-done.refs_2_.refs_3_
  72.4 5.7 %shard_map.109.refs_0_ = bf16[128,2048]{1,0:T(8,128)(2,1)S(1)} custom-call(s32[3]{0:T(128)S(1)} %pad_add_fusion.place_ref, bf16[128,4096]{1,0:T(8,128)(2,1)S(1)} %bitcast.31, bf16[128,512]{1,0:T(8,128)(2,1)S(1)} %pad_maximum_fusion.refs_0_.refs_1_, bf16[128,512]{1,0:T(8,128)(2,1)S(1)} %pad_maximum_fusion.refs_0_.refs_1_, ...), custom_call_target="tpu_custom_call" | custom-call | flops 1073741824 | bytes 1048576 | tf_op jit(solution)/shard_map/pallas_call | solution.py:104
  78.2 5.7 %shard_map.110.refs_1_ = bf16[128,2048]{1,0:T(8,128)(2,1)S(1)} custom-call(s32[3]{0:T(128)S(1)} %pad_add_fusion.place_ref, bf16[128,4096]{1,0:T(8,128)(2,1)S(1)} %bitcast.32, bf16[128,512]{1,0:T(8,128)(2,1)S(1)} %pad_maximum_fusion.refs_0_.refs_1_, bf16[128,512]{1,0:T(8,128)(2,1)S(1)} %pad_maximum_fusion.refs_0_.refs_1_, ...), custom_call_target="tpu_custom_call" | custom-call | flops 1073741824 | bytes 1048576 | tf_op jit(solution)/shard_map/pallas_call | solution.py:104
  90.7 5.5 %collective-permute-done.10.refs_5_ = bf16[128,2048]{1,0:T(8,128)(2,1)S(1)} collective-permute-done((bf16[128,2048]{1,0:T(8,128)(2,1)S(1)}, bf16[128,2048]{1,0:T(8,128)(2,1)S(1)}, u32[]{:S(2)}, u32[]{:S(2)}) %collective-permute-start.10) | collective-permute-done | bytes 524320 | tf_op jit(solution)/shard_map/ppermute | solution.py:50
  96.2 11.2 %collective-permute-done.9.refs_4_ = bf16[128,2048]{1,0:T(8,128)(2,1)S(1)} collective-permute-done((bf16[128,2048]{1,0:T(8,128)(2,1)S(1)}, bf16[128,2048]{1,0:T(8,128)(2,1)S(1)}, u32[]{:S(2)}, u32[]{:S(2)}) %collective-permute-start.9) | collective-permute-done | bytes 524320 | tf_op jit(solution)/shard_map/ppermute | solution.py:50
  107.4 2.9 shard_map.111
  113.1 5.6 %collective-permute-done.16.right_ref = bf16[128,2048]{1,0:T(8,128)(2,1)S(1)} collective-permute-done((bf16[128,2048]{1,0:T(8,128)(2,1)S(1)}, bf16[128,2048]{1,0:T(8,128)(2,1)S(1)}, u32[]{:S(2)}, u32[]{:S(2)}) %collective-permute-start.16) | collective-permute-done | bytes 524320 | tf_op jit(solution)/shard_map/ppermute | solution.py:50
  123.1 4.0 shard_map.112
  138.2 5.9 %make.1 = (bf16[1024,2560]{1,0:T(8,128)(2,1)}, bf16[256,2048]{1,0:T(8,128)(2,1)S(1)}, f32[128,4096]{1,0:T(8,128)}) custom-call(s32[3]{0:T(128)S(1)} %pad_add_fusion.place_ref, bf16[128,512]{1,0:T(8,128)(2,1)S(1)} %get-tuple-element.20.here_own, bf16[128,512]{1,0:T(8,128)(2,1)S(1)} %copy-done.4, bf16[128,512]{1,0:T(8,128)(2,1)S(1)} %collective-permute-done.13.above_own, ...), custom_call_target="tpu_custom_call" | custom-call | flops 1073741824 | bytes 5242880 | tf_op jit(solution)/shard_map/make/pallas_call | solution.py:404
  144.1 13.1 %all-to-all-start = ((bf16[128,8,2560]{2,1,0:T(8,128)(2,1)}), bf16[128,8,2560]{2,1,0:T(8,128)(2,1)}, u32[]{:S(2)}, u32[]{:S(2)}) async-start(bf16[128,8,2560]{2,1,0:T(8,128)(2,1)} %bitcast.35), calls=%async_computation | async-start | bytes 10485760 | tf_op jit(solution)/shard_map/all_to_all | solution.py:33
  157.2 3.3 convert_bitcast_fusion
  160.5 57.0 %all-to-all-done = bf16[128,8,2560]{2,1,0:T(8,128)(2,1)} async-done(((bf16[128,8,2560]{2,1,0:T(8,128)(2,1)}), bf16[128,8,2560]{2,1,0:T(8,128)(2,1)}, u32[]{:S(2)}, u32[]{:S(2)}) %all-to-all-start) | async-done | bytes 5242912 | tf_op jit(solution)/shard_map/all_to_all | solution.py:33
  217.6 10.1 %all-to-all-start.2 = ((bf16[128,8,2048]{2,1,0:T(8,128)(2,1)}), bf16[128,8,2048]{2,1,0:T(8,128)(2,1)}, u32[]{:S(2)}, u32[]{:S(2)}) async-start(bf16[128,8,2048]{2,1,0:T(8,128)(2,1)} %convert_bitcast_fusion), calls=%async_computation.2 | async-start | bytes 8388608 | tf_op jit(solution)/shard_map/all_to_all | solution.py:33
  227.7 24.1 %shard_map.114 = bf16[1024,2560]{1,0:T(8,128)(2,1)} custom-call(bf16[1024,2560]{1,0:T(8,128)(2,1)} %bitcast.12.got_ref, bf16[4096,768]{1,0:T(8,128)(2,1)} %bitcast.40, bf16[4096,768]{1,0:T(8,128)(2,1)} %bitcast.42, bf16[768,4096]{1,0:T(8,128)(2,1)} %bitcast.44), custom_call_target="tpu_custom_call" | custom-call | flops 12079595520 | bytes 29360128 | tf_op jit(solution)/shard_map/pallas_call | solution.py:288
  251.8 24.7 %all-to-all-done.2 = bf16[128,8,2048]{2,1,0:T(8,128)(2,1)} async-done(((bf16[128,8,2048]{2,1,0:T(8,128)(2,1)}), bf16[128,8,2048]{2,1,0:T(8,128)(2,1)}, u32[]{:S(2)}, u32[]{:S(2)}) %all-to-all-start.2) | async-done | bytes 4194336 | tf_op jit(solution)/shard_map/all_to_all | solution.py:33
  276.5 9.4 %all-to-all-start.1 = ((bf16[128,8,2560]{2,1,0:T(8,128)(2,1)}), bf16[128,8,2560]{2,1,0:T(8,128)(2,1)}, u32[]{:S(2)}, u32[]{:S(2)}) async-start(bf16[128,8,2560]{2,1,0:T(8,128)(2,1)} %bitcast.36), calls=%async_computation.1 | async-start | bytes 10485760 | tf_op jit(solution)/shard_map/all_to_all | solution.py:33
  285.9 20.6 %shard_map.115 = bf16[1024,2048]{1,0:T(8,128)(2,1)} custom-call(bf16[1024,2048]{1,0:T(8,128)(2,1)} %bitcast.19.got_ref, bf16[4096,768]{1,0:T(8,128)(2,1)} %bitcast.41, bf16[4096,768]{1,0:T(8,128)(2,1)} %bitcast.43, bf16[768,4096]{1,0:T(8,128)(2,1)} %bitcast.45), custom_call_target="tpu_custom_call" | custom-call | flops 9663676416 | bytes 27262976 | tf_op jit(solution)/shard_map/pallas_call | solution.py:288
  306.5 39.7 %all-to-all-done.1 = bf16[128,8,2560]{2,1,0:T(8,128)(2,1)} async-done(((bf16[128,8,2560]{2,1,0:T(8,128)(2,1)}), bf16[128,8,2560]{2,1,0:T(8,128)(2,1)}, u32[]{:S(2)}, u32[]{:S(2)}) %all-to-all-start.1) | async-done | bytes 5242912 | tf_op jit(solution)/shard_map/all_to_all | solution.py:33
  346.3 10.1 %all-to-all-start.3 = ((bf16[128,8,2048]{2,1,0:T(8,128)(2,1)}), bf16[128,8,2048]{2,1,0:T(8,128)(2,1)}, u32[]{:S(2)}, u32[]{:S(2)}) async-start(bf16[128,8,2048]{2,1,0:T(8,128)(2,1)} %bitcast.37), calls=%async_computation.3 | async-start | bytes 8388608 | tf_op jit(solution)/shard_map/all_to_all | solution.py:33
  360.8 3.6 fusion
  364.8 40.4 %all-to-all-done.3 = bf16[128,8,2048]{2,1,0:T(8,128)(2,1)} async-done(((bf16[128,8,2048]{2,1,0:T(8,128)(2,1)}), bf16[128,8,2048]{2,1,0:T(8,128)(2,1)}, u32[]{:S(2)}, u32[]{:S(2)}) %all-to-all-start.3) | async-done | bytes 4194336 | tf_op jit(solution)/shard_map/all_to_all | solution.py:33
  405.2 4.9 %finish.1 = bf16[128,4096]{1,0:T(8,128)(2,1)} custom-call(f32[128,4096]{1,0:T(8,128)S(1)} %maximum_add_fusion.low_ref.high_ref, f32[128,4096]{1,0:T(8,128)S(1)} %maximum_add_fusion.low_ref.high_ref, bf16[256,1024]{1,0:T(8,128)(2,1)S(1)} %get-tuple-element.32.split_ref, bf16[1024,2048]{1,0:T(8,128)(2,1)} %bitcast.21.back_ref), custom_call_target="tpu_custom_call" | custom-call | flops 1073741824 | bytes 7340032 | tf_op jit(solution)/shard_map/finish/pallas_call | solution.py:439
  (72 shorter events, 50.0 us)
Async XLA Ops:
  1.8 46.6 %collective-permute-start.11 = (bf16[2048,512]{1,0:T(8,128)(2,1)S(1)}, bf16[2048,512]{1,0:T(8,128)(2,1)S(1)}, u32[]{:S(2)}, u32[]{:S(2)}) collective-permute-start(bf16[2048,512]{1,0:T(8,128)(2,1)S(1)} %constant_dynamic-slice_fusion), channel_id=1, source_target_pairs={{0,20},{1,21},{2,22},{3,23},{4,16},{5,17},{6,18},{7,19},{8,28},{9,... | collective-permute-start | bytes 6291464 | tf_op jit(solution)/shard_map/ppermute | solution.py:180
  48.4 70.3 %collective-permute-start.12 = (bf16[2048,512]{1,0:T(8,128)(2,1)S(1)}, bf16[2048,512]{1,0:T(8,128)(2,1)}, u32[]{:S(2)}, u32[]{:S(2)}) collective-permute-start(bf16[2048,512]{1,0:T(8,128)(2,1)S(1)} %collective-permute-done.11.refs_6_.fetched_ref), channel_id=1, source_target_pairs={{0,8},{8,0},{1,9},{9,1},{2,10},{10,2},{3,11},{11,3},{4,12},{12,4},... | collective-permute-start | bytes 6291464 | tf_op jit(solution)/shard_map/ppermute | solution.py:185
  49.9 7.8 %collective-permute-start.6 = (bf16[128,512]{1,0:T(8,128)(2,1)S(1)}, bf16[128,512]{1,0:T(8,128)(2,1)S(1)}, u32[]{:S(2)}, u32[]{:S(2)}) collective-permute-start(bf16[128,512]{1,0:T(8,128)(2,1)S(1)} %pad_maximum_fusion.refs_0_.refs_1_), channel_id=1, source_target_pairs={{7,0},{4,1},{5,2},{6,3},{3,4},{0,5},{1,6},{2,7},{15,8},{12,9},{13,... | collective-permute-start | bytes 393224 | tf_op jit(solution)/shard_map/ppermute | solution.py:61
  52.7 8.7 %collective-permute-start.5 = (bf16[128,512]{1,0:T(8,128)(2,1)S(1)}, bf16[128,512]{1,0:T(8,128)(2,1)S(1)}, u32[]{:S(2)}, u32[]{:S(2)}) collective-permute-start(bf16[128,512]{1,0:T(8,128)(2,1)S(1)} %pad_maximum_fusion.refs_0_.refs_1_), channel_id=1, source_target_pairs={{6,0},{7,1},{4,2},{5,3},{2,4},{3,5},{0,6},{1,7},{14,8},{15,9},{12,... | collective-permute-start | bytes 393224 | tf_op jit(solution)/shard_map/ppermute | solution.py:61
  54.6 10.5 %collective-permute-start.4 = (bf16[128,512]{1,0:T(8,128)(2,1)S(1)}, bf16[128,512]{1,0:T(8,128)(2,1)S(1)}, u32[]{:S(2)}, u32[]{:S(2)}) collective-permute-start(bf16[128,512]{1,0:T(8,128)(2,1)S(1)} %pad_maximum_fusion.refs_0_.refs_1_), channel_id=1, source_target_pairs={{5,0},{6,1},{7,2},{4,3},{1,4},{2,5},{3,6},{0,7},{13,8},{14,9},{15,... | collective-permute-start | bytes 393224 | tf_op jit(solution)/shard_map/ppermute | solution.py:61
  57.0 9.8 %collective-permute-start.3 = (bf16[128,512]{1,0:T(8,128)(2,1)S(1)}, bf16[128,512]{1,0:T(8,128)(2,1)S(1)}, u32[]{:S(2)}, u32[]{:S(2)}) collective-permute-start(bf16[128,512]{1,0:T(8,128)(2,1)S(1)} %pad_maximum_fusion.refs_0_.refs_1_), channel_id=1, source_target_pairs={{4,0},{5,1},{6,2},{7,3},{0,4},{1,5},{2,6},{3,7},{12,8},{13,9},{14,... | collective-permute-start | bytes 393224 | tf_op jit(solution)/shard_map/ppermute | solution.py:61
  57.7 9.1 %collective-permute-start.2 = (bf16[128,512]{1,0:T(8,128)(2,1)S(1)}, bf16[128,512]{1,0:T(8,128)(2,1)S(1)}, u32[]{:S(2)}, u32[]{:S(2)}) collective-permute-start(bf16[128,512]{1,0:T(8,128)(2,1)S(1)} %pad_maximum_fusion.refs_0_.refs_1_), channel_id=1, source_target_pairs={{3,0},{0,1},{1,2},{2,3},{7,4},{4,5},{5,6},{6,7},{11,8},{8,9},{9,10... | collective-permute-start | bytes 393224 | tf_op jit(solution)/shard_map/ppermute | solution.py:61
  61.4 5.9 %collective-permute-start.1 = (bf16[128,512]{1,0:T(8,128)(2,1)S(1)}, bf16[128,512]{1,0:T(8,128)(2,1)S(1)}, u32[]{:S(2)}, u32[]{:S(2)}) collective-permute-start(bf16[128,512]{1,0:T(8,128)(2,1)S(1)} %pad_maximum_fusion.refs_0_.refs_1_), channel_id=1, source_target_pairs={{2,0},{3,1},{0,2},{1,3},{6,4},{7,5},{4,6},{5,7},{10,8},{11,9},{8,1... | collective-permute-start | bytes 393224 | tf_op jit(solution)/shard_map/ppermute | solution.py:61
  65.1 6.1 %collective-permute-start = (bf16[128,512]{1,0:T(8,128)(2,1)S(1)}, bf16[128,512]{1,0:T(8,128)(2,1)S(1)}, u32[]{:S(2)}, u32[]{:S(2)}) collective-permute-start(bf16[128,512]{1,0:T(8,128)(2,1)S(1)} %pad_maximum_fusion.refs_0_.refs_1_), channel_id=1, source_target_pairs={{1,0},{2,1},{3,2},{0,3},{5,4},{6,5},{7,6},{4,7},{9,8},{10,9},{11,1... | collective-permute-start | bytes 393224 | tf_op jit(solution)/shard_map/ppermute | solution.py:61
  78.1 11.1 %collective-permute-start.7 = (bf16[128,2048]{1,0:T(8,128)(2,1)S(1)}, bf16[128,2048]{1,0:T(8,128)(2,1)S(1)}, u32[]{:S(2)}, u32[]{:S(2)}) collective-permute-start(bf16[128,2048]{1,0:T(8,128)(2,1)S(1)} %shard_map.109.refs_0_), channel_id=1, source_target_pairs={{0,1},{1,2},{2,3},{3,0},{4,5},{5,6},{6,7},{7,4},{8,9},{9,10},{10,1... | collective-permute-start | bytes 1572872 | tf_op jit(solution)/shard_map/ppermute | solution.py:50
  83.9 12.3 %collective-permute-start.10 = (bf16[128,2048]{1,0:T(8,128)(2,1)S(1)}, bf16[128,2048]{1,0:T(8,128)(2,1)S(1)}, u32[]{:S(2)}, u32[]{:S(2)}) collective-permute-start(bf16[128,2048]{1,0:T(8,128)(2,1)S(1)} %shard_map.110.refs_1_), channel_id=1, source_target_pairs={{0,3},{1,0},{2,1},{3,2},{4,7},{5,4},{6,5},{7,6},{8,11},{9,8},{10,9... | collective-permute-start | bytes 1572872 | tf_op jit(solution)/shard_map/ppermute | solution.py:50
  85.4 22.0 %collective-permute-start.9 = (bf16[128,2048]{1,0:T(8,128)(2,1)S(1)}, bf16[128,2048]{1,0:T(8,128)(2,1)S(1)}, u32[]{:S(2)}, u32[]{:S(2)}) collective-permute-start(bf16[128,2048]{1,0:T(8,128)(2,1)S(1)} %shard_map.109.refs_0_), channel_id=1, source_target_pairs={{0,3},{1,0},{2,1},{3,2},{4,7},{5,4},{6,5},{7,6},{8,11},{9,8},{10,9... | collective-permute-start | bytes 1572872 | tf_op jit(solution)/shard_map/ppermute | solution.py:50
  85.9 21.6 %collective-permute-start.8 = (bf16[128,2048]{1,0:T(8,128)(2,1)S(1)}, bf16[128,2048]{1,0:T(8,128)(2,1)S(1)}, u32[]{:S(2)}, u32[]{:S(2)}) collective-permute-start(bf16[128,2048]{1,0:T(8,128)(2,1)S(1)} %shard_map.110.refs_1_), channel_id=1, source_target_pairs={{0,1},{1,2},{2,3},{3,0},{4,5},{5,6},{6,7},{7,4},{8,9},{9,10},{10,1... | collective-permute-start | bytes 1572872 | tf_op jit(solution)/shard_map/ppermute | solution.py:50
  89.2 23.8 %collective-permute-start.15 = (bf16[128,2048]{1,0:T(8,128)(2,1)S(1)}, bf16[128,2048]{1,0:T(8,128)(2,1)S(1)}, u32[]{:S(2)}, u32[]{:S(2)}) collective-permute-start(bf16[128,2048]{1,0:T(8,128)(2,1)S(1)} %collective-permute-done.7.refs_2_), channel_id=1, source_target_pairs={{0,1},{1,2},{2,3},{3,0},{4,5},{5,6},{6,7},{7,4},{8,9},{9,10},{10,1... | collective-permute-start | bytes 1572872 | tf_op jit(solution)/shard_map/ppermute | solution.py:50
  96.2 22.5 %collective-permute-start.16 = (bf16[128,2048]{1,0:T(8,128)(2,1)S(1)}, bf16[128,2048]{1,0:T(8,128)(2,1)S(1)}, u32[]{:S(2)}, u32[]{:S(2)}) collective-permute-start(bf16[128,2048]{1,0:T(8,128)(2,1)S(1)} %collective-permute-done.10.refs_5_), channel_id=1, source_target_pairs={{0,3},{1,0},{2,1},{3,2},{4,7},{5,4},{6,5},{7,6},{8,11},{9,8},{10,9... | collective-permute-start | bytes 1572872 | tf_op jit(solution)/shard_map/ppermute | solution.py:50
  110.4 22.1 %collective-permute-start.13 = (bf16[128,512]{1,0:T(8,128)(2,1)}, bf16[128,512]{1,0:T(8,128)(2,1)S(1)}, u32[]{:S(2)}, u32[]{:S(2)}) collective-permute-start(bf16[128,512]{1,0:T(8,128)(2,1)} %get-tuple-element.22), channel_id=1, source_target_pairs={{0,3},{1,0},{2,1},{3,2},{4,7},{5,4},{6,5},{7,6},{8,11},{9,8},{10,9... | collective-permute-start | bytes 393224 | tf_op jit(solution)/shard_map/ppermute | solution.py:50
  110.4 22.1 %collective-permute-start.18 = (bf16[128,512]{1,0:T(8,128)(2,1)}, bf16[128,512]{1,0:T(8,128)(2,1)S(1)}, u32[]{:S(2)}, u32[]{:S(2)}) collective-permute-start(bf16[128,512]{1,0:T(8,128)(2,1)} %get-tuple-element.24), channel_id=1, source_target_pairs={{0,1},{1,2},{2,3},{3,0},{4,5},{5,6},{6,7},{7,4},{8,9},{9,10},{10,1... | collective-permute-start | bytes 393224 | tf_op jit(solution)/shard_map/ppermute | solution.py:50
  121.6 13.7 %collective-permute-start.17 = (bf16[128,1024]{1,0:T(8,128)(2,1)S(1)}, bf16[128,1024]{1,0:T(8,128)(2,1)S(1)}, u32[]{:S(2)}, u32[]{:S(2)}) collective-permute-start(bf16[128,1024]{1,0:T(8,128)(2,1)S(1)} %shard_map.113), channel_id=1, source_target_pairs={{0,2},{1,3},{2,0},{3,1},{4,6},{5,7},{6,4},{7,5},{8,10},{9,11},{10,... | collective-permute-start | bytes 786440 | tf_op jit(solution)/shard_map/ppermute | solution.py:50
  127.7 7.6 %collective-permute-start.14 = (bf16[128,512]{1,0:T(8,128)(2,1)}, bf16[128,512]{1,0:T(8,128)(2,1)S(1)}, u32[]{:S(2)}, u32[]{:S(2)}) collective-permute-start(bf16[128,512]{1,0:T(8,128)(2,1)} %get-tuple-element.23), channel_id=1, source_target_pairs={{0,3},{1,0},{2,1},{3,2},{4,7},{5,4},{6,5},{7,6},{8,11},{9,8},{10,9... | collective-permute-start | bytes 393224 | tf_op jit(solution)/shard_map/ppermute | solution.py:50
  129.1 6.3 %collective-permute-start.19 = (bf16[128,512]{1,0:T(8,128)(2,1)}, bf16[128,512]{1,0:T(8,128)(2,1)S(1)}, u32[]{:S(2)}, u32[]{:S(2)}) collective-permute-start(bf16[128,512]{1,0:T(8,128)(2,1)} %get-tuple-element.25), channel_id=1, source_target_pairs={{0,1},{1,2},{2,3},{3,0},{4,5},{5,6},{6,7},{7,4},{8,9},{9,10},{10,1... | collective-permute-start | bytes 393224 | tf_op jit(solution)/shard_map/ppermute | solution.py:50
  144.1 73.4 %all-to-all-start = ((bf16[128,8,2560]{2,1,0:T(8,128)(2,1)}), bf16[128,8,2560]{2,1,0:T(8,128)(2,1)}, u32[]{:S(2)}, u32[]{:S(2)}) async-start(bf16[128,8,2560]{2,1,0:T(8,128)(2,1)} %bitcast.35), calls=%async_computation | async-start | bytes 10485760 | tf_op jit(solution)/shard_map/all_to_all | solution.py:33
  217.6 58.9 %all-to-all-start.2 = ((bf16[128,8,2048]{2,1,0:T(8,128)(2,1)}), bf16[128,8,2048]{2,1,0:T(8,128)(2,1)}, u32[]{:S(2)}, u32[]{:S(2)}) async-start(bf16[128,8,2048]{2,1,0:T(8,128)(2,1)} %convert_bitcast_fusion), calls=%async_computation.2 | async-start | bytes 8388608 | tf_op jit(solution)/shard_map/all_to_all | solution.py:33
  276.5 69.8 %all-to-all-start.1 = ((bf16[128,8,2560]{2,1,0:T(8,128)(2,1)}), bf16[128,8,2560]{2,1,0:T(8,128)(2,1)}, u32[]{:S(2)}, u32[]{:S(2)}) async-start(bf16[128,8,2560]{2,1,0:T(8,128)(2,1)} %bitcast.36), calls=%async_computation.1 | async-start | bytes 10485760 | tf_op jit(solution)/shard_map/all_to_all | solution.py:33
  346.3 58.9 %all-to-all-start.3 = ((bf16[128,8,2048]{2,1,0:T(8,128)(2,1)}), bf16[128,8,2048]{2,1,0:T(8,128)(2,1)}, u32[]{:S(2)}, u32[]{:S(2)}) async-start(bf16[128,8,2048]{2,1,0:T(8,128)(2,1)} %bitcast.37), calls=%async_computation.3 | async-start | bytes 8388608 | tf_op jit(solution)/shard_map/all_to_all | solution.py:33
  (13 other events, 173.4 us)

commit v8 on v7

--- a/solution.py
+++ b/solution.py
@@ -8,6 +8,7 @@
 from jax.sharding import Mesh, PartitionSpec as P
 
 
+HQ = 32
 KVH = 2
 DH = 128
 TOP = 8
@@ -62,14 +63,14 @@
     return blocks
 
 
-def attend_kernel(place_ref, query_ref, *refs):
+def attend_kernel(place_ref, query_ref, *refs, whose):
     *block_refs, out_ref, bias, flipped, held = refs
     tok = query_ref.shape[0]
     heads = query_ref.shape[1] // DH
 
     @pl.when(pl.program_id(0) == 0)
     def _():
-        query_pos = place_ref[0] * tok + lax.broadcasted_iota(jnp.int32, (tok, tok), 0)
+        query_pos = place_ref[whose] * tok + lax.broadcasted_iota(jnp.int32, (tok, tok), 0)
         for ahead in range(8):
             high = place_ref[1] if ahead < 4 else 1 - place_ref[1]
             source = high * 4 + lax.rem(place_ref[2] + ahead, 4)
@@ -91,10 +92,11 @@
             out_ref[:, at] = out[i * tok : (i + 1) * tok]
 
 
-def attend(place, queries, blocks, head):
+def attend(place, queries, blocks, head, whose=0):
     tok = queries.shape[0]
     keys = len(blocks) * tok
-    half = queries.shape[1] // KVH
+    half = HQ * DH // KVH
+    first = head * (queries.shape[1] // half - 1)
     block = 4 * DH
     steps = half // block
     specs = [
@@ -102,11 +104,11 @@
         pl.BlockSpec((tok, DH), lambda i, p: (0, KVH + head)),
     ]
     return pl.pallas_call(
-        attend_kernel,
+        functools.partial(attend_kernel, whose=whose),
         grid_spec=pltpu.PrefetchScalarGridSpec(
             num_scalar_prefetch=1,
             grid=(steps,),
-            in_specs=[pl.BlockSpec((tok, block), lambda i, p: (0, head * steps + i))] + specs * len(blocks),
+            in_specs=[pl.BlockSpec((tok, block), lambda i, p: (0, first * steps + i))] + specs * len(blocks),
             out_specs=pl.BlockSpec((tok, block), lambda i, p: (0, i)),
             scratch_shapes=[
                 pltpu.VMEM((tok, keys), F32), pltpu.VMEM((DH, keys), BF), pltpu.VMEM((keys, DH), BF)
@@ -172,16 +174,37 @@
     )(core, *flat, *weight)
 
 
-def project(attended, out_weight):
+def half_kernel(core_ref, in_ref, out_ref):
+    out_ref[...] = in_ref[...]
+
+
+def half_of(weight, core):
+    rows, wide = weight.shape[0] // 2, weight.shape[1]
+    steps = 4
+    return pl.pallas_call(
+        half_kernel,
+        name="half",
+        grid_spec=pltpu.PrefetchScalarGridSpec(
+            num_scalar_prefetch=1,
+            grid=(steps,),
+            in_specs=[pl.BlockSpec((rows // steps, wide), lambda i, c: (c[0] * steps + i, 0))],
+            out_specs=pl.BlockSpec((rows // steps, wide), lambda i, c: (i, 0)),
+        ),
+        out_shape=jax.ShapeDtypeStruct((rows, wide), BF),
+        compiler_params=pltpu.CompilerParams(vmem_limit_bytes=16 * 1024 * 1024),
+        cost_estimate=pl.CostEstimate(flops=0, bytes_accessed=4 * rows * wide, transcendentals=0),
+    )(core, pltpu.with_memory_space_constraint(weight, pltpu.HBM))
+
+
+def project(attended, far_second, out_weight):
     first, second = attended
-    tok, half = first.shape
+    tok, _ = first.shape
     core = lax.axis_index("core")
-    mine = lax.dynamic_slice_in_dim(out_weight, core * half, half, axis=0)
+    mine = half_of(out_weight, core.reshape(1))
     fetched = lax.ppermute(mine, ALL, neighbour_pairs())
     below_a, above_a = shift(first, 1), shift(first, -1)
     below_b, above_b = shift(second, 1), shift(second, -1)
     far_a = shift(below_a, 1)
-    far_b = shift(above_b, -1)
     other = lax.ppermute(fetched, "core", [(0, 1), (1, 0)])
     near = [(first, second), (below_a, below_b), (above_a, above_b)]
     which = core.reshape(1)
@@ -193,7 +216,7 @@
     above_own, below_own = shift(own[1], -1), shift(own[2], 1)
     pair = columns(pair_body, which, near, [fetched, other], specs, shapes)
     far = columns(
-        far_kernel, which, [(far_a, far_b)], [out_weight, fetched, other],
+        far_kernel, which, [(far_a, far_second)], [out_weight, fetched, other],
         whole((tok, 2 * PACK)), jax.ShapeDtypeStruct((tok, 2 * PACK), BF),
     )
     from_far = shift(far, 2)
@@ -385,14 +408,18 @@
     down_weight,
 ):
     tok, _ = hidden.shape[1:]
-    place = jnp.stack([lax.axis_index(CTX), lax.axis_index("xh"), lax.axis_index("y")])
-    gathered = gather_pair(keys[0], values[0])
-    first = attend(place, queries[0], gathered, 0)
-    second = attend(place, queries[0], gathered, 1)
+    xh, y = lax.axis_index("xh"), lax.axis_index("y")
+    place = jnp.stack([lax.axis_index(CTX), xh, y, xh * 4 + (y + 2) % 4])
+    blocks = gather_pair(keys[0], values[0])
+    far_query = shift(queries[0][:, WIDTH // 2 :], 2)
+    near_query = pltpu.with_memory_space_constraint(queries[0], pltpu.HBM)
+    first = attend(place, near_query, blocks, 0)
+    second = attend(place, near_query, blocks, 1)
+    far_second = attend(place, far_query, blocks, 1, 3)
 
     pick, pick_rest, pick_last, split, split_rest, split_last = prep(routes[0], slot_scores[0])
 
-    columns_home = project((first, second), out_weight)
+    columns_home = project((first, second), far_second, out_weight)
 
     shape = jax.ShapeDtypeStruct
     weights = gate_weight[0], up_weight[0], down_weight[0]

time: 415 us -> 416 us (level)
  waiting for transfers between devices: 242 us -> 222 us
  starting transfers between devices: 71.4 us -> 83.8 us
  Pallas kernels: 77.7 us -> 87.3 us
    ppermute x11, waiting for transfers between devices: 26.4 us -> 7.67 us  [shift(): return lax.ppermute(block, 'y', [(i, (i + step) % 4) for i in range(4)])]
    all_to_all x4, starting transfers between devices: 42.8 us -> 52.7 us  [exchange(): return lax.all_to_all(blocks, axes, split_axis=0, concat_axis=0, tiled=True)]
    pallas_call x2 -> x4, Pallas kernels: 11.4 us -> 20.9 us  [the longest x3 18.5 us: attend(): pl.pallas_call(functools.partial(attend_kernel, whose=whose), grid_spec=p...]
  transfers between devices with their start and end apart: 24 -> 24, of which waited for: 15 -> 14; matrix products, arithmetic and copies ran while one was open for 3% -> 3% of each run, Pallas kernels for 16% -> 18%
where the time goes in v8:
time: 416 us; the launch traced here: 411 us
  waiting for transfers between devices  222 us (53%)
  Pallas kernels  87.3 us (21%)
  starting transfers between devices  83.8 us (20%)
  local copies, waits for them, and re-layouts  9.62 us (2%)
  matrix products  7.32 us (2%)
    all_to_all x4, waiting for transfers between devices, exchange(): return lax.all_to_all(blocks, axes, split_axis=0, concat_axis=0, tiled=True)  162 us
    all_to_all x4, starting transfers between devices, exchange(): return lax.all_to_all(blocks, axes, split_axis=0, concat_axis=0, tiled=True)  52.7 us
    ppermute x1, waiting for transfers between devices, project(): fetched = lax.ppermute(mine, ALL, neighbour_pairs())  45.3 us
    pallas_call x2, Pallas kernels, experts(): pl.pallas_call(expert_kernel, grid=(SLOTS // TILE,), in_specs=[tiled((TIL...  44.7 us
    pallas_call x3, Pallas kernels, attend(): pl.pallas_call(functools.partial(attend_kernel, whose=whose), grid_spec=p...  18.5 us
    ppermute x11, starting transfers between devices, shift(): return lax.ppermute(block, 'y', [(i, (i + step) % 4) for i in range(4)])  15.1 us
    ppermute x7, starting transfers between devices, gather_pair(): blocks.append(lax.ppermute(pair, CTX, pairs))  13.2 us
    pallas_call x3, Pallas kernels, columns(): pl.pallas_call(body, grid=(wide // COLUMNS,), in_specs=[pl.BlockSpec(memo...  9.87 us
  transfers between devices with their start and end apart: 24, of which 14 were waited for; matrix products, arithmetic and copies ran while one was open for 3% of the time, Pallas kernels for 18%

profile of v8, /device:TPU:91, one launch (start us, length us, event | category | flops | bytes accessed | tf_op | source)
XLA Modules:
  0.0 410.6 jit_solution(470142325910467599)
XLA Ops:
  3.7 45.3 %collective-permute-done.11.refs_6_.fetched_ref = bf16[2048,512]{1,0:T(8,128)(2,1)S(1)} collective-permute-done((bf16[2048,512]{1,0:T(8,128)(2,1)S(1)}, bf16[2048,512]{1,0:T(8,128)(2,1)S(1)}, u32[]{:S(2)}, u32[]{:S(2)}) %collective-permute-start.11) | collective-permute-done | bytes 2097184 | tf_op jit(solution)/shard_map/ppermute | solution.py:204
  62.0 3.0 collective-permute-start.1
  68.4 4.4 %collective-permute-done.refs_2_.refs_3_ = bf16[128,512]{1,0:T(8,128)(2,1)S(1)} collective-permute-done((bf16[128,512]{1,0:T(8,128)(2,1)S(1)}, bf16[128,512]{1,0:T(8,128)(2,1)S(1)}, u32[]{:S(2)}, u32[]{:S(2)}) %collective-permute-start) | collective-permute-done | bytes 131104 | tf_op jit(solution)/shard_map/ppermute | solution.py:62
  72.8 6.4 %shard_map.109.refs_0_ = bf16[128,2048]{1,0:T(8,128)(2,1)S(1)} custom-call(s32[4]{0:T(128)S(1)} %pad_add_fusion.place_ref, bf16[128,4096]{1,0:T(8,128)(2,1)} %bitcast.38, bf16[128,512]{1,0:T(8,128)(2,1)S(1)} %pad_maximum_fusion.refs_0_.refs_1_, bf16[128,512]{1,0:T(8,128)(2,1)S(1)} %pad_maximum_fusion.refs_0_.refs_1_, ...), custom_call_target="tpu_custom_call" | custom-call | flops 1073741824 | bytes 1048576 | tf_op jit(solution)/shard_map/pallas_call | solution.py:106
  80.7 6.4 %shard_map.110.refs_1_ = bf16[128,2048]{1,0:T(8,128)(2,1)S(1)} custom-call(s32[4]{0:T(128)S(1)} %pad_add_fusion.place_ref, bf16[128,4096]{1,0:T(8,128)(2,1)} %bitcast.39, bf16[128,512]{1,0:T(8,128)(2,1)S(1)} %pad_maximum_fusion.refs_0_.refs_1_, bf16[128,512]{1,0:T(8,128)(2,1)S(1)} %pad_maximum_fusion.refs_0_.refs_1_, ...), custom_call_target="tpu_custom_call" | custom-call | flops 1073741824 | bytes 1048576 | tf_op jit(solution)/shard_map/pallas_call | solution.py:106
  90.4 5.7 %shard_map.113.right_ref = bf16[128,2048]{1,0:T(8,128)(2,1)S(1)} custom-call(s32[4]{0:T(128)S(1)} %pad_add_fusion.place_ref, bf16[128,2048]{1,0:T(8,128)(2,1)S(1)} %collective-permute-done.16.query_ref, bf16[128,512]{1,0:T(8,128)(2,1)S(1)} %pad_maximum_fusion.refs_0_.refs_1_, bf16[128,512]{1,0:T(8,128)(2,1)S(1)} %pad_maximum_fusion.refs_0_.refs_1_, ...), custom_call_target="tpu_custom_call" | custom-call | flops 1073741824 | bytes 1048576 | tf_op jit(solution)/shard_map/pallas_call | solution.py:106
  105.1 4.4 %collective-permute-done.15.left_ref = bf16[128,2048]{1,0:T(8,128)(2,1)S(1)} collective-permute-done((bf16[128,2048]{1,0:T(8,128)(2,1)S(1)}, bf16[128,2048]{1,0:T(8,128)(2,1)S(1)}, u32[]{:S(2)}, u32[]{:S(2)}) %collective-permute-start.15) | collective-permute-done | bytes 524320 | tf_op jit(solution)/shard_map/ppermute | solution.py:51
  109.4 3.0 shard_map.114
  112.4 3.4 collective-permute-start.17
  115.8 4.0 shard_map.112
  128.7 5.9 %make.1 = (bf16[1024,2560]{1,0:T(8,128)(2,1)}, bf16[256,2048]{1,0:T(8,128)(2,1)S(1)}, f32[128,4096]{1,0:T(8,128)}) custom-call(s32[4]{0:T(128)S(1)} %pad_add_fusion.place_ref, bf16[128,512]{1,0:T(8,128)(2,1)S(1)} %get-tuple-element.20.here_own, bf16[128,512]{1,0:T(8,128)(2,1)S(1)} %copy-done.3, bf16[128,512]{1,0:T(8,128)(2,1)S(1)} %collective-permute-done.13.above_own, ...), custom_call_target="tpu_custom_call" | custom-call | flops 1073741824 | bytes 5242880 | tf_op jit(solution)/shard_map/make/pallas_call | solution.py:431
  134.6 23.1 %all-to-all-start = ((bf16[128,8,2560]{2,1,0:T(8,128)(2,1)}), bf16[128,8,2560]{2,1,0:T(8,128)(2,1)}, u32[]{:S(2)}, u32[]{:S(2)}) async-start(bf16[128,8,2560]{2,1,0:T(8,128)(2,1)} %bitcast.34), calls=%async_computation | async-start | bytes 10485760 | tf_op jit(solution)/shard_map/all_to_all | solution.py:34
  157.7 3.3 convert_bitcast_fusion
  161.0 57.0 %all-to-all-done = bf16[128,8,2560]{2,1,0:T(8,128)(2,1)} async-done(((bf16[128,8,2560]{2,1,0:T(8,128)(2,1)}), bf16[128,8,2560]{2,1,0:T(8,128)(2,1)}, u32[]{:S(2)}, u32[]{:S(2)}) %all-to-all-start) | async-done | bytes 5242912 | tf_op jit(solution)/shard_map/all_to_all | solution.py:34
  218.0 10.1 %all-to-all-start.2 = ((bf16[128,8,2048]{2,1,0:T(8,128)(2,1)}), bf16[128,8,2048]{2,1,0:T(8,128)(2,1)}, u32[]{:S(2)}, u32[]{:S(2)}) async-start(bf16[128,8,2048]{2,1,0:T(8,128)(2,1)} %convert_bitcast_fusion), calls=%async_computation.2 | async-start | bytes 8388608 | tf_op jit(solution)/shard_map/all_to_all | solution.py:34
  228.2 24.1 %shard_map.115 = bf16[1024,2560]{1,0:T(8,128)(2,1)} custom-call(bf16[1024,2560]{1,0:T(8,128)(2,1)} %bitcast.13.got_ref, bf16[4096,768]{1,0:T(8,128)(2,1)} %bitcast.42, bf16[4096,768]{1,0:T(8,128)(2,1)} %bitcast.44, bf16[768,4096]{1,0:T(8,128)(2,1)} %bitcast.46), custom_call_target="tpu_custom_call" | custom-call | flops 12079595520 | bytes 29360128 | tf_op jit(solution)/shard_map/pallas_call | solution.py:311
  252.2 24.7 %all-to-all-done.2 = bf16[128,8,2048]{2,1,0:T(8,128)(2,1)} async-done(((bf16[128,8,2048]{2,1,0:T(8,128)(2,1)}), bf16[128,8,2048]{2,1,0:T(8,128)(2,1)}, u32[]{:S(2)}, u32[]{:S(2)}) %all-to-all-start.2) | async-done | bytes 4194336 | tf_op jit(solution)/shard_map/all_to_all | solution.py:34
  277.0 9.4 %all-to-all-start.1 = ((bf16[128,8,2560]{2,1,0:T(8,128)(2,1)}), bf16[128,8,2560]{2,1,0:T(8,128)(2,1)}, u32[]{:S(2)}, u32[]{:S(2)}) async-start(bf16[128,8,2560]{2,1,0:T(8,128)(2,1)} %bitcast.35), calls=%async_computation.1 | async-start | bytes 10485760 | tf_op jit(solution)/shard_map/all_to_all | solution.py:34
  286.4 20.6 %shard_map.116 = bf16[1024,2048]{1,0:T(8,128)(2,1)} custom-call(bf16[1024,2048]{1,0:T(8,128)(2,1)} %bitcast.20.got_ref, bf16[4096,768]{1,0:T(8,128)(2,1)} %bitcast.43, bf16[4096,768]{1,0:T(8,128)(2,1)} %bitcast.45, bf16[768,4096]{1,0:T(8,128)(2,1)} %bitcast.47), custom_call_target="tpu_custom_call" | custom-call | flops 9663676416 | bytes 27262976 | tf_op jit(solution)/shard_map/pallas_call | solution.py:311
  307.0 39.8 %all-to-all-done.1 = bf16[128,8,2560]{2,1,0:T(8,128)(2,1)} async-done(((bf16[128,8,2560]{2,1,0:T(8,128)(2,1)}), bf16[128,8,2560]{2,1,0:T(8,128)(2,1)}, u32[]{:S(2)}, u32[]{:S(2)}) %all-to-all-start.1) | async-done | bytes 5242912 | tf_op jit(solution)/shard_map/all_to_all | solution.py:34
  346.7 10.1 %all-to-all-start.3 = ((bf16[128,8,2048]{2,1,0:T(8,128)(2,1)}), bf16[128,8,2048]{2,1,0:T(8,128)(2,1)}, u32[]{:S(2)}, u32[]{:S(2)}) async-start(bf16[128,8,2048]{2,1,0:T(8,128)(2,1)} %bitcast.36), calls=%async_computation.3 | async-start | bytes 8388608 | tf_op jit(solution)/shard_map/all_to_all | solution.py:34
  361.2 3.6 fusion
  365.3 40.4 %all-to-all-done.3 = bf16[128,8,2048]{2,1,0:T(8,128)(2,1)} async-done(((bf16[128,8,2048]{2,1,0:T(8,128)(2,1)}), bf16[128,8,2048]{2,1,0:T(8,128)(2,1)}, u32[]{:S(2)}, u32[]{:S(2)}) %all-to-all-start.3) | async-done | bytes 4194336 | tf_op jit(solution)/shard_map/all_to_all | solution.py:34
  405.7 4.9 %finish.1 = bf16[128,4096]{1,0:T(8,128)(2,1)} custom-call(f32[128,4096]{1,0:T(8,128)S(1)} %maximum_add_fusion.low_ref.high_ref, f32[128,4096]{1,0:T(8,128)S(1)} %maximum_add_fusion.low_ref.high_ref, bf16[256,1024]{1,0:T(8,128)(2,1)S(1)} %get-tuple-element.32.split_ref, bf16[1024,2048]{1,0:T(8,128)(2,1)} %bitcast.22.back_ref), custom_call_target="tpu_custom_call" | custom-call | flops 1073741824 | bytes 7340032 | tf_op jit(solution)/shard_map/finish/pallas_call | solution.py:466
  (72 shorter events, 47.5 us)
Async XLA Ops:
  2.4 46.6 %collective-permute-start.11 = (bf16[2048,512]{1,0:T(8,128)(2,1)S(1)}, bf16[2048,512]{1,0:T(8,128)(2,1)S(1)}, u32[]{:S(2)}, u32[]{:S(2)}) collective-permute-start(bf16[2048,512]{1,0:T(8,128)(2,1)S(1)} %half.1), channel_id=1, source_target_pairs={{0,20},{1,21},{2,22},{3,23},{4,16},{5,17},{6,18},{7,19},{8,28},{9,... | collective-permute-start | bytes 6291464 | tf_op jit(solution)/shard_map/ppermute | solution.py:204
  49.0 60.4 %collective-permute-start.12 = (bf16[2048,512]{1,0:T(8,128)(2,1)S(1)}, bf16[2048,512]{1,0:T(8,128)(2,1)}, u32[]{:S(2)}, u32[]{:S(2)}) collective-permute-start(bf16[2048,512]{1,0:T(8,128)(2,1)S(1)} %collective-permute-done.11.refs_6_.fetched_ref), channel_id=1, source_target_pairs={{0,8},{8,0},{1,9},{9,1},{2,10},{10,2},{3,11},{11,3},{4,12},{12,4},... | collective-permute-start | bytes 6291464 | tf_op jit(solution)/shard_map/ppermute | solution.py:208
  50.6 7.8 %collective-permute-start.6 = (bf16[128,512]{1,0:T(8,128)(2,1)S(1)}, bf16[128,512]{1,0:T(8,128)(2,1)S(1)}, u32[]{:S(2)}, u32[]{:S(2)}) collective-permute-start(bf16[128,512]{1,0:T(8,128)(2,1)S(1)} %pad_maximum_fusion.refs_0_.refs_1_), channel_id=1, source_target_pairs={{7,0},{4,1},{5,2},{6,3},{3,4},{0,5},{1,6},{2,7},{15,8},{12,9},{13,... | collective-permute-start | bytes 393224 | tf_op jit(solution)/shard_map/ppermute | solution.py:62
  53.4 8.7 %collective-permute-start.5 = (bf16[128,512]{1,0:T(8,128)(2,1)S(1)}, bf16[128,512]{1,0:T(8,128)(2,1)S(1)}, u32[]{:S(2)}, u32[]{:S(2)}) collective-permute-start(bf16[128,512]{1,0:T(8,128)(2,1)S(1)} %pad_maximum_fusion.refs_0_.refs_1_), channel_id=1, source_target_pairs={{6,0},{7,1},{4,2},{5,3},{2,4},{3,5},{0,6},{1,7},{14,8},{15,9},{12,... | collective-permute-start | bytes 393224 | tf_op jit(solution)/shard_map/ppermute | solution.py:62
  55.3 10.5 %collective-permute-start.4 = (bf16[128,512]{1,0:T(8,128)(2,1)S(1)}, bf16[128,512]{1,0:T(8,128)(2,1)S(1)}, u32[]{:S(2)}, u32[]{:S(2)}) collective-permute-start(bf16[128,512]{1,0:T(8,128)(2,1)S(1)} %pad_maximum_fusion.refs_0_.refs_1_), channel_id=1, source_target_pairs={{5,0},{6,1},{7,2},{4,3},{1,4},{2,5},{3,6},{0,7},{13,8},{14,9},{15,... | collective-permute-start | bytes 393224 | tf_op jit(solution)/shard_map/ppermute | solution.py:62
  57.6 9.8 %collective-permute-start.3 = (bf16[128,512]{1,0:T(8,128)(2,1)S(1)}, bf16[128,512]{1,0:T(8,128)(2,1)S(1)}, u32[]{:S(2)}, u32[]{:S(2)}) collective-permute-start(bf16[128,512]{1,0:T(8,128)(2,1)S(1)} %pad_maximum_fusion.refs_0_.refs_1_), channel_id=1, source_target_pairs={{4,0},{5,1},{6,2},{7,3},{0,4},{1,5},{2,6},{3,7},{12,8},{13,9},{14,... | collective-permute-start | bytes 393224 | tf_op jit(solution)/shard_map/ppermute | solution.py:62
  58.4 10.0 %collective-permute-start.2 = (bf16[128,512]{1,0:T(8,128)(2,1)S(1)}, bf16[128,512]{1,0:T(8,128)(2,1)S(1)}, u32[]{:S(2)}, u32[]{:S(2)}) collective-permute-start(bf16[128,512]{1,0:T(8,128)(2,1)S(1)} %pad_maximum_fusion.refs_0_.refs_1_), channel_id=1, source_target_pairs={{3,0},{0,1},{1,2},{2,3},{7,4},{4,5},{5,6},{6,7},{11,8},{8,9},{9,10... | collective-permute-start | bytes 393224 | tf_op jit(solution)/shard_map/ppermute | solution.py:62
  62.0 6.4 %collective-permute-start.1 = (bf16[128,512]{1,0:T(8,128)(2,1)S(1)}, bf16[128,512]{1,0:T(8,128)(2,1)S(1)}, u32[]{:S(2)}, u32[]{:S(2)}) collective-permute-start(bf16[128,512]{1,0:T(8,128)(2,1)S(1)} %pad_maximum_fusion.refs_0_.refs_1_), channel_id=1, source_target_pairs={{2,0},{3,1},{0,2},{1,3},{6,4},{7,5},{4,6},{5,7},{10,8},{11,9},{8,1... | collective-permute-start | bytes 393224 | tf_op jit(solution)/shard_map/ppermute | solution.py:62
  65.8 7.0 %collective-permute-start = (bf16[128,512]{1,0:T(8,128)(2,1)S(1)}, bf16[128,512]{1,0:T(8,128)(2,1)S(1)}, u32[]{:S(2)}, u32[]{:S(2)}) collective-permute-start(bf16[128,512]{1,0:T(8,128)(2,1)S(1)} %pad_maximum_fusion.refs_0_.refs_1_), channel_id=1, source_target_pairs={{1,0},{2,1},{3,2},{0,3},{5,4},{6,5},{7,6},{4,7},{9,8},{10,9},{11,1... | collective-permute-start | bytes 393224 | tf_op jit(solution)/shard_map/ppermute | solution.py:62
  67.4 20.9 %collective-permute-start.16 = (bf16[128,2048]{1,0:T(8,128)(2,1)S(1)}, bf16[128,2048]{1,0:T(8,128)(2,1)S(1)}, u32[]{:S(2)}, u32[]{:S(2)}) collective-permute-start(bf16[128,2048]{1,0:T(8,128)(2,1)S(1)} %slice.20), channel_id=1, source_target_pairs={{0,2},{1,3},{2,0},{3,1},{4,6},{5,7},{6,4},{7,5},{8,10},{9,11},{10,... | collective-permute-start | bytes 1572872 | tf_op jit(solution)/shard_map/ppermute | solution.py:51
  79.2 10.7 %collective-permute-start.7 = (bf16[128,2048]{1,0:T(8,128)(2,1)S(1)}, bf16[128,2048]{1,0:T(8,128)(2,1)S(1)}, u32[]{:S(2)}, u32[]{:S(2)}) collective-permute-start(bf16[128,2048]{1,0:T(8,128)(2,1)S(1)} %shard_map.109.refs_0_), channel_id=1, source_target_pairs={{0,1},{1,2},{2,3},{3,0},{4,5},{5,6},{6,7},{7,4},{8,9},{9,10},{10,1... | collective-permute-start | bytes 1572872 | tf_op jit(solution)/shard_map/ppermute | solution.py:51
  79.3 16.8 %collective-permute-start.9 = (bf16[128,2048]{1,0:T(8,128)(2,1)S(1)}, bf16[128,2048]{1,0:T(8,128)(2,1)S(1)}, u32[]{:S(2)}, u32[]{:S(2)}) collective-permute-start(bf16[128,2048]{1,0:T(8,128)(2,1)S(1)} %shard_map.109.refs_0_), channel_id=1, source_target_pairs={{0,3},{1,0},{2,1},{3,2},{4,7},{5,4},{6,5},{7,6},{8,11},{9,8},{10,9... | collective-permute-start | bytes 1572872 | tf_op jit(solution)/shard_map/ppermute | solution.py:51
  87.2 9.3 %collective-permute-start.10 = (bf16[128,2048]{1,0:T(8,128)(2,1)S(1)}, bf16[128,2048]{1,0:T(8,128)(2,1)S(1)}, u32[]{:S(2)}, u32[]{:S(2)}) collective-permute-start(bf16[128,2048]{1,0:T(8,128)(2,1)S(1)} %shard_map.110.refs_1_), channel_id=1, source_target_pairs={{0,3},{1,0},{2,1},{3,2},{4,7},{5,4},{6,5},{7,6},{8,11},{9,8},{10,9... | collective-permute-start | bytes 1572872 | tf_op jit(solution)/shard_map/ppermute | solution.py:51
  88.3 10.4 %collective-permute-start.8 = (bf16[128,2048]{1,0:T(8,128)(2,1)S(1)}, bf16[128,2048]{1,0:T(8,128)(2,1)S(1)}, u32[]{:S(2)}, u32[]{:S(2)}) collective-permute-start(bf16[128,2048]{1,0:T(8,128)(2,1)S(1)} %shard_map.110.refs_1_), channel_id=1, source_target_pairs={{0,1},{1,2},{2,3},{3,0},{4,5},{5,6},{6,7},{7,4},{8,9},{9,10},{10,1... | collective-permute-start | bytes 1572872 | tf_op jit(solution)/shard_map/ppermute | solution.py:51
  89.9 19.5 %collective-permute-start.15 = (bf16[128,2048]{1,0:T(8,128)(2,1)S(1)}, bf16[128,2048]{1,0:T(8,128)(2,1)S(1)}, u32[]{:S(2)}, u32[]{:S(2)}) collective-permute-start(bf16[128,2048]{1,0:T(8,128)(2,1)S(1)} %collective-permute-done.7.refs_2_), channel_id=1, source_target_pairs={{0,1},{1,2},{2,3},{3,0},{4,5},{5,6},{6,7},{7,4},{8,9},{9,10},{10,1... | collective-permute-start | bytes 1572872 | tf_op jit(solution)/shard_map/ppermute | solution.py:51
  101.7 23.5 %collective-permute-start.13 = (bf16[128,512]{1,0:T(8,128)(2,1)}, bf16[128,512]{1,0:T(8,128)(2,1)S(1)}, u32[]{:S(2)}, u32[]{:S(2)}) collective-permute-start(bf16[128,512]{1,0:T(8,128)(2,1)} %get-tuple-element.22), channel_id=1, source_target_pairs={{0,3},{1,0},{2,1},{3,2},{4,7},{5,4},{6,5},{7,6},{8,11},{9,8},{10,9... | collective-permute-start | bytes 393224 | tf_op jit(solution)/shard_map/ppermute | solution.py:51
  102.9 22.2 %collective-permute-start.18 = (bf16[128,512]{1,0:T(8,128)(2,1)}, bf16[128,512]{1,0:T(8,128)(2,1)S(1)}, u32[]{:S(2)}, u32[]{:S(2)}) collective-permute-start(bf16[128,512]{1,0:T(8,128)(2,1)} %get-tuple-element.24), channel_id=1, source_target_pairs={{0,1},{1,2},{2,3},{3,0},{4,5},{5,6},{6,7},{7,4},{8,9},{9,10},{10,1... | collective-permute-start | bytes 393224 | tf_op jit(solution)/shard_map/ppermute | solution.py:51
  112.4 13.4 %collective-permute-start.17 = (bf16[128,1024]{1,0:T(8,128)(2,1)S(1)}, bf16[128,1024]{1,0:T(8,128)(2,1)S(1)}, u32[]{:S(2)}, u32[]{:S(2)}) collective-permute-start(bf16[128,1024]{1,0:T(8,128)(2,1)S(1)} %shard_map.114), channel_id=1, source_target_pairs={{0,2},{1,3},{2,0},{3,1},{4,6},{5,7},{6,4},{7,5},{8,10},{9,11},{10,... | collective-permute-start | bytes 786440 | tf_op jit(solution)/shard_map/ppermute | solution.py:51
  120.4 5.2 %collective-permute-start.14 = (bf16[128,512]{1,0:T(8,128)(2,1)}, bf16[128,512]{1,0:T(8,128)(2,1)S(1)}, u32[]{:S(2)}, u32[]{:S(2)}) collective-permute-start(bf16[128,512]{1,0:T(8,128)(2,1)} %get-tuple-element.23), channel_id=1, source_target_pairs={{0,3},{1,0},{2,1},{3,2},{4,7},{5,4},{6,5},{7,6},{8,11},{9,8},{10,9... | collective-permute-start | bytes 393224 | tf_op jit(solution)/shard_map/ppermute | solution.py:51
  121.3 4.5 %collective-permute-start.19 = (bf16[128,512]{1,0:T(8,128)(2,1)}, bf16[128,512]{1,0:T(8,128)(2,1)S(1)}, u32[]{:S(2)}, u32[]{:S(2)}) collective-permute-start(bf16[128,512]{1,0:T(8,128)(2,1)} %get-tuple-element.25), channel_id=1, source_target_pairs={{0,1},{1,2},{2,3},{3,0},{4,5},{5,6},{6,7},{7,4},{8,9},{9,10},{10,1... | collective-permute-start | bytes 393224 | tf_op jit(solution)/shard_map/ppermute | solution.py:51
  134.6 83.4 %all-to-all-start = ((bf16[128,8,2560]{2,1,0:T(8,128)(2,1)}), bf16[128,8,2560]{2,1,0:T(8,128)(2,1)}, u32[]{:S(2)}, u32[]{:S(2)}) async-start(bf16[128,8,2560]{2,1,0:T(8,128)(2,1)} %bitcast.34), calls=%async_computation | async-start | bytes 10485760 | tf_op jit(solution)/shard_map/all_to_all | solution.py:34
  218.0 58.9 %all-to-all-start.2 = ((bf16[128,8,2048]{2,1,0:T(8,128)(2,1)}), bf16[128,8,2048]{2,1,0:T(8,128)(2,1)}, u32[]{:S(2)}, u32[]{:S(2)}) async-start(bf16[128,8,2048]{2,1,0:T(8,128)(2,1)} %convert_bitcast_fusion), calls=%async_computation.2 | async-start | bytes 8388608 | tf_op jit(solution)/shard_map/all_to_all | solution.py:34
  277.0 69.8 %all-to-all-start.1 = ((bf16[128,8,2560]{2,1,0:T(8,128)(2,1)}), bf16[128,8,2560]{2,1,0:T(8,128)(2,1)}, u32[]{:S(2)}, u32[]{:S(2)}) async-start(bf16[128,8,2560]{2,1,0:T(8,128)(2,1)} %bitcast.35), calls=%async_computation.1 | async-start | bytes 10485760 | tf_op jit(solution)/shard_map/all_to_all | solution.py:34
  346.7 58.9 %all-to-all-start.3 = ((bf16[128,8,2048]{2,1,0:T(8,128)(2,1)}), bf16[128,8,2048]{2,1,0:T(8,128)(2,1)}, u32[]{:S(2)}, u32[]{:S(2)}) async-start(bf16[128,8,2048]{2,1,0:T(8,128)(2,1)} %bitcast.36), calls=%async_computation.3 | async-start | bytes 8388608 | tf_op jit(solution)/shard_map/all_to_all | solution.py:34
  (12 other events, 154.5 us)

commit v9 on v7

--- a/solution.py
+++ b/solution.py
@@ -387,8 +387,9 @@
     tok, _ = hidden.shape[1:]
     place = jnp.stack([lax.axis_index(CTX), lax.axis_index("xh"), lax.axis_index("y")])
     gathered = gather_pair(keys[0], values[0])
-    first = attend(place, queries[0], gathered, 0)
-    second = attend(place, queries[0], gathered, 1)
+    held = pltpu.with_memory_space_constraint(queries[0], pltpu.HBM)
+    first = attend(place, held, gathered, 0)
+    second = attend(place, held, gathered, 1)
 
     pick, pick_rest, pick_last, split, split_rest, split_last = prep(routes[0], slot_scores[0])
 

time: 415 us -> 415 us (level)
  transfers between devices with their start and end apart: 24 -> 24, of which waited for: 15 -> 15; matrix products, arithmetic and copies ran while one was open for 3% -> 3% of each run, Pallas kernels for 16% -> 17%
where the time goes in v9:
time: 415 us; the launch traced here: 410 us
  waiting for transfers between devices  241 us (58%)
  Pallas kernels  79.2 us (19%)
  starting transfers between devices  71.7 us (17%)
  local copies, waits for them, and re-layouts  10.3 us (2%)
  matrix products  7.32 us (2%)
    all_to_all x4, waiting for transfers between devices, exchange(): return lax.all_to_all(blocks, axes, split_axis=0, concat_axis=0, tiled=True)  162 us
    ppermute x1, waiting for transfers between devices, project(): fetched = lax.ppermute(mine, ALL, neighbour_pairs())  45.3 us
    pallas_call x2, Pallas kernels, experts(): pl.pallas_call(expert_kernel, grid=(SLOTS // TILE,), in_specs=[tiled((TIL...  44.7 us
    all_to_all x4, starting transfers between devices, exchange(): return lax.all_to_all(blocks, axes, split_axis=0, concat_axis=0, tiled=True)  42.8 us
    ppermute x11, waiting for transfers between devices, shift(): return lax.ppermute(block, 'y', [(i, (i + step) % 4) for i in range(4)])  26.1 us
    ppermute x7, starting transfers between devices, gather_pair(): blocks.append(lax.ppermute(pair, CTX, pairs))  13.2 us
    ppermute x11, starting transfers between devices, shift(): return lax.ppermute(block, 'y', [(i, (i + step) % 4) for i in range(4)])  12.8 us
    pallas_call x2, Pallas kernels, attend(): pl.pallas_call(attend_kernel, grid_spec=pltpu.PrefetchScalarGridSpec(num_...  12.8 us
  transfers between devices with their start and end apart: 24, of which 15 were waited for; matrix products, arithmetic and copies ran while one was open for 3% of the time, Pallas kernels for 17%

profile of v9, /device:TPU:91, one launch (start us, length us, event | category | flops | bytes accessed | tf_op | source)
XLA Modules:
  0.0 410.4 jit_solution(3172501979508043720)
XLA Ops:
  3.1 45.3 %collective-permute-done.11.refs_6_.fetched_ref = bf16[2048,512]{1,0:T(8,128)(2,1)S(1)} collective-permute-done((bf16[2048,512]{1,0:T(8,128)(2,1)S(1)}, bf16[2048,512]{1,0:T(8,128)(2,1)S(1)}, u32[]{:S(2)}, u32[]{:S(2)}) %collective-permute-start.11) | collective-permute-done | bytes 2097184 | tf_op jit(solution)/shard_map/ppermute | solution.py:180
  61.4 3.0 collective-permute-start.1
  67.2 4.0 collective-permute-done.refs_2_.refs_3_
  71.2 6.4 %shard_map.109.refs_0_ = bf16[128,2048]{1,0:T(8,128)(2,1)S(1)} custom-call(s32[3]{0:T(128)S(1)} %pad_add_fusion.place_ref, bf16[128,4096]{1,0:T(8,128)(2,1)} %bitcast.44, bf16[128,512]{1,0:T(8,128)(2,1)S(1)} %pad_maximum_fusion.refs_0_.refs_1_, bf16[128,512]{1,0:T(8,128)(2,1)S(1)} %pad_maximum_fusion.refs_0_.refs_1_, ...), custom_call_target="tpu_custom_call" | custom-call | flops 1073741824 | bytes 1048576 | tf_op jit(solution)/shard_map/pallas_call | solution.py:104
  77.7 6.4 %shard_map.110.refs_1_ = bf16[128,2048]{1,0:T(8,128)(2,1)S(1)} custom-call(s32[3]{0:T(128)S(1)} %pad_add_fusion.place_ref, bf16[128,4096]{1,0:T(8,128)(2,1)} %bitcast.45, bf16[128,512]{1,0:T(8,128)(2,1)S(1)} %pad_maximum_fusion.refs_0_.refs_1_, bf16[128,512]{1,0:T(8,128)(2,1)S(1)} %pad_maximum_fusion.refs_0_.refs_1_, ...), custom_call_target="tpu_custom_call" | custom-call | flops 1073741824 | bytes 1048576 | tf_op jit(solution)/shard_map/pallas_call | solution.py:104
  90.2 6.1 %collective-permute-done.10.refs_5_ = bf16[128,2048]{1,0:T(8,128)(2,1)S(1)} collective-permute-done((bf16[128,2048]{1,0:T(8,128)(2,1)S(1)}, bf16[128,2048]{1,0:T(8,128)(2,1)S(1)}, u32[]{:S(2)}, u32[]{:S(2)}) %collective-permute-start.10) | collective-permute-done | bytes 524320 | tf_op jit(solution)/shard_map/ppermute | solution.py:50
  96.4 11.2 %collective-permute-done.9.refs_4_ = bf16[128,2048]{1,0:T(8,128)(2,1)S(1)} collective-permute-done((bf16[128,2048]{1,0:T(8,128)(2,1)S(1)}, bf16[128,2048]{1,0:T(8,128)(2,1)S(1)}, u32[]{:S(2)}, u32[]{:S(2)}) %collective-permute-start.9) | collective-permute-done | bytes 524320 | tf_op jit(solution)/shard_map/ppermute | solution.py:50
  107.6 2.9 shard_map.111
  113.2 5.6 %collective-permute-done.16.right_ref = bf16[128,2048]{1,0:T(8,128)(2,1)S(1)} collective-permute-done((bf16[128,2048]{1,0:T(8,128)(2,1)S(1)}, bf16[128,2048]{1,0:T(8,128)(2,1)S(1)}, u32[]{:S(2)}, u32[]{:S(2)}) %collective-permute-start.16) | collective-permute-done | bytes 524320 | tf_op jit(solution)/shard_map/ppermute | solution.py:50
  123.4 4.0 shard_map.112
  138.4 5.9 %make.1 = (bf16[1024,2560]{1,0:T(8,128)(2,1)}, bf16[256,2048]{1,0:T(8,128)(2,1)S(1)}, f32[128,4096]{1,0:T(8,128)}) custom-call(s32[3]{0:T(128)S(1)} %pad_add_fusion.place_ref, bf16[128,512]{1,0:T(8,128)(2,1)S(1)} %get-tuple-element.20.here_own, bf16[128,512]{1,0:T(8,128)(2,1)S(1)} %copy-done.3, bf16[128,512]{1,0:T(8,128)(2,1)S(1)} %collective-permute-done.13.above_own, ...), custom_call_target="tpu_custom_call" | custom-call | flops 1073741824 | bytes 5242880 | tf_op jit(solution)/shard_map/make/pallas_call | solution.py:405
  144.3 13.1 %all-to-all-start = ((bf16[128,8,2560]{2,1,0:T(8,128)(2,1)}), bf16[128,8,2560]{2,1,0:T(8,128)(2,1)}, u32[]{:S(2)}, u32[]{:S(2)}) async-start(bf16[128,8,2560]{2,1,0:T(8,128)(2,1)} %bitcast.33), calls=%async_computation | async-start | bytes 10485760 | tf_op jit(solution)/shard_map/all_to_all | solution.py:33
  157.5 3.3 convert_bitcast_fusion
  160.8 57.0 %all-to-all-done = bf16[128,8,2560]{2,1,0:T(8,128)(2,1)} async-done(((bf16[128,8,2560]{2,1,0:T(8,128)(2,1)}), bf16[128,8,2560]{2,1,0:T(8,128)(2,1)}, u32[]{:S(2)}, u32[]{:S(2)}) %all-to-all-start) | async-done | bytes 5242912 | tf_op jit(solution)/shard_map/all_to_all | solution.py:33
  217.8 10.1 %all-to-all-start.2 = ((bf16[128,8,2048]{2,1,0:T(8,128)(2,1)}), bf16[128,8,2048]{2,1,0:T(8,128)(2,1)}, u32[]{:S(2)}, u32[]{:S(2)}) async-start(bf16[128,8,2048]{2,1,0:T(8,128)(2,1)} %convert_bitcast_fusion), calls=%async_computation.2 | async-start | bytes 8388608 | tf_op jit(solution)/shard_map/all_to_all | solution.py:33
  228.0 24.1 %shard_map.114 = bf16[1024,2560]{1,0:T(8,128)(2,1)} custom-call(bf16[1024,2560]{1,0:T(8,128)(2,1)} %bitcast.12.got_ref, bf16[4096,768]{1,0:T(8,128)(2,1)} %bitcast.38, bf16[4096,768]{1,0:T(8,128)(2,1)} %bitcast.40, bf16[768,4096]{1,0:T(8,128)(2,1)} %bitcast.42), custom_call_target="tpu_custom_call" | custom-call | flops 12079595520 | bytes 29360128 | tf_op jit(solution)/shard_map/pallas_call | solution.py:288
  252.0 24.7 %all-to-all-done.2 = bf16[128,8,2048]{2,1,0:T(8,128)(2,1)} async-done(((bf16[128,8,2048]{2,1,0:T(8,128)(2,1)}), bf16[128,8,2048]{2,1,0:T(8,128)(2,1)}, u32[]{:S(2)}, u32[]{:S(2)}) %all-to-all-start.2) | async-done | bytes 4194336 | tf_op jit(solution)/shard_map/all_to_all | solution.py:33
  276.8 9.4 %all-to-all-start.1 = ((bf16[128,8,2560]{2,1,0:T(8,128)(2,1)}), bf16[128,8,2560]{2,1,0:T(8,128)(2,1)}, u32[]{:S(2)}, u32[]{:S(2)}) async-start(bf16[128,8,2560]{2,1,0:T(8,128)(2,1)} %bitcast.34), calls=%async_computation.1 | async-start | bytes 10485760 | tf_op jit(solution)/shard_map/all_to_all | solution.py:33
  286.2 20.6 %shard_map.115 = bf16[1024,2048]{1,0:T(8,128)(2,1)} custom-call(bf16[1024,2048]{1,0:T(8,128)(2,1)} %bitcast.19.got_ref, bf16[4096,768]{1,0:T(8,128)(2,1)} %bitcast.39, bf16[4096,768]{1,0:T(8,128)(2,1)} %bitcast.41, bf16[768,4096]{1,0:T(8,128)(2,1)} %bitcast.43), custom_call_target="tpu_custom_call" | custom-call | flops 9663676416 | bytes 27262976 | tf_op jit(solution)/shard_map/pallas_call | solution.py:288
  306.8 39.7 %all-to-all-done.1 = bf16[128,8,2560]{2,1,0:T(8,128)(2,1)} async-done(((bf16[128,8,2560]{2,1,0:T(8,128)(2,1)}), bf16[128,8,2560]{2,1,0:T(8,128)(2,1)}, u32[]{:S(2)}, u32[]{:S(2)}) %all-to-all-start.1) | async-done | bytes 5242912 | tf_op jit(solution)/shard_map/all_to_all | solution.py:33
  346.5 10.1 %all-to-all-start.3 = ((bf16[128,8,2048]{2,1,0:T(8,128)(2,1)}), bf16[128,8,2048]{2,1,0:T(8,128)(2,1)}, u32[]{:S(2)}, u32[]{:S(2)}) async-start(bf16[128,8,2048]{2,1,0:T(8,128)(2,1)} %bitcast.35), calls=%async_computation.3 | async-start | bytes 8388608 | tf_op jit(solution)/shard_map/all_to_all | solution.py:33
  361.0 3.6 fusion
  365.1 40.4 %all-to-all-done.3 = bf16[128,8,2048]{2,1,0:T(8,128)(2,1)} async-done(((bf16[128,8,2048]{2,1,0:T(8,128)(2,1)}), bf16[128,8,2048]{2,1,0:T(8,128)(2,1)}, u32[]{:S(2)}, u32[]{:S(2)}) %all-to-all-start.3) | async-done | bytes 4194336 | tf_op jit(solution)/shard_map/all_to_all | solution.py:33
  405.5 4.9 %finish.1 = bf16[128,4096]{1,0:T(8,128)(2,1)} custom-call(f32[128,4096]{1,0:T(8,128)S(1)} %maximum_add_fusion.low_ref.high_ref, f32[128,4096]{1,0:T(8,128)S(1)} %maximum_add_fusion.low_ref.high_ref, bf16[256,1024]{1,0:T(8,128)(2,1)S(1)} %get-tuple-element.32.split_ref, bf16[1024,2048]{1,0:T(8,128)(2,1)} %bitcast.21.back_ref), custom_call_target="tpu_custom_call" | custom-call | flops 1073741824 | bytes 7340032 | tf_op jit(solution)/shard_map/finish/pallas_call | solution.py:440
  (70 shorter events, 48.1 us)
Async XLA Ops:
  1.8 46.6 %collective-permute-start.11 = (bf16[2048,512]{1,0:T(8,128)(2,1)S(1)}, bf16[2048,512]{1,0:T(8,128)(2,1)S(1)}, u32[]{:S(2)}, u32[]{:S(2)}) collective-permute-start(bf16[2048,512]{1,0:T(8,128)(2,1)S(1)} %constant_dynamic-slice_fusion), channel_id=1, source_target_pairs={{0,20},{1,21},{2,22},{3,23},{4,16},{5,17},{6,18},{7,19},{8,28},{9,... | collective-permute-start | bytes 6291464 | tf_op jit(solution)/shard_map/ppermute | solution.py:180
  48.4 70.5 %collective-permute-start.12 = (bf16[2048,512]{1,0:T(8,128)(2,1)S(1)}, bf16[2048,512]{1,0:T(8,128)(2,1)}, u32[]{:S(2)}, u32[]{:S(2)}) collective-permute-start(bf16[2048,512]{1,0:T(8,128)(2,1)S(1)} %collective-permute-done.11.refs_6_.fetched_ref), channel_id=1, source_target_pairs={{0,8},{8,0},{1,9},{9,1},{2,10},{10,2},{3,11},{11,3},{4,12},{12,4},... | collective-permute-start | bytes 6291464 | tf_op jit(solution)/shard_map/ppermute | solution.py:185
  49.9 7.8 %collective-permute-start.6 = (bf16[128,512]{1,0:T(8,128)(2,1)S(1)}, bf16[128,512]{1,0:T(8,128)(2,1)S(1)}, u32[]{:S(2)}, u32[]{:S(2)}) collective-permute-start(bf16[128,512]{1,0:T(8,128)(2,1)S(1)} %pad_maximum_fusion.refs_0_.refs_1_), channel_id=1, source_target_pairs={{7,0},{4,1},{5,2},{6,3},{3,4},{0,5},{1,6},{2,7},{15,8},{12,9},{13,... | collective-permute-start | bytes 393224 | tf_op jit(solution)/shard_map/ppermute | solution.py:61
  52.7 8.7 %collective-permute-start.5 = (bf16[128,512]{1,0:T(8,128)(2,1)S(1)}, bf16[128,512]{1,0:T(8,128)(2,1)S(1)}, u32[]{:S(2)}, u32[]{:S(2)}) collective-permute-start(bf16[128,512]{1,0:T(8,128)(2,1)S(1)} %pad_maximum_fusion.refs_0_.refs_1_), channel_id=1, source_target_pairs={{6,0},{7,1},{4,2},{5,3},{2,4},{3,5},{0,6},{1,7},{14,8},{15,9},{12,... | collective-permute-start | bytes 393224 | tf_op jit(solution)/shard_map/ppermute | solution.py:61
  54.6 10.5 %collective-permute-start.4 = (bf16[128,512]{1,0:T(8,128)(2,1)S(1)}, bf16[128,512]{1,0:T(8,128)(2,1)S(1)}, u32[]{:S(2)}, u32[]{:S(2)}) collective-permute-start(bf16[128,512]{1,0:T(8,128)(2,1)S(1)} %pad_maximum_fusion.refs_0_.refs_1_), channel_id=1, source_target_pairs={{5,0},{6,1},{7,2},{4,3},{1,4},{2,5},{3,6},{0,7},{13,8},{14,9},{15,... | collective-permute-start | bytes 393224 | tf_op jit(solution)/shard_map/ppermute | solution.py:61
  57.0 9.8 %collective-permute-start.3 = (bf16[128,512]{1,0:T(8,128)(2,1)S(1)}, bf16[128,512]{1,0:T(8,128)(2,1)S(1)}, u32[]{:S(2)}, u32[]{:S(2)}) collective-permute-start(bf16[128,512]{1,0:T(8,128)(2,1)S(1)} %pad_maximum_fusion.refs_0_.refs_1_), channel_id=1, source_target_pairs={{4,0},{5,1},{6,2},{7,3},{0,4},{1,5},{2,6},{3,7},{12,8},{13,9},{14,... | collective-permute-start | bytes 393224 | tf_op jit(solution)/shard_map/ppermute | solution.py:61
  57.7 9.1 %collective-permute-start.2 = (bf16[128,512]{1,0:T(8,128)(2,1)S(1)}, bf16[128,512]{1,0:T(8,128)(2,1)S(1)}, u32[]{:S(2)}, u32[]{:S(2)}) collective-permute-start(bf16[128,512]{1,0:T(8,128)(2,1)S(1)} %pad_maximum_fusion.refs_0_.refs_1_), channel_id=1, source_target_pairs={{3,0},{0,1},{1,2},{2,3},{7,4},{4,5},{5,6},{6,7},{11,8},{8,9},{9,10... | collective-permute-start | bytes 393224 | tf_op jit(solution)/shard_map/ppermute | solution.py:61
  61.4 5.9 %collective-permute-start.1 = (bf16[128,512]{1,0:T(8,128)(2,1)S(1)}, bf16[128,512]{1,0:T(8,128)(2,1)S(1)}, u32[]{:S(2)}, u32[]{:S(2)}) collective-permute-start(bf16[128,512]{1,0:T(8,128)(2,1)S(1)} %pad_maximum_fusion.refs_0_.refs_1_), channel_id=1, source_target_pairs={{2,0},{3,1},{0,2},{1,3},{6,4},{7,5},{4,6},{5,7},{10,8},{11,9},{8,1... | collective-permute-start | bytes 393224 | tf_op jit(solution)/shard_map/ppermute | solution.py:61
  65.1 6.1 %collective-permute-start = (bf16[128,512]{1,0:T(8,128)(2,1)S(1)}, bf16[128,512]{1,0:T(8,128)(2,1)S(1)}, u32[]{:S(2)}, u32[]{:S(2)}) collective-permute-start(bf16[128,512]{1,0:T(8,128)(2,1)S(1)} %pad_maximum_fusion.refs_0_.refs_1_), channel_id=1, source_target_pairs={{1,0},{2,1},{3,2},{0,3},{5,4},{6,5},{7,6},{4,7},{9,8},{10,9},{11,1... | collective-permute-start | bytes 393224 | tf_op jit(solution)/shard_map/ppermute | solution.py:61
  77.6 11.1 %collective-permute-start.7 = (bf16[128,2048]{1,0:T(8,128)(2,1)S(1)}, bf16[128,2048]{1,0:T(8,128)(2,1)S(1)}, u32[]{:S(2)}, u32[]{:S(2)}) collective-permute-start(bf16[128,2048]{1,0:T(8,128)(2,1)S(1)} %shard_map.109.refs_0_), channel_id=1, source_target_pairs={{0,1},{1,2},{2,3},{3,0},{4,5},{5,6},{6,7},{7,4},{8,9},{9,10},{10,1... | collective-permute-start | bytes 1572872 | tf_op jit(solution)/shard_map/ppermute | solution.py:50
  84.1 12.2 %collective-permute-start.10 = (bf16[128,2048]{1,0:T(8,128)(2,1)S(1)}, bf16[128,2048]{1,0:T(8,128)(2,1)S(1)}, u32[]{:S(2)}, u32[]{:S(2)}) collective-permute-start(bf16[128,2048]{1,0:T(8,128)(2,1)S(1)} %shard_map.110.refs_1_), channel_id=1, source_target_pairs={{0,3},{1,0},{2,1},{3,2},{4,7},{5,4},{6,5},{7,6},{8,11},{9,8},{10,9... | collective-permute-start | bytes 1572872 | tf_op jit(solution)/shard_map/ppermute | solution.py:50
  85.6 21.9 %collective-permute-start.9 = (bf16[128,2048]{1,0:T(8,128)(2,1)S(1)}, bf16[128,2048]{1,0:T(8,128)(2,1)S(1)}, u32[]{:S(2)}, u32[]{:S(2)}) collective-permute-start(bf16[128,2048]{1,0:T(8,128)(2,1)S(1)} %shard_map.109.refs_0_), channel_id=1, source_target_pairs={{0,3},{1,0},{2,1},{3,2},{4,7},{5,4},{6,5},{7,6},{8,11},{9,8},{10,9... | collective-permute-start | bytes 1572872 | tf_op jit(solution)/shard_map/ppermute | solution.py:50
  86.1 21.5 %collective-permute-start.8 = (bf16[128,2048]{1,0:T(8,128)(2,1)S(1)}, bf16[128,2048]{1,0:T(8,128)(2,1)S(1)}, u32[]{:S(2)}, u32[]{:S(2)}) collective-permute-start(bf16[128,2048]{1,0:T(8,128)(2,1)S(1)} %shard_map.110.refs_1_), channel_id=1, source_target_pairs={{0,1},{1,2},{2,3},{3,0},{4,5},{5,6},{6,7},{7,4},{8,9},{9,10},{10,1... | collective-permute-start | bytes 1572872 | tf_op jit(solution)/shard_map/ppermute | solution.py:50
  88.7 24.5 %collective-permute-start.15 = (bf16[128,2048]{1,0:T(8,128)(2,1)S(1)}, bf16[128,2048]{1,0:T(8,128)(2,1)S(1)}, u32[]{:S(2)}, u32[]{:S(2)}) collective-permute-start(bf16[128,2048]{1,0:T(8,128)(2,1)S(1)} %collective-permute-done.7.refs_2_), channel_id=1, source_target_pairs={{0,1},{1,2},{2,3},{3,0},{4,5},{5,6},{6,7},{7,4},{8,9},{9,10},{10,1... | collective-permute-start | bytes 1572872 | tf_op jit(solution)/shard_map/ppermute | solution.py:50
  96.3 22.5 %collective-permute-start.16 = (bf16[128,2048]{1,0:T(8,128)(2,1)S(1)}, bf16[128,2048]{1,0:T(8,128)(2,1)S(1)}, u32[]{:S(2)}, u32[]{:S(2)}) collective-permute-start(bf16[128,2048]{1,0:T(8,128)(2,1)S(1)} %collective-permute-done.10.refs_5_), channel_id=1, source_target_pairs={{0,3},{1,0},{2,1},{3,2},{4,7},{5,4},{6,5},{7,6},{8,11},{9,8},{10,9... | collective-permute-start | bytes 1572872 | tf_op jit(solution)/shard_map/ppermute | solution.py:50
  110.5 22.2 %collective-permute-start.13 = (bf16[128,512]{1,0:T(8,128)(2,1)}, bf16[128,512]{1,0:T(8,128)(2,1)S(1)}, u32[]{:S(2)}, u32[]{:S(2)}) collective-permute-start(bf16[128,512]{1,0:T(8,128)(2,1)} %get-tuple-element.22), channel_id=1, source_target_pairs={{0,3},{1,0},{2,1},{3,2},{4,7},{5,4},{6,5},{7,6},{8,11},{9,8},{10,9... | collective-permute-start | bytes 393224 | tf_op jit(solution)/shard_map/ppermute | solution.py:50
  110.5 22.2 %collective-permute-start.18 = (bf16[128,512]{1,0:T(8,128)(2,1)}, bf16[128,512]{1,0:T(8,128)(2,1)S(1)}, u32[]{:S(2)}, u32[]{:S(2)}) collective-permute-start(bf16[128,512]{1,0:T(8,128)(2,1)} %get-tuple-element.24), channel_id=1, source_target_pairs={{0,1},{1,2},{2,3},{3,0},{4,5},{5,6},{6,7},{7,4},{8,9},{9,10},{10,1... | collective-permute-start | bytes 393224 | tf_op jit(solution)/shard_map/ppermute | solution.py:50
  121.7 13.8 %collective-permute-start.17 = (bf16[128,1024]{1,0:T(8,128)(2,1)S(1)}, bf16[128,1024]{1,0:T(8,128)(2,1)S(1)}, u32[]{:S(2)}, u32[]{:S(2)}) collective-permute-start(bf16[128,1024]{1,0:T(8,128)(2,1)S(1)} %shard_map.113), channel_id=1, source_target_pairs={{0,2},{1,3},{2,0},{3,1},{4,6},{5,7},{6,4},{7,5},{8,10},{9,11},{10,... | collective-permute-start | bytes 786440 | tf_op jit(solution)/shard_map/ppermute | solution.py:50
  128.0 7.6 %collective-permute-start.14 = (bf16[128,512]{1,0:T(8,128)(2,1)}, bf16[128,512]{1,0:T(8,128)(2,1)S(1)}, u32[]{:S(2)}, u32[]{:S(2)}) collective-permute-start(bf16[128,512]{1,0:T(8,128)(2,1)} %get-tuple-element.23), channel_id=1, source_target_pairs={{0,3},{1,0},{2,1},{3,2},{4,7},{5,4},{6,5},{7,6},{8,11},{9,8},{10,9... | collective-permute-start | bytes 393224 | tf_op jit(solution)/shard_map/ppermute | solution.py:50
  129.4 6.2 %collective-permute-start.19 = (bf16[128,512]{1,0:T(8,128)(2,1)}, bf16[128,512]{1,0:T(8,128)(2,1)S(1)}, u32[]{:S(2)}, u32[]{:S(2)}) collective-permute-start(bf16[128,512]{1,0:T(8,128)(2,1)} %get-tuple-element.25), channel_id=1, source_target_pairs={{0,1},{1,2},{2,3},{3,0},{4,5},{5,6},{6,7},{7,4},{8,9},{9,10},{10,1... | collective-permute-start | bytes 393224 | tf_op jit(solution)/shard_map/ppermute | solution.py:50
  144.3 73.5 %all-to-all-start = ((bf16[128,8,2560]{2,1,0:T(8,128)(2,1)}), bf16[128,8,2560]{2,1,0:T(8,128)(2,1)}, u32[]{:S(2)}, u32[]{:S(2)}) async-start(bf16[128,8,2560]{2,1,0:T(8,128)(2,1)} %bitcast.33), calls=%async_computation | async-start | bytes 10485760 | tf_op jit(solution)/shard_map/all_to_all | solution.py:33
  217.8 58.9 %all-to-all-start.2 = ((bf16[128,8,2048]{2,1,0:T(8,128)(2,1)}), bf16[128,8,2048]{2,1,0:T(8,128)(2,1)}, u32[]{:S(2)}, u32[]{:S(2)}) async-start(bf16[128,8,2048]{2,1,0:T(8,128)(2,1)} %convert_bitcast_fusion), calls=%async_computation.2 | async-start | bytes 8388608 | tf_op jit(solution)/shard_map/all_to_all | solution.py:33
  276.8 69.8 %all-to-all-start.1 = ((bf16[128,8,2560]{2,1,0:T(8,128)(2,1)}), bf16[128,8,2560]{2,1,0:T(8,128)(2,1)}, u32[]{:S(2)}, u32[]{:S(2)}) async-start(bf16[128,8,2560]{2,1,0:T(8,128)(2,1)} %bitcast.34), calls=%async_computation.1 | async-start | bytes 10485760 | tf_op jit(solution)/shard_map/all_to_all | solution.py:33
  346.5 58.9 %all-to-all-start.3 = ((bf16[128,8,2048]{2,1,0:T(8,128)(2,1)}), bf16[128,8,2048]{2,1,0:T(8,128)(2,1)}, u32[]{:S(2)}, u32[]{:S(2)}) async-start(bf16[128,8,2048]{2,1,0:T(8,128)(2,1)} %bitcast.35), calls=%async_computation.3 | async-start | bytes 8388608 | tf_op jit(solution)/shard_map/all_to_all | solution.py:33
  (12 other events, 172.5 us)
